TPU v7x, 32 devices: a whole 2x2x4 slice. The times are simulated.
32 devices in a mesh: dp: 4 (over x, core), gate: 8 (over z, y).
Axes of the slice: x: 2, y: 2, z: 4, core: 2. Of those that a mesh axis runs over, the one named last changes fastest.
Arguments:
- frames: bfloat16 [20, 16, 16384], P(None, None, 'dp'), may hold values from -6 to 6
- regions: int32 [16384], P('dp'), may hold values from 0 to 7, as said below
- valid: int32 [15, 16384], P(None, 'dp'), may hold values from 0 to 1, as said below
- step_count: int32 [4], replicated, may hold values from 1 to 20
- conv_w: float32 [2, 4, 128, 1296], P(None, None, 'gate'), may hold values from -0.15625 to 0.15625
- cell_params: float32 [2, 7, 128], P(None, None, 'gate'), may hold values from -3 to 3
- head_w: float32 [16, 128], replicated, may hold values from -0.5 to 0.5
- head_b: float32 [16], replicated, may hold values from -2 to 2
- conv_mom: float32 [2, 4, 128, 1296], P(None, None, 'gate'), may hold values from -0.0009765625 to 0.0009765625
- cell_mom: float32 [2, 7, 128], P(None, None, 'gate'), may hold values from -0.005859375 to 0.005859375
- head_mom: float32 [16, 128], replicated, may hold values from -0.005859375 to 0.005859375
- bias_mom: float32 [16], replicated, may hold values from -0.01171875 to 0.01171875
- conv_avg: float32 [2, 4, 128, 1296], P(None, None, 'gate'), may hold values from -0.15625 to 0.15625
- cell_avg: float32 [2, 7, 128], P(None, None, 'gate'), may hold values from -3 to 3
- head_avg: float32 [16, 128], replicated, may hold values from -0.5 to 0.5
- bias_avg: float32 [16], replicated, may hold values from -2 to 2
Outputs:
- loss: float32 [], replicated
- conv_mom_new: float32 [2, 4, 128, 1296], P(None, None, 'gate')
- conv_avg_new: float32 [2, 4, 128, 1296], P(None, None, 'gate')
- conv_new: float32 [2, 4, 128, 1296], P(None, None, 'gate')
- conv_low: bfloat16 [2, 4, 128, 1296], P(None, None, 'gate')
- cell_mom_new: float32 [2, 7, 128], P(None, None, 'gate')
- cell_avg_new: float32 [2, 7, 128], P(None, None, 'gate')
- cell_new: float32 [2, 7, 128], P(None, None, 'gate')
- cell_low: bfloat16 [2, 7, 128], P(None, None, 'gate')
- head_mom_new: float32 [16, 128], replicated
- head_avg_new: float32 [16, 128], replicated
- head_new: float32 [16, 128], replicated
- head_low: bfloat16 [16, 128], replicated
- bias_mom_new: float32 [16], replicated
- bias_avg_new: float32 [16], replicated
- bias_new: float32 [16], replicated
- bias_low: bfloat16 [16], replicated
Inputs may be any that keep to these rules, and one draw needn't show every extreme that they name: `regions`: each device's canvas of 32 x 128 pixels is cut into four column bands, each cut into an upper and a lower rectangle; pixel ids are 2 x band + (1 if lower); every id 0 to 7 occurs on every canvas, and the first and last row and column of a canvas always differ in id. `valid`: on canvas b of the 4 canvases each value is 1 with probability (20 + (75 * b) // max(3, 1)) / 100, independently.
All inputs are finite; a program needn't handle non-finite values.
Results may differ from a plain program's by a relative error of at most 0.0059.
Values may be sent and summed in bfloat16 or wider, within the bound.
No kernel may reach another device: no remote copies, remote signals or barrier semaphores. Data moves between devices by JAX's collectives and lax.ppermute only.
A program may use at most 256 MiB of HBM per device.

v0:
```python
import functools

import jax
import jax.numpy as jnp
from jax import lax
from jax.experimental import pallas as pl
from jax.experimental.pallas import tpu as pltpu
from jax.sharding import PartitionSpec as P

EIN = 5
EOUT = 15
COLS = 128

MU = 0.9
RATE_SCALE = 0.05
F32 = jnp.float32
BF16 = jnp.bfloat16
VMEM_LIMIT = 60 * 1024 * 1024


def ring_order(groups):
    wide = groups // 4
    if wide <= 1:
        return list(range(groups))
    order = [(z, 0) for z in range(4)]
    for z in range(3, -1, -1):
        ys = range(1, wide) if z % 2 else range(wide - 1, 0, -1)
        order += [(z, y) for y in ys]
    return [z * wide + y for z, y in order]


def split_steps(steps, most):
    calls = -(-steps // most)
    base, extra = divmod(steps, calls)
    return [base + (1 if i < extra else 0) for i in range(calls)]


def nesterov(param, grad, mom, avg, steps_done, rate):
    mom_new = MU * mom + grad
    param_new = param - rate * (grad + MU * mom_new)
    avg_new = avg + (param_new - avg) / (steps_done + 1.0)
    return [mom_new, avg_new, param_new, param_new.astype(BF16)]


def logistic(v):
    return 0.5 * jnp.tanh(0.5 * v) + 0.5


def dot_nt(a, b):
    return lax.dot_general(a, b, (((1,), (1,)), ((), ())), preferred_element_type=F32)


def dot_tn(a, b):
    return lax.dot_general(a, b, (((0,), (0,)), ((), ())), preferred_element_type=F32)


def cut(total, pieces):
    base, extra = divmod(total, pieces)
    spans, at = [], 0
    for i in range(pieces):
        size = base + (1 if i < extra else 0)
        spans.append((at, size))
        at += size
    return spans


def cut_by_four(total, pieces):
    spans, at = [], 0
    for i in range(pieces):
        left = pieces - i
        size = total - at if left == 1 else (total - at) // left // 4 * 4
        if size:
            spans.append((at, size))
        at += size
    return spans


class Geometry:
    def __init__(self, groups, pixels):
        self.rows = pixels // COLS
        self.own = COLS // groups
        self.halo = min(5, self.own // 2)
        self.calls = [(0, n) for n in split_steps(EIN, self.halo)] + [(1, n) for n in split_steps(EOUT, self.halo)]
        self.front = self.own + 4 * self.halo
        self.back = self.own + 2 * self.halo
        self.union = self.front + (len(self.calls) - 1) * self.halo
        self.window = -(-(self.union + 2) * self.rows // 256) * 256


TAPS = [(dr, dc) for dr in (-1, 0, 1) for dc in (-1, 0, 1)]
CELL_COLS = 16


def window_kernel(geo, start, frames, valid, regions, win, meta, mrm, mrp, mcm, mcp, count, lhs, pick):
    rows, own, halo, union, width = geo.rows, geo.own, geo.halo, geo.union, geo.window
    nf = frames.shape[0]
    nv = valid.shape[0]
    lhs[:nf, :] = frames[...]
    lhs[nf : nf + nv, :] = valid[...].astype(F32).astype(BF16)
    lhs[nf + nv : nf + nv + 1, :] = regions[...].astype(F32).astype(BF16)
    per = 256 // rows
    source = lax.broadcasted_iota(jnp.int32, (COLS, 256), 0)
    lane = lax.broadcasted_iota(jnp.int32, (COLS, 256), 1)
    lane_row = lax.broadcasted_iota(jnp.int32, (1, 256), 1) % rows

    def one(n, carry):
        column = (start[0] + n * per + lane // rows) % COLS
        hit = (source == column).astype(F32).astype(BF16)
        for r in range(rows):
            keep = (lane_row == r).astype(F32).astype(BF16)
            pick[r * COLS : (r + 1) * COLS, :] = hit * keep
        got = jnp.dot(lhs[...], pick[...], preferred_element_type=F32)
        at = pl.multiple_of(n * 256, 256)
        win[:, pl.ds(at, 256)] = got[:nf].astype(BF16)
        meta[:, pl.ds(at, 256)] = got[nf:]
        return carry

    lax.fori_loop(0, width // 256, one, 0)
    px = union * rows
    ids = meta[nv : nv + 1, :]
    bands = jnp.floor(ids * 0.5)
    here = ids[:, rows : rows + px]
    band_here = bands[:, rows : rows + px]
    picked = [
        ids[:, rows - 1 : rows - 1 + px] == here,
        ids[:, rows + 1 : rows + 1 + px] == here,
        bands[:, :px] == band_here,
        bands[:, 2 * rows : 2 * rows + px] == band_here,
    ]
    row_at = lax.broadcasted_iota(jnp.int32, (8, px), 0)
    stack = jnp.zeros((8, px), F32)
    for k, m in enumerate(picked):
        stack = jnp.where(row_at == k, jnp.broadcast_to(m.astype(F32), (8, px)), stack)
    stack = stack.astype(BF16)
    sel = lax.broadcasted_iota(jnp.int32, (8, 128), 0)
    for k, out in enumerate((mrm, mrp, mcm, mcp)):
        out[...] = dot_tn(stack, (sel == k).astype(F32).astype(BF16)).astype(BF16)
    a = (2 * halo + 1) * rows
    count[...] = jnp.broadcast_to(jnp.sum(meta[:nv, a : a + own * rows]), count.shape)


def window_call(geo, start, frames, valid, regions):
    nf, nv = frames.shape[0], valid.shape[0]
    pixels = frames.shape[1]
    px = geo.union * geo.rows
    smem = pl.BlockSpec(memory_space=pltpu.SMEM)
    vmem = pl.BlockSpec(memory_space=pltpu.VMEM)
    total = nf + nv + 1
    return pl.pallas_call(
        functools.partial(window_kernel, geo),
        in_specs=[smem, vmem, vmem, vmem],
        out_specs=[vmem] * 7,
        out_shape=[
            jax.ShapeDtypeStruct((nf, geo.window), BF16),
            jax.ShapeDtypeStruct((nv + 1, geo.window), F32),
        ]
        + [jax.ShapeDtypeStruct((px, 128), BF16)] * 4
        + [jax.ShapeDtypeStruct((8, 128), F32)],
        scratch_shapes=[pltpu.VMEM((total, pixels), BF16), pltpu.VMEM((pixels, 256), BF16)],
        compiler_params=pltpu.CompilerParams(vmem_limit_bytes=VMEM_LIMIT),
        cost_estimate=pl.CostEstimate(
            flops=2 * total * pixels * geo.window, bytes_accessed=10 << 20, transcendentals=0
        ),
        name="window",
    )(start, frames, valid, regions)


def pack_kernel(groups, rank, conv, cells, out0, out1):
    share, depth9 = conv.shape[2:]
    chans9 = out0.shape[-1] - CELL_COLS - 9 * 128
    chans = chans9 // 9
    depth = chans + 128
    row = lax.broadcasted_iota(jnp.int32, (7, CELL_COLS), 0)
    col = lax.broadcasted_iota(jnp.int32, (7, CELL_COLS), 1)
    half = (rank[0] & 1) * 2
    for l, at, gate, out in ((0, 0, rank[0], out0), (1, 0, half, out1), (1, share, half + 1, out1)):
        w = conv[l, gate].astype(BF16)
        parts = [w[:, k * depth + chans : (k + 1) * depth] for k in range(9)]
        parts += [w[:, k * depth : k * depth + chans] for k in range(9)]
        rest = cells[:, l, :]
        cols = jnp.zeros((share, CELL_COLS), F32)
        for k in range(3):
            low = rest.astype(BF16)
            rest = rest - low.astype(F32)
            sel = ((row == gate) & (col == k)) | ((row == gate + 4) & (col == 3 + k))
            cols = cols + dot_tn(low, sel.astype(F32).astype(BF16))
        parts.append(cols.astype(BF16))
        line = jnp.concatenate(parts, 1)
        for g in range(groups):
            out[g, at : at + share, :] = line


def pack_call(groups, rank, conv_w, cells, sent_w):
    share = conv_w.shape[2]
    return plain_call(
        functools.partial(pack_kernel, groups),
        "pack",
        [jax.ShapeDtypeStruct((groups, k * share, sent_w), BF16) for k in (1, 2)],
        rank,
        conv_w,
        cells,
        smem=1,
    )


def peephole_rows(wf):
    tail = wf[:, 9 * 128 :]
    depth = tail.shape[1]
    col = lax.broadcasted_iota(jnp.int32, (8, depth), 1)
    at = depth - CELL_COLS + 3
    sel = ((col >= at) & (col < at + 3)).astype(F32).astype(BF16)
    got = dot_nt(sel, tail)
    return [got[0:1, k * 128 : (k + 1) * 128] for k in range(3)]


def make_variants(geo, h, r0, hb, mrm, mrp, base):
    m = h.shape[0]
    g0 = base * geo.rows + r0
    hb[0, r0 : r0 + m, :] = pltpu.roll(h, 1, 0).astype(BF16) * mrm[g0 : g0 + m, :]
    hb[1, r0 : r0 + m, :] = h.astype(BF16)
    hb[2, r0 : r0 + m, :] = pltpu.roll(h, m - 1, 0).astype(BF16) * mrp[g0 : g0 + m, :]


def forward_kernel(geo, layer, base, steps, first, gather, *refs):
    refs = list(refs)
    if gather:
        rank, pieces, refs = refs[0], refs[1 : 1 + gather], refs[1 + gather :]
    if not first:
        near, far = refs[:2]
        refs = refs[2:]
    if gather:
        cols, win, meta, mrm, mrp = refs[:5]
        wf = refs[12]
        refs = refs[5:12] + refs[13:]
    else:
        cols, win, meta, wf, mrm, mrp = refs[:6]
        refs = refs[6:]
    gates_out, cprev_out, hvar_out, hnew_out, xown_out, state_out, send_out = refs[:7]
    hb, hnext, cb, xs, keeps, peeps = refs[7:]
    rows, halo, own, front, back = geo.rows, geo.halo, geo.own, geo.front, geo.back
    chans = win.shape[0]
    chans9 = 9 * chans
    lanes = (front - 2) * rows
    x0 = (base + 2) * rows
    step = pl.program_id(0)

    @pl.when(step == 0)
    def _():
        hb[:, front * rows :, :] = jnp.zeros((3, rows, 128), BF16)
        if first:
            hb[:, : front * rows, :] = jnp.zeros((3, front * rows, 128), BF16)
            hnext[...] = jnp.zeros_like(hnext)
            cb[...] = jnp.zeros_like(cb)
        else:
            nb = back * rows
            make_variants(geo, near[:, :128].astype(F32), 0, hb, mrm, mrp, base)
            make_variants(geo, far[:, :128].astype(F32), nb, hb, mrm, mrp, base)
            for c in (0, front - 1):
                hnext[:, c * rows : (c + 1) * rows, :] = jnp.zeros((3, rows, 128), BF16)
            cb[:nb, :] = near[:, 128:].astype(F32)
            cb[nb:, :] = far[:, 128:].astype(F32)
        if gather:
            for k, piece in enumerate(pieces):
                if gather == 4:
                    wf[pl.ds(pl.multiple_of((rank[0] ^ k) * 128, 128), 128), :] = piece[...]
                    continue
                peers, span = piece.shape[0], piece.shape[1] // 2
                half = pl.multiple_of(((rank[0] ^ k) & 1) * 256, 256)
                for g in range(peers):
                    for j in range(2):
                        at = pl.multiple_of(half + j * 128 + g * span, span)
                        wf[pl.ds(at, span), :] = piece[g, j * span : (j + 1) * span, :]
        ids = meta[meta.shape[0] - 1 :, :]
        here = ids[:, x0 : x0 + lanes]
        for tap, (dr, dc) in enumerate(TAPS):
            off = x0 + dc * rows + dr
            same = (ids[:, off : off + lanes] == here).astype(F32)
            keeps[tap * chans : (tap + 1) * chans, :] = jnp.broadcast_to(same, (chans, lanes)).astype(BF16)
        ones = lax.broadcasted_iota(jnp.int32, (CELL_COLS, lanes), 0) < 3
        xs[chans9:, :] = ones.astype(F32).astype(BF16)
        for k, row in enumerate(peephole_rows(wf)):
            peeps[k : k + 1, :] = row

    s0, sn = (2 * halo - 1) * rows, (own + 2) * rows
    for v in range(3):
        hvar_out[0, v, :, :] = hb[v, s0 : s0 + sn, :]
    cprev_out[0, :, :] = cb[halo * rows : (halo + back) * rows, :].astype(BF16)
    for tap, (dr, dc) in enumerate(TAPS):
        off = x0 + dc * rows + dr
        part = slice(tap * chans, (tap + 1) * chans)
        xs[part, :] = win[:, off : off + lanes] * keeps[part, :]
    q0 = (2 * halo - 1) * rows
    xown_out[0, :, :] = xs[:, q0 : q0 + own * rows]

    for c0, cw in cut_by_four(front - 2, 4):
        r0, m = (c0 + 1) * rows, cw * rows
        zero = front * rows
        lefts, rights = [], []
        for c in range(c0 + 1, c0 + 1 + cw):
            for at, side, starts in ((c - 1, 0, lefts), (c + 1, 1, rights)):
                starts.append(pl.multiple_of(zero + cols[side * geo.union + base + c] * (at * rows - zero), rows))
        parts = []
        for dr in range(3):
            parts.append(jnp.concatenate([hb[dr, pl.ds(at, rows), :] for at in lefts], 0))
            parts.append(hb[dr, r0 : r0 + m, :])
            parts.append(jnp.concatenate([hb[dr, pl.ds(at, rows), :] for at in rights], 0))
        z = dot_nt(jnp.concatenate(parts, 1), wf[:, : 9 * 128]) + lax.dot_general(
            xs[:, r0 - rows : r0 - rows + m], wf[:, 9 * 128 :], (((0,), (1,)), ((), ())), preferred_element_type=F32
        )
        c = cb[r0 : r0 + m, :]
        gi = logistic(z[:, 0:128] + peeps[0:1, :] * c)
        gf = logistic(z[:, 128:256] + peeps[1:2, :] * c)
        gg = jnp.tanh(z[:, 384:512])
        cn = gf * c + gi * gg
        go = logistic(z[:, 256:384] + peeps[2:3, :] * cn)
        h = go * jnp.tanh(cn)
        cb[r0 : r0 + m, :] = cn
        make_variants(geo, h, r0, hnext, mrm, mrp, base)
        lo, hi = max(c0 + 1, halo), min(c0 + 1 + cw, halo + back)
        a, b = (lo - c0 - 1) * rows, (hi - c0 - 1) * rows
        o = (lo - halo) * rows
        n = b - a
        if n > 0:
            gates_out[0, 0, o : o + n, :] = gi[a:b].astype(BF16)
            gates_out[0, 1, o : o + n, :] = gf[a:b].astype(BF16)
            gates_out[0, 2, o : o + n, :] = go[a:b].astype(BF16)
            gates_out[0, 3, o : o + n, :] = gg[a:b].astype(BF16)
            hnew_out[0, o : o + n, :] = h[a:b].astype(BF16)

    hb[:, : front * rows, :] = hnext[...]

    @pl.when(step == steps - 1)
    def _():
        a, b = halo * rows, (halo + back) * rows
        state_out[:, :128] = hb[1, a:b, :]
        state_out[:, 128:] = cb[a:b, :].astype(BF16)
        a, b = 3 * halo * rows, 5 * halo * rows
        send_out[:, :128] = hb[1, a:b, :]
        send_out[:, 128:] = cb[a:b, :].astype(BF16)


def whole(shape):
    return pl.BlockSpec(shape, lambda *_: (0,) * len(shape))


def forward_call(geo, layer, base, first_frame, steps, state, win, meta, weights, masks):
    rows, own, front, back = geo.rows, geo.own, geo.front, geo.back
    chans = win.shape[0] // (EIN + EOUT)
    gather = len(weights) - 1 if isinstance(weights, tuple) else 0
    sent_w = weights[1].shape[-1] if gather else weights.shape[1]
    depth = sent_w - 9 * 128
    by_step = lambda *dims: pl.BlockSpec((1,) + dims, lambda t: (t,) + (0,) * len(dims))
    lead = list(weights) if gather else []
    cols, masks = masks[4], masks[:2]
    smem = pl.BlockSpec(memory_space=pltpu.SMEM)
    operands = lead + list(state) + [cols, win, meta] + ([] if gather else [weights]) + list(masks)
    in_specs = [smem] if gather else []
    in_specs += [whole(v.shape) for v in lead[1:]]
    in_specs += [whole(s.shape) for s in state]
    in_specs += [smem, pl.BlockSpec((chans, win.shape[1]), lambda t: (first_frame + t, 0))]
    in_specs += [whole(v.shape) for v in operands[len(lead) + len(state) + 2 :]]
    shapes = [
        (steps, 4, back * rows, 128),
        (steps, back * rows, 128),
        (steps, 3, (own + 2) * rows, 128),
        (steps, back * rows, 128),
        (steps, depth, own * rows),
    ]
    flat = [(back * rows, 256), (2 * geo.halo * rows, 256)] + ([(512, sent_w)] if gather else [])
    outs = [jax.ShapeDtypeStruct(s, BF16) for s in shapes + flat]
    out_specs = [by_step(*s[1:]) for s in shapes] + [whole(s) for s in flat]
    px = front * rows
    return pl.pallas_call(
        functools.partial(forward_kernel, geo, layer, base, steps, not state, gather),
        grid=(steps,),
        in_specs=in_specs,
        out_specs=out_specs,
        out_shape=outs,
        scratch_shapes=[
            pltpu.VMEM((3, px + rows, 128), BF16),
            pltpu.VMEM((3, px, 128), BF16),
            pltpu.VMEM((px, 128), F32),
            pltpu.VMEM((depth, px - 2 * rows), BF16),
            pltpu.VMEM((9 * chans, px - 2 * rows), BF16),
            pltpu.VMEM((8, 128), F32),
        ],
        compiler_params=pltpu.CompilerParams(vmem_limit_bytes=VMEM_LIMIT),
        cost_estimate=pl.CostEstimate(
            flops=steps * px * 512 * 1296 * 2, bytes_accessed=8 << 20, transcendentals=steps * px * 640
        ),
        name=f"forward_{base}",
    )(*operands)


def backward_kernel(geo, layer, base, steps, first_live, first, last, carried, *refs):
    refs = list(refs)
    if carried:
        sums_in, head_in = refs[:2]
        refs = refs[2:]
    if not first:
        local, far = refs[:2]
        refs = refs[2:]
    cols, gates, cprev, wf, mrm, mrp = refs[:6]
    refs = refs[6:]
    if layer == 1:
        hnew, target, meta, head, head_b = refs[:5]
        refs = refs[5:]
    dz_out, sums_out, head_out, carry_out, send_out = refs[:5]
    dh, dc, dz_near, dz_far, peeps, wb = refs[5:]
    rows, halo, own, back = geo.rows, geo.halo, geo.own, geo.back
    o0, on = halo * rows, own * rows
    half = back // 2
    step = pl.program_id(0)

    @pl.when(step == 0)
    def _():
        sums_out[...] = sums_in[...] if carried else jnp.zeros_like(sums_out)
        head_out[...] = head_in[...] if carried else jnp.zeros_like(head_out)
        for tap in range(9):
            across, along = tap % 3 * 512, tap // 3 * 128
            wb[across : across + 512, along : along + 128] = wf[:, tap * 128 : (tap + 1) * 128]
        edge = jnp.zeros((4, rows, 128), BF16)
        dz_near[:, :rows, :] = edge
        dz_far[:, :rows, :] = edge
        dz_far[:, (back - half) * rows :, :] = edge
        for k, row in enumerate(peephole_rows(wf)):
            peeps[k : k + 1, :] = row
        if first:
            dh[...] = jnp.zeros_like(dh)
            dc[...] = jnp.zeros_like(dc)
        else:
            nf = 2 * halo * rows
            dh[:nf, :] = far[:, :128]
            dc[:nf, :] = far[:, 128:]
            dh[nf:, :] = local[:, :128]
            dc[nf:, :] = local[:, 128:]

    if layer == 1:
        guess = dot_nt(head[...], hnew[0]) + head_b[...]
        a0 = (base + halo + 1) * rows
        err = guess - target[:, a0 : a0 + back * rows].astype(F32)
        dy = meta[pl.ds(first_live + steps - 1 - step, 1), a0 : a0 + back * rows] * err
        low = dy.astype(BF16)
        head_out[:, 0:128] += jnp.dot(low[:, o0 : o0 + on], hnew[0, o0 : o0 + on, :], preferred_element_type=F32)
        own_dy = low[:, o0 : o0 + on].astype(F32)
        head_out[:, 128:129] += jnp.sum(own_dy, 1, keepdims=True)
        head_out[:, 129:130] += jnp.sum((dy * err)[:, o0 : o0 + on], 1, keepdims=True)
        dh[...] = (dh[...].astype(F32) + dot_tn(low, head[...])).astype(BF16)

    def gates_chunk(c0, cw):
        r0, m = c0 * rows, cw * rows
        span = slice(r0, r0 + m)
        gi, gf, go, gg = (gates[0, n, span, :] for n in range(4))
        pi, pf, po = (peeps[n : n + 1, :].astype(BF16) for n in range(3))
        c = cprev[0, span, :]
        cn = gf * c + gi * gg
        tc = jnp.tanh(cn)
        u = dh[span, :] * go
        w = u * tc
        d_o = w * (1 - go)
        d_c = dc[span, :] + u * ((1 - tc) * (1 + tc)) + d_o * po
        a_i = d_c * gi
        d_i = a_i * gg * (1 - gi)
        d_g = a_i * ((1 - gg) * (1 + gg))
        a_f = d_c * gf
        d_f = a_f * c * (1 - gf)
        dc[span, :] = a_f + d_i * pi + d_f * pf
        store, p0 = (dz_near, rows + r0) if c0 <= half else (dz_far, r0 - half * rows)
        for n, d in enumerate((d_i, d_f, d_o, d_g)):
            store[n, p0 : p0 + m, :] = d
        a = max(r0, o0) - r0
        b = min(r0 + m, o0 + on) - r0
        if b > a:
            for n, d in enumerate((d_i * c, d_f * c, d_o * cn)):
                part = d[a:b].astype(F32).reshape((b - a) // 8, 8, 128)
                sums_out[n * 8 : (n + 1) * 8, :] += jnp.sum(part, 0)

    def hidden_chunk(c0, cw):
        r0, m = c0 * rows, cw * rows
        g0 = (base + halo) * rows + r0
        parts = []
        for side, shift in ((0, 1), (None, 0), (1, -1)):
            pieces = []
            for c in range(c0 + shift, c0 + cw + shift):
                ref, at = (dz_near, (c + 1) * rows) if c <= half else (dz_far, (c - half) * rows)
                if side is not None:
                    at = pl.multiple_of(cols[side * geo.union + base + halo + c] * at, rows)
                pieces.append((ref, at))
            for n in range(4):
                parts.append(jnp.concatenate([ref[n, pl.ds(at, rows), :] for ref, at in pieces], 0))
        acc = jnp.dot(jnp.concatenate(parts, 1), wb[...], preferred_element_type=F32)
        above = pltpu.roll(acc[:, :128] * mrm[g0 : g0 + m, :].astype(F32), m - 1, 0)
        below = pltpu.roll(acc[:, 256:] * mrp[g0 : g0 + m, :].astype(F32), 1, 0)
        dh[r0 : r0 + m, :] = (acc[:, 128:256] + above + below).astype(BF16)

    for c0, cw in cut(half + 1, 2):
        gates_chunk(c0, cw)
    hidden_chunk(0, half)
    for c0, cw in cut(back - half - 1, 2):
        gates_chunk(half + 1 + c0, cw)
    hidden_chunk(half, back - half)
    lo = (half + 1 - halo) * rows
    for n in range(4):
        dz_out[0, :lo, n * 128 : (n + 1) * 128] = dz_near[n, rows + o0 : rows + o0 + lo, :]
        dz_out[0, lo:, n * 128 : (n + 1) * 128] = dz_far[n, rows : rows + on - lo, :]

    @pl.when(step == steps - 1)
    def _():
        carry_out[:, :128] = dh[o0 : o0 + on, :]
        carry_out[:, 128:] = dc[o0 : o0 + on, :]
        ns = 2 * halo * rows
        s0 = o0 + on - ns
        send_out[:, :128] = dh[s0 : s0 + ns, :]
        send_out[:, 128:] = dc[s0 : s0 + ns, :]


def backward_call(geo, layer, base, steps, last, carried, state, saved, wf, masks, extra):
    rows, own, back, halo = geo.rows, geo.own, geo.back, geo.halo
    by_step = lambda *dims: pl.BlockSpec((1,) + dims, lambda t: (steps - 1 - t,) + (0,) * len(dims))
    first_live = saved["t"] - EIN
    lead = list(carried) + list(state)
    cols, masks = masks[4], masks[:2]
    operands = lead + [cols, saved["gates"], saved["cprev"], wf] + list(masks)
    in_specs = [whole(s.shape) for s in lead] + [pl.BlockSpec(memory_space=pltpu.SMEM)]
    in_specs += [by_step(4, back * rows, 128), by_step(back * rows, 128)]
    in_specs += [whole(v.shape) for v in operands[len(lead) + 3 :]]
    if layer == 1:
        win, meta, head, head_b = extra
        operands += [saved["hnew"], win, meta, head, head_b]
        t0 = saved["t"]
        in_specs += [
            by_step(back * rows, 128),
            pl.BlockSpec((head.shape[0], win.shape[1]), lambda t: (t0 + steps - 1 - t, 0)),
            whole(meta.shape),
            whole(head.shape),
            whole(head_b.shape),
        ]
    outs = [
        jax.ShapeDtypeStruct((steps, own * rows, 512), BF16),
        jax.ShapeDtypeStruct((24, 128), F32),
        jax.ShapeDtypeStruct((16, 256), F32),
        jax.ShapeDtypeStruct((own * rows, 256), BF16),
        jax.ShapeDtypeStruct((2 * halo * rows, 256), BF16),
    ]
    out_specs = [by_step(own * rows, 512)] + [whole(o.shape) for o in outs[1:]]
    px = back * rows
    return pl.pallas_call(
        functools.partial(backward_kernel, geo, layer, base, steps, first_live, not state, last, bool(carried)),
        grid=(steps,),
        in_specs=in_specs,
        out_specs=out_specs,
        out_shape=outs,
        scratch_shapes=[
            pltpu.VMEM((px, 128), BF16),
            pltpu.VMEM((px, 128), BF16),
            pltpu.VMEM((4, (back // 2 + 2) * rows, 128), BF16),
            pltpu.VMEM((4, (back - back // 2 + 1) * rows, 128), BF16),
            pltpu.VMEM((8, 128), F32),
            pltpu.VMEM((3 * 512, 3 * 128), BF16),
        ],
        compiler_params=pltpu.CompilerParams(vmem_limit_bytes=VMEM_LIMIT),
        cost_estimate=pl.CostEstimate(
            flops=steps * px * 512 * 1536 * 2, bytes_accessed=8 << 20, transcendentals=steps * px * 128
        ),
        name=f"backward_{base}",
    )(*operands)


def split_low(v, axis=0):
    hi = v.astype(BF16)
    return jnp.concatenate([hi, (v - hi.astype(F32)).astype(BF16)], axis)


def joined(v):
    half = v.shape[0] // 2
    return v[:half].astype(F32) + v[half:].astype(F32)


def weight_kernel(geo, base, steps, add, final, small, *refs):
    refs = list(refs)
    if final:
        rank, refs = refs[0], refs[1:]
    if add:
        acc, refs = refs[0], refs[1:]
    if small:
        sums0, sums1, bias1, head, count = refs[:5]
        refs = refs[5:]
    dz, hvar, xown, mcm, mcp = refs[:5]
    outs, rhs = refs[5:-1], refs[-1]
    rows, own, halo = geo.rows, geo.own, geo.halo
    on = own * rows
    g0 = (base + 2 * halo) * rows
    wide = hvar.shape[-1]
    part = pl.program_id(0)
    if final:
        odd = (rank[0] & 1) == 1

    def put(g):
        at = slice(0, g.shape[0])
        if add:
            g = g + acc[at, :]
        if not final:
            outs[0][at, :] = g
            return g
        keep, send = outs[:2]
        for j in range(2):
            even_gate = g[:, 2 * j * wide : (2 * j + 1) * wide]
            odd_gate = g[:, (2 * j + 1) * wide : (2 * j + 2) * wide]
            keep[j, at, :] = jnp.where(odd, odd_gate, even_gate)
            send[j, at, :] = jnp.where(odd, even_gate, odd_gate).astype(BF16)
        return g

    @pl.when(part < 3)
    def _():
        for dc in range(3):
            for j in range(steps):
                v = hvar[j, 0, dc * rows : dc * rows + on, :]
                if dc == 0:
                    v = v * mcm[g0 : g0 + on, :]
                elif dc == 2:
                    v = v * mcp[g0 : g0 + on, :]
                rhs[j * on : (j + 1) * on, dc * wide : (dc + 1) * wide] = v
        put(dot_tn(rhs[...], dz[...]))

    @pl.when(part == 3)
    def _():
        depth = xown.shape[1]
        inputs = None
        for j in range(steps):
            got = jnp.dot(xown[j], dz[j * on : (j + 1) * on, :], preferred_element_type=F32)
            inputs = got if inputs is None else inputs + got
        bias = put(inputs)[depth - CELL_COLS : depth - CELL_COLS + 8]
        if final and not small:
            outs[2][...] = bias
        if small:
            few = []
            for row, sums in ((bias, sums0), (bias1[...], sums1)):
                few += [row[0:1, k * wide : (k + 1) * wide] for k in range(4)]
                few.append(jnp.sum(sums[...].reshape(3, 8, wide), 1))
            few = jnp.concatenate(few + [jnp.zeros((2, wide), F32)], 0)
            col = lax.broadcasted_iota(jnp.int32, (16, wide), 1)
            extra = jnp.where(col == 2, jnp.broadcast_to(count[0:1, :], (16, wide)), head[:, wide:])
            few = jnp.concatenate([few, head[:, :wide], extra], 0)
            outs[2][...] = few
            outs[1][0, depth : depth + 96, :] = split_low(few)


def weight_call(geo, base, steps, acc, dz, hvar, xown, mcm, mcp, rank=None, small=()):
    on = geo.own * geo.rows
    dz = dz.reshape(steps * on, 512)
    final = rank is not None
    band = 3 * hvar.shape[-1]
    operands = ([rank] if final else []) + ([] if acc is None else [acc]) + list(small) + [dz, hvar, xown, mcm, mcp]
    specs = [pl.BlockSpec(memory_space=pltpu.SMEM)] if final else []
    specs += [] if acc is None else [pl.BlockSpec((band, 512), lambda i: (i, 0))]
    specs += [whole(v.shape) for v in small] + [whole(dz.shape)]
    specs += [pl.BlockSpec((steps, 1) + hvar.shape[2:], lambda i: (0, jnp.minimum(i, 2), 0, 0))]
    specs += [whole(v.shape) for v in (xown, mcm, mcp)]
    out_shape = jax.ShapeDtypeStruct((4 * band, 512), F32)
    out_specs = pl.BlockSpec((band, 512), lambda i: (i, 0))
    if final:
        out_shape = [
            jax.ShapeDtypeStruct((2, 4 * band, 128), F32),
            jax.ShapeDtypeStruct((2, 4 * band, 128), BF16),
            jax.ShapeDtypeStruct((48, 128) if small else (8, 512), F32),
        ]
        out_specs = [pl.BlockSpec((2, band, 128), lambda i: (0, i, 0))] * 2 + [whole(out_shape[2].shape)]
    return pl.pallas_call(
        functools.partial(weight_kernel, geo, base, steps, acc is not None, final, bool(small)),
        grid=(4,),
        in_specs=specs,
        out_specs=out_specs,
        out_shape=out_shape,
        scratch_shapes=[pltpu.VMEM((steps * on, band), BF16)],
        compiler_params=pltpu.CompilerParams(vmem_limit_bytes=VMEM_LIMIT),
        cost_estimate=pl.CostEstimate(
            flops=steps * on * 512 * 1296 * 2, bytes_accessed=16 << 20, transcendentals=0
        ),
        name=f"weights_{base}",
    )(*operands)


SMALL_AT = 1408


def core_stage_kernel(rank, keep, got, *refs):
    depth = refs[1].shape[0] if len(refs) > 2 else refs[0].shape[0]
    high = (rank[0] & 2) == 2
    small = len(refs) > 2
    if small:
        few, keep_out, send_out, few_out = refs
    else:
        keep_out, send_out = refs
    a = keep[0, :depth, :] + got[0, :depth, :].astype(F32)
    b = keep[1, :depth, :] + got[1, :depth, :].astype(F32)
    keep_out[...] = jnp.where(high, b, a)
    send_out[:depth, :] = jnp.where(high, a, b).astype(BF16)
    if small:
        total = few[...] + joined(got[0, depth : depth + 96, :])
        few_out[...] = total
        send_out[depth:, :] = split_low(total)


def chip_stage_kernel(groups, keep, got, *refs):
    depth, wide = keep.shape
    small = len(refs) > 1
    if small:
        few, out = refs
    else:
        (out,) = refs
    width = depth - CELL_COLS
    share = wide // groups
    total = (keep[...] + got[:depth, :].astype(F32)).T[:, :width].astype(BF16)
    if small:
        sums = few[...] + joined(got[depth:, :])
        head = split_low(sums[16:32], 1)
        extra = split_low(sums[32:, :16], 1)
        fill = jnp.zeros((16, SMALL_AT - width - 2 * share - 32), BF16)
    for g in range(groups):
        part = total[g * share : (g + 1) * share, :]
        if not small:
            out[g, :, :] = part
        else:
            cells = split_low(sums[:16, g * share : (g + 1) * share], 1)
            out[g, :, :] = jnp.concatenate([part, cells, extra, fill, head], 1)


def sum_stage_kernel(got, out):
    total = got[0].astype(F32)
    for g in range(1, got.shape[0]):
        total = total + got[g].astype(F32)
    out[...] = total


def finish_kernel(rate, chans, got, steps_done, *refs):
    (cell_refs, head_refs, bias_refs), refs = (refs[:3], refs[3:6], refs[6:9]), refs[9:]
    shard, scalars, loss, cell_outs, head_outs, bias_outs = refs[0], refs[1], refs[2], refs[3:7], refs[7:11], refs[11:]
    total = got[0].astype(F32)
    for g in range(1, got.shape[0]):
        total = total + got[g].astype(F32)
    width = shard.shape[1]
    share = total.shape[0]
    shard[...] = total[:, :width]
    cells = total[:, width : width + share] + total[:, width + share : width + 2 * share]
    at = width + 2 * share
    extra = total[:, at : at + 16] + total[:, at + 16 : at + 32]
    head = total[:, SMALL_AT : SMALL_AT + 128] + total[:, SMALL_AT + 128 :]
    count = chans * extra[0:1, 2:3]
    scale = 2.0 / count
    fresh = [1.0 / (jnp.full((1, 1), steps_done[k].astype(F32)) + 1.0) for k in range(4)]
    loss[...] = jnp.sum(extra[:, 1:2], 0, keepdims=True) / count
    lane = lax.broadcasted_iota(jnp.int32, (8, 128), 1)
    scalars[...] = jnp.where(lane == 0, scale, jnp.where(lane == 1, rate, fresh[0]))

    def update(refs, outs, at, grad, fresh):
        param, mom, avg = (v[at] for v in refs)
        grad = grad * scale
        m = MU * mom + grad
        p = param - rate * (grad + MU * m)
        outs[0][at] = m
        outs[1][at] = avg + (p - avg) * fresh
        outs[2][at] = p
        outs[3][at] = p.astype(BF16)

    for l in range(2):
        update(cell_refs, cell_outs, (slice(None), l, slice(None)), cells[l * 7 : (l + 1) * 7, :], fresh[1])
    update(head_refs, head_outs, (slice(None), slice(None)), head, fresh[2])
    row = lax.broadcasted_iota(jnp.int32, (16, 16), 0)
    col = lax.broadcasted_iota(jnp.int32, (16, 16), 1)
    bias = jnp.sum(jnp.where(row == col, jnp.broadcast_to(extra[:, 0:1], (16, 16)), 0.0), 0, keepdims=True)
    update(bias_refs, bias_outs, (slice(None), slice(None)), bias, fresh[3])


def plain_call(kernel, name, out_shape, *operands, smem=0, moved=4 << 20, smem_at=()):
    where = [pltpu.SMEM if i < smem or i in smem_at else pltpu.VMEM for i in range(len(operands))]
    specs = [pl.BlockSpec(memory_space=m) for m in where]
    return pl.pallas_call(
        kernel,
        in_specs=specs,
        out_shape=out_shape,
        compiler_params=pltpu.CompilerParams(vmem_limit_bytes=VMEM_LIMIT),
        cost_estimate=pl.CostEstimate(flops=1 << 20, bytes_accessed=moved, transcendentals=0),
        name=name,
    )(*operands)


def core_stage(name, rank, depth, keep, got, small):
    wide = keep.shape[2]
    more = 96 if small else 0
    shapes = [jax.ShapeDtypeStruct((depth, wide), F32), jax.ShapeDtypeStruct((depth + more, wide), BF16)]
    shapes += [jax.ShapeDtypeStruct(v.shape, F32) for v in small]
    return plain_call(core_stage_kernel, "core_stage_" + name, shapes, rank, keep, got, *small, smem=1)


def chip_stage(name, groups, keep, got, small):
    depth, wide = keep.shape
    lanes = SMALL_AT + 256 if small else depth - CELL_COLS
    shape = jax.ShapeDtypeStruct((groups, wide // groups, lanes), BF16)
    kernel = functools.partial(chip_stage_kernel, groups)
    return plain_call(kernel, "chip_stage_" + name, shape, keep, got, *small, moved=2 << 20)


def sum_stage(name, got):
    shape = jax.ShapeDtypeStruct(got.shape[1:], F32)
    return plain_call(sum_stage_kernel, "sum_stage_" + name, shape, got, moved=1 << 20)


def finish_stage(rate, chans, width, got, step_count, small_args):
    shapes = [
        jax.ShapeDtypeStruct((got.shape[1], width), F32),
        jax.ShapeDtypeStruct((8, 128), F32),
        jax.ShapeDtypeStruct((1, 1), F32),
    ]
    for v in small_args[::3]:
        shapes += [jax.ShapeDtypeStruct(v.shape, F32)] * 3 + [jax.ShapeDtypeStruct(v.shape, BF16)]
    kernel = functools.partial(finish_kernel, rate, chans)
    return plain_call(kernel, "finish", shapes, got, step_count, *small_args, moved=1 << 20, smem_at=(1,))


def update_kernel(rank, scalars, *refs):
    pieces = (refs[:4], refs[4:8])
    param, mom, avg, mom_out, avg_out, new_out, low_out, grad = refs[8:]
    layer = pl.program_id(0)
    chans = (grad.shape[-1] - 9 * 128) // 9
    scale, rate, fresh = (scalars[0:1, k : k + 1] for k in range(3))
    for l in range(2):

        @pl.when(layer == l)
        def _():
            for k, piece in enumerate(pieces[l]):
                v = piece[...]
                parts = []
                for tap in range(9):
                    parts.append(v[:, 9 * 128 + tap * chans : 9 * 128 + (tap + 1) * chans])
                    parts.append(v[:, tap * 128 : (tap + 1) * 128])
                grad[rank[0] ^ k] = jnp.concatenate(parts, 1) * scale

    g = grad[...]
    m = MU * mom[0] + g
    p = param[0] - rate * (g + MU * m)
    mom_out[0] = m
    new_out[0] = p
    low_out[0] = p.astype(BF16)
    avg_out[0] = avg[0] + (p - avg[0]) * fresh


def update_call(rank, scalars, pieces, param, mom, avg):
    layers, gates, share, width = param.shape
    block = pl.BlockSpec((1, gates, share, width), lambda l: (l, 0, 0, 0))
    smem = pl.BlockSpec(memory_space=pltpu.SMEM)
    shape = jax.ShapeDtypeStruct(param.shape, F32)
    return pl.pallas_call(
        update_kernel,
        grid=(layers,),
        in_specs=[smem, whole(scalars.shape)] + [whole(v.shape) for v in pieces] + [block] * 3,
        out_specs=[block] * 4,
        out_shape=[shape] * 3 + [jax.ShapeDtypeStruct(param.shape, BF16)],
        scratch_shapes=[pltpu.VMEM((gates, share, width), F32)],
        compiler_params=pltpu.CompilerParams(vmem_limit_bytes=VMEM_LIMIT),
        cost_estimate=pl.CostEstimate(flops=1 << 20, bytes_accessed=6 << 20, transcendentals=0),
        name="update",
    )(rank, scalars, *pieces, param, mom, avg)


def swap_pairs(size, bit):
    return [(i, i ^ bit) for i in range(size)]


def butterfly_bits(size):
    bits, bit = [], 1
    while bit < size:
        bits.append(bit)
        bit *= 2
    return bits


def gather_dp(piece, ranks):
    me = lax.axis_index("dp")
    for bit in butterfly_bits(ranks)[1:] + [1]:
        other = lax.ppermute(piece, "dp", swap_pairs(ranks, bit))
        high = (me & bit) != 0
        pair = jnp.stack([jnp.where(high, other, piece), jnp.where(high, piece, other)])
        if bit == 1:
            piece = jnp.swapaxes(pair, 0, 1).reshape((-1,) + piece.shape[1:])
        else:
            piece = pair.reshape((-1,) + piece.shape[1:])
    return piece


def scatter_sum_dp(whole_sum, ranks, small):
    me = lax.axis_index("dp")
    value = whole_sum
    bits = butterfly_bits(ranks)
    for n, bit in enumerate([1] + bits[:0:-1]):
        if bit == 1:
            halves = value.reshape((ranks // 2, 2) + value.shape[1:])
            low, high = halves[:, 0], halves[:, 1]
        else:
            half = value.shape[0] // 2
            low, high = value[:half], value[half:]
        mine_high = (me & bit) != 0
        send = jnp.where(mine_high, low, high).astype(BF16)
        keep = jnp.where(mine_high, high, low)
        pairs = swap_pairs(ranks, bit)
        value = keep + lax.ppermute(send, "dp", pairs).astype(F32)
        hi = lax.reduce_precision(small, 8, 7)
        got = lax.ppermute(jnp.stack([hi, small - hi]).astype(BF16), "dp", pairs).astype(F32)
        small = small + (got[0] + got[1])
    return value[0], small


def gathered_weights(conv_w, cell_params, dp_at, groups, ranks, chans):
    share = conv_w.shape[2]
    wide = share * groups
    taps = conv_w.reshape(2, 4 * share, 9, chans + wide).astype(BF16)
    parts = [
        taps[..., chans:].reshape(2, 4 * share, 9 * wide),
        taps[..., :chans].reshape(2, 4 * share, 9 * chans),
    ]
    cells = jnp.stack([cell_params[:, :4], jnp.pad(cell_params[:, 4:], ((0, 0), (0, 1), (0, 0)))], -1)
    cell_hi = lax.reduce_precision(cells, 8, 7)
    cell_mid = lax.reduce_precision(cells - cell_hi, 8, 7)
    cell_lo = cells - cell_hi - cell_mid
    cell_parts = jnp.stack([cell_hi, cell_mid, cell_lo], -1).astype(BF16).reshape(2, 4 * share, 6)
    parts.append(jnp.pad(cell_parts, ((0, 0), (0, 0), (0, CELL_COLS - 6))))
    packed = jnp.concatenate(parts, -1)
    slab = 4 * share // ranks
    sent_w = packed.shape[-1]
    mine = lax.dynamic_slice_in_dim(packed.reshape(2, ranks, slab, sent_w), dp_at, 1, 1)[:, 0]
    everyone = lax.all_to_all(
        jnp.broadcast_to(mine[None], (groups, 2, slab, sent_w)), "gate", 0, 0, tiled=True
    )
    gathered = gather_dp(everyone[None], ranks)
    full = gathered.transpose(2, 1, 0, 3, 4).reshape(2, groups, 4, share, sent_w)
    full = full.transpose(0, 2, 1, 3, 4).reshape(2, 4 * wide, sent_w)
    return [full[0], full[1]]


def on_device(
    frames,
    regions,
    valid,
    step_count,
    conv_w,
    cell_params,
    head_w,
    head_b,
    conv_mom,
    cell_mom,
    head_mom,
    bias_mom,
    conv_avg,
    cell_avg,
    head_avg,
    bias_avg,
):
    share = conv_w.shape[2]
    chans = frames.shape[1]
    pixels = frames.shape[2]
    wide = head_w.shape[1]
    groups = lax.axis_size("gate")
    ranks = lax.axis_size("dp")
    geo = Geometry(groups, pixels)
    rows, own, halo, front, back, union = geo.rows, geo.own, geo.halo, geo.front, geo.back, geo.union
    gate_at = lax.axis_index("gate")
    dp_at = lax.axis_index("dp")

    order = ring_order(groups)
    place = [order.index(g) for g in range(groups)]
    spot = jnp.asarray(place, jnp.int32)[gate_at]
    from_right = [(order[(i + 1) % groups], order[i]) for i in range(groups)]
    from_left = [(order[i], order[(i + 1) % groups]) for i in range(groups)]

    slab = 4 * share // ranks
    packed_w = 9 * (wide + chans)
    sent_w = packed_w + CELL_COLS
    direct = ranks == 4 and slab == share and share % 16 == 0
    rank = dp_at.astype(jnp.int32).reshape(1)

    start = jnp.mod(spot * own - 2 * halo - 1, COLS).astype(jnp.int32).reshape(1)
    win, meta, mrm, mrp, mcm, mcp, counted = window_call(
        geo, start, frames.reshape(-1, pixels), valid, regions.reshape(1, pixels)
    )
    first_row = lax.slice_in_dim(regions, 0, COLS) // 2
    bands = lax.dynamic_slice_in_dim(jnp.concatenate([first_row, first_row]), start[0], union + 2)
    same = (bands[1:] == bands[:-1]).astype(jnp.int32)
    cols = jnp.concatenate([same[:-1], same[1:]])
    masks = (mrm, mrp, mcm, mcp, cols)

    head_low = head_w.astype(BF16)
    head_bias = head_b[:, None]
    if direct:
        by_core, by_chip = swap_pairs(ranks, 1), swap_pairs(ranks, 2)
        cells_first = jnp.swapaxes(cell_params, 0, 1)
        mine0, mine1 = pack_call(groups, rank, conv_w, cells_first, sent_w)
        mixed0 = lax.all_to_all(mine0, "gate", 0, 0, tiled=True).reshape(groups * share, sent_w)
        mixed0, win, mine1 = lax.optimization_barrier((mixed0, win, mine1))
        over_x = lax.ppermute(mixed0, "dp", by_chip)
        over_core = lax.ppermute(mixed0, "dp", by_core)
        weights = [(rank, mixed0, over_core, over_x, lax.ppermute(over_x, "dp", by_core))]
        mixed1 = lax.all_to_all(mine1, "gate", 0, 0, tiled=True)
        weights.append((rank, mixed1))
    else:
        weights = gathered_weights(conv_w, cell_params, dp_at, groups, ranks, chans)

    state = ()
    kept = []
    t = 0
    for n, (layer, steps) in enumerate(geo.calls):
        base = n * halo
        first_frame = t if layer == 0 else t - 1
        got = forward_call(geo, layer, base, first_frame, steps, state, win, meta, weights[layer], masks)
        if len(got) > 7:
            weights[layer] = got[7]
        if direct and n == 0:
            mixed1, sent = lax.optimization_barrier((weights[1][1], got[6]))
            weights[1] = (rank, mixed1, lax.ppermute(mixed1, "dp", swap_pairs(ranks, 1)))
            got = [*got[:6], sent, *got[7:]]
        kept.append(dict(gates=got[0], cprev=got[1], hvar=got[2], hnew=got[3], xown=got[4], t=t))
        out = got[5]
        t += steps
        if n + 1 < len(geo.calls):
            far = lax.ppermute(got[6], "gate", from_right)
            state = (out, far)

    state = ()
    grads = [None, None]
    cell_sums = [None, None]
    head_sums = None
    for n in range(len(geo.calls) - 1, -1, -1):
        layer, steps = geo.calls[n]
        base = n * halo
        saved = kept[n]
        extra = (win, meta, head_low, head_bias) if layer == 1 else None
        carried = () if cell_sums[layer] is None else (cell_sums[layer], head_sums)
        got = backward_call(
            geo, layer, base, steps, n == 0, carried, state, saved, weights[layer], masks, extra
        )
        if n > 0:
            far = lax.ppermute(got[4], "gate", from_left)
            state = (got[3], far)
        cell_sums[layer] = got[1]
        if layer == 1:
            head_sums = got[2]
        done = direct and (n == 0 or geo.calls[n - 1][0] != layer)
        dz = got[0]
        if done and layer == 0:
            keep1, send1, dz = lax.optimization_barrier((*core_stage("1", rank, sent_w, grads[1][0], crossed1, ()), dz))
            crossed1 = lax.ppermute(send1, "dp", swap_pairs(ranks, 2))
        grads[layer] = weight_call(
            geo,
            base,
            steps,
            grads[layer],
            dz,
            saved["hvar"],
            saved["xown"],
            masks[2],
            masks[3],
            rank if done else None,
            (cell_sums[0], cell_sums[1], grads[1][2], head_sums, counted) if done and layer == 0 else (),
        )
        if done and layer == 1:
            send1, far = lax.optimization_barrier((grads[1][1], far))
            state = (got[3], far)
            crossed1 = lax.ppermute(send1, "dp", swap_pairs(ranks, 1))
    if direct:
        pairs = swap_pairs(ranks, 1)
        across = swap_pairs(ranks, 2)
        keep0, send0, few = grads[0]
        send0, crossed1 = lax.optimization_barrier((send0, crossed1))
        crossed0 = lax.ppermute(send0, "dp", pairs)
        message1, crossed0 = lax.optimization_barrier((chip_stage("1", groups, keep1, crossed1, ()), crossed0))
        mixed1 = lax.all_to_all(message1, "gate", 0, 0, tiled=True)
        keep0, send0, few = core_stage("0", rank, sent_w, keep0, crossed0, (few,))
        crossed0 = lax.ppermute(send0, "dp", across)
        shard1, crossed0 = lax.optimization_barrier((sum_stage("1", mixed1), crossed0))
        from_dp1 = [lax.ppermute(shard1, "dp", swap_pairs(ranks, k)) for k in (1, 2, 3)]
        message0 = chip_stage("0", groups, keep0, crossed0, (few,))
        mixed0 = lax.all_to_all(message0, "gate", 0, 0, tiled=True)
        *from_dp1, mixed0 = lax.optimization_barrier((*from_dp1, mixed0))
        total_pixels = EOUT * pixels * ranks
        flip = lambda v: jnp.swapaxes(v, 0, 1)
        small_args = [cells_first, flip(cell_mom), flip(cell_avg), head_w, head_mom, head_avg]
        small_args += [v[None] for v in (head_b, bias_mom, bias_avg)]
        rate = float(RATE_SCALE * chans * total_pixels**0.5)
        done = finish_stage(rate, chans, packed_w, mixed0, step_count, small_args)
        shard0, scalars, loss = done[:3]
        pieces = [shard0] + [lax.ppermute(shard0, "dp", swap_pairs(ranks, k)) for k in (1, 2, 3)]
        pieces += [shard1] + from_dp1
        outs = [loss[0, 0]]
        outs += update_call(rank, scalars, pieces, conv_w, conv_mom, conv_avg)
        outs += [flip(v) for v in done[3:7]] + list(done[7:11]) + [v[0] for v in done[11:15]]
        return tuple(outs)

    rate = RATE_SCALE * chans * jnp.sqrt(jnp.float32(EOUT * pixels * ranks))
    counts_done = step_count.astype(F32)
    biases = jnp.stack([g[packed_w].reshape(4, wide) for g in grads])
    cells = jnp.concatenate([biases, jnp.stack(cell_sums).reshape(2, 3, 8, wide).sum(2)], 1)
    grads = [g[:packed_w].T for g in grads]
    loss_sum = jnp.sum(head_sums[:, 129])
    shared_small = jnp.concatenate(
        [head_sums[:, :128].reshape(-1), head_sums[:, 128], loss_sum[None], counted[0, :1]]
    )
    small = jnp.concatenate([cells.reshape(-1), shared_small])
    big = jnp.stack(grads).reshape(2, 4, groups, share, packed_w).transpose(2, 1, 3, 0, 4)
    big = big.reshape(groups, ranks, slab, 2, packed_w).transpose(1, 0, 2, 3, 4)
    part, small = scatter_sum_dp(big, ranks, small)
    ncell = 14 * wide
    for_gate = small[:ncell].reshape(14, groups, share).transpose(1, 0, 2).reshape(groups, 14 * share)
    to_gate = jnp.concatenate(
        [for_gate, jnp.broadcast_to(small[None, ncell:], (groups, small.shape[0] - ncell))], 1
    )
    hi = lax.reduce_precision(to_gate, 8, 7)
    lo = (to_gate - hi).astype(BF16)
    hi = hi.astype(BF16)
    width = slab * 2 * packed_w
    message = jnp.concatenate([part.reshape(groups, width).astype(BF16), hi, lo], 1)
    got = lax.all_to_all(message, "gate", 0, 0, tiled=True).astype(F32)
    got = jnp.sum(got.reshape(groups, -1), 0)
    nsmall = to_gate.shape[1]
    small_sum = got[width : width + nsmall] + got[width + nsmall :]
    piece = got[:width].reshape(1, slab, 2, packed_w)
    rows_all = gather_dp(piece, ranks).reshape(4 * share, 2, packed_w).transpose(1, 0, 2)
    count = chans * small_sum[-1]
    scale = 2.0 / count
    rows_all = rows_all * scale
    grad_conv = jnp.concatenate(
        [
            rows_all[..., 9 * wide :].reshape(2, 4 * share, 9, chans),
            rows_all[..., : 9 * wide].reshape(2, 4 * share, 9, wide),
        ],
        -1,
    ).reshape(conv_w.shape)
    grad_cell = small_sum[: 14 * share].reshape(2, 7, share) * scale
    rest = small_sum[14 * share :]
    grad_head = rest[: chans * wide].reshape(chans, wide) * scale
    grad_bias = rest[chans * wide : chans * wide + chans] * scale
    loss = rest[chans * wide + chans] / count

    outs = [loss]
    outs += nesterov(conv_w, grad_conv, conv_mom, conv_avg, counts_done[0], rate)
    outs += nesterov(cell_params, grad_cell, cell_mom, cell_avg, counts_done[1], rate)
    outs += nesterov(head_w, grad_head, head_mom, head_avg, counts_done[2], rate)
    outs += nesterov(head_b, grad_bias, bias_mom, bias_avg, counts_done[3], rate)
    return tuple(outs)


def solution(mesh):
    in_specs = (
        P(None, None, "dp"),
        P("dp"),
        P(None, "dp"),
        P(),
        P(None, None, "gate", None),
        P(None, None, "gate"),
        P(),
        P(),
        P(None, None, "gate", None),
        P(None, None, "gate"),
        P(),
        P(),
        P(None, None, "gate", None),
        P(None, None, "gate"),
        P(),
        P(),
    )
    out_specs = (
        P(),
        P(None, None, "gate", None),
        P(None, None, "gate", None),
        P(None, None, "gate", None),
        P(None, None, "gate", None),
        P(None, None, "gate"),
        P(None, None, "gate"),
        P(None, None, "gate"),
        P(None, None, "gate"),
        P(),
        P(),
        P(),
        P(),
        P(),
        P(),
        P(),
        P(),
    )
    return jax.shard_map(
        on_device, mesh=mesh, in_specs=in_specs, out_specs=out_specs, check_vma=False
    )
```

profile of v0, /device:TPU:0, one launch (start us, length us, event | category | flops | bytes accessed | tf_op | source)
XLA Modules:
  0.0 291.0 jit_solution(12367471839496129839)
XLA Ops:
  0.7 2.4 pack.1
  3.0 7.3 %all-to-all-start = ((bf16[8,16,1312]{2,1,0:T(8,128)(2,1)}), bf16[8,16,1312]{2,1,0:T(8,128)(2,1)S(1)}, u32[]{:S(2)}, u32[]{:S(2)}) async-start(bf16[8,16,1312]{2,1,0:T(8,128)(2,1)} %get-tuple-element.120), calls=%async_computation | async-start | bytes 720896 | tf_op jit(solution)/shard_map/all_to_all | solution.py:996
  10.3 1.2 dynamic_slice.6
  12.9 10.4 %window.1 = (bf16[320,1792]{1,0:T(8,128)(2,1)}, f32[16,1792]{1,0:T(8,128)}, bf16[1632,128]{1,0:T(8,128)(2,1)}, bf16[1632,128]{1,0:T(8,128)(2,1)}, bf16[1632,128]...) custom-call(s32[1]{0:T(128)} %bitcast.4.start, bf16[320,4096]{1,0:T(8,128)(2,1)} %bitcast.38, ...), custom_call_target="tpu_custom_call" | custom-call | flops 4932501504 | bytes 10485760 | tf_op jit(solution)/shard_map/window/pallas_call | solution.py:149
  23.4 1.6 collective-permute-start.1
  25.0 6.0 %all-to-all-start.1 = ((bf16[8,32,1312]{2,1,0:T(8,128)(2,1)}), bf16[8,32,1312]{2,1,0:T(8,128)(2,1)S(1)}, u32[]{:S(2)}, u32[]{:S(2)}) async-start(bf16[8,32,1312]{2,1,0:T(8,128)(2,1)} %get-tuple-element.123), calls=%async_computation.1 | async-start | bytes 1441792 | tf_op jit(solution)/shard_map/all_to_all | solution.py:1001
  31.1 2.2 collective-permute-done.1.refs_3_
  34.0 1.0 collective-permute-done.2.refs_4_
  35.7 17.7 %forward_0.1 = (bf16[5,4,832,128]{3,2,1,0:T(8,128)(2,1)}, bf16[5,832,128]{2,1,0:T(8,128)(2,1)}, bf16[5,3,576,128]{3,2,1,0:T(8,128)(2,1)}, bf16[5,832,128]{2,1,0:...) custom-call(s32[1]{0:T(128)} %bitcast.rank.refs_0_, ...), custom_call_target="tpu_custom_call" | custom-call | flops 7644119040 | bytes 8388608 | tf_op jit(solution)/shard_map/forward_0/pallas_call | solution.py:373
  53.6 1.8 collective-permute-start.4
  55.4 5.0 %collective-permute-done.4.refs_4_ = bf16[320,256]{1,0:T(8,128)(2,1)S(1)} collective-permute-done((bf16[320,256]{1,0:T(8,128)(2,1)}, bf16[320,256]{1,0:T(8,128)(2,1)S(1)}, u32[]{:S(2)}, u32[]{:S(2)}) %collective-permute-start.4) | collective-permute-done | bytes 163872 | tf_op jit(solution)/shard_map/ppermute | solution.py:1023
  61.3 17.8 %forward_5.1 = (bf16[5,4,832,128]{3,2,1,0:T(8,128)(2,1)}, bf16[5,832,128]{2,1,0:T(8,128)(2,1)}, bf16[5,3,576,128]{3,2,1,0:T(8,128)(2,1)}, bf16[5,832,128]{2,1,0:...) custom-call(s32[1]{0:T(128)} %bitcast.rank.refs_0_, ...), custom_call_target="tpu_custom_call" | custom-call | flops 7644119040 | bytes 8388608 | tf_op jit(solution)/shard_map/forward_5/pallas_call | solution.py:373
  79.1 1.8 collective-permute-start.5
  80.9 4.1 %collective-permute-done.5.refs_1_ = bf16[320,256]{1,0:T(8,128)(2,1)S(1)} collective-permute-done((bf16[320,256]{1,0:T(8,128)(2,1)}, bf16[320,256]{1,0:T(8,128)(2,1)S(1)}, u32[]{:S(2)}, u32[]{:S(2)}) %collective-permute-start.5) | collective-permute-done | bytes 163872 | tf_op jit(solution)/shard_map/ppermute | solution.py:1023
  85.7 17.4 %forward_10.1 = (bf16[5,4,832,128]{3,2,1,0:T(8,128)(2,1)}, bf16[5,832,128]{2,1,0:T(8,128)(2,1)}, bf16[5,3,576,128]{3,2,1,0:T(8,128)(2,1)}, bf16[5,832,128]{2,1,0...) custom-call(bf16[832,256]{1,0:T(8,128)(2,1)} %get-tuple-element.133.refs_0_, ...), custom_call_target="tpu_custom_call" | custom-call | flops 7644119040 | bytes 8388608 | tf_op jit(solution)/shard_map/forward_10/pallas_call | solution.py:373
  103.1 2.0 collective-permute-start.6
  106.4 2.5 collective-permute-done.6.refs_1_
  109.6 17.4 %forward_15.1 = (bf16[5,4,832,128]{3,2,1,0:T(8,128)(2,1)}, bf16[5,832,128]{2,1,0:T(8,128)(2,1)}, bf16[5,3,576,128]{3,2,1,0:T(8,128)(2,1)}, bf16[5,832,128]{2,1,0...) custom-call(bf16[832,256]{1,0:T(8,128)(2,1)} %get-tuple-element.136.refs_0_, ...), custom_call_target="tpu_custom_call" | custom-call | flops 7644119040 | bytes 8388608 | tf_op jit(solution)/shard_map/forward_15/pallas_call | solution.py:373
  127.0 16.6 %backward_15.1 = (bf16[5,512,512]{2,1,0:T(8,128)(2,1)}, f32[24,128]{1,0:T(8,128)}, f32[16,256]{1,0:T(8,128)}, bf16[512,256]{1,0:T(8,128)(2,1)}, bf16[320,256]{1,0:T(8,128)(2,1)}) custom-call(s32[102]{0:T(128)} %pad_add_fusion.1.refs_5_.refs_2_.refs_0_.refs_4_, bf16[5,4,832,128]{3,2,1,0:T(8,128)(2,1)} %get-tuple-element.138.refs_1_, ...), custom_call_target="tpu_custom_call" | custom-call | flops 6543114240 | bytes 8388608 | tf_op jit(solution)/shard_map/backward_15/pallas_call | solution.py:547
  143.6 1.8 collective-permute-start.7
  145.4 8.2 %weights_15.1.refs_0_ = f32[1536,512]{1,0:T(8,128)} custom-call(bf16[2560,512]{1,0:T(8,128)(2,1)} %bitcast.50, bf16[5,3,576,128]{3,2,1,0:T(8,128)(2,1)} %get-tuple-element.142.refs_1_, bf16[5,160,512]{2,1,0:T(8,128)(2,1)} %get-tuple-element.143.refs_2_, bf16[1632,128]{1,0:T(8,128)(2,1)} %get-tuple-element.144.refs_3_.refs_4_.refs_5_.refs_9_, ...), custom_call_target="tpu_custom_call" | custom-call | flops 3397386240 | bytes 16777216 | tf_op jit(solution)/shard_map/weights_15/pallas_call | solution.py:668
  154.3 16.3 %backward_10.1 = (bf16[5,512,512]{2,1,0:T(8,128)(2,1)}, f32[24,128]{1,0:T(8,128)}, f32[16,256]{1,0:T(8,128)}, bf16[512,256]{1,0:T(8,128)(2,1)}, bf16[320,256]{1,0:T(8,128)(2,1)}) custom-call(f32[24,128]{1,0:T(8,128)} %get-tuple-element.146.refs_0_, f32[16,256]{1,0:T(8,128)} %get-tuple-element.147.refs_1_, bf16[512,256]{1,0:T(8,128)(2,1)} %get-tuple-element.148.refs_2_, ...), custom_call_target="tpu_custom_call" | custom-call | flops 6543114240 | bytes 8388608 | tf_op jit(solution)/shard_map/backward_10/pallas_call | solution.py:547
  170.6 1.7 collective-permute-start.8
  172.4 8.6 %weights_10.1.refs_1_ = f32[1536,512]{1,0:T(8,128)} custom-call(f32[1536,512]{1,0:T(8,128)} %weights_15.1.refs_0_, bf16[2560,512]{1,0:T(8,128)(2,1)} %bitcast.26, bf16[5,3,576,128]{3,2,1,0:T(8,128)(2,1)} %get-tuple-element.154.refs_2_, bf16[5,160,512]{2,1,0:T(8,128)(2,1)} %get-tuple-element.155.refs_3_, ...), custom_call_target="tpu_custom_call" | custom-call | flops 3397386240 | bytes 16777216 | tf_op jit(solution)/shard_map/weights_10/pallas_call | solution.py:668
  181.7 16.7 %backward_5.1 = (bf16[5,512,512]{2,1,0:T(8,128)(2,1)}, f32[24,128]{1,0:T(8,128)}, f32[16,256]{1,0:T(8,128)}, bf16[512,256]{1,0:T(8,128)(2,1)}, bf16[320,256]{1,0:T(8,128)(2,1)}) custom-call(f32[24,128]{1,0:T(8,128)} %get-tuple-element.156.refs_0_, f32[16,256]{1,0:T(8,128)} %get-tuple-element.157.refs_1_, bf16[512,256]{1,0:T(8,128)(2,1)} %get-tuple-element.158.refs_2_, ...), custom_call_target="tpu_custom_call" | custom-call | flops 6543114240 | bytes 8388608 | tf_op jit(solution)/shard_map/backward_5/pallas_call | solution.py:547
  198.3 1.5 collective-permute-start.9
  199.9 8.5 %weights_5.1 = (f32[2,1536,128]{2,1,0:T(8,128)}, bf16[2,1536,128]{2,1,0:T(8,128)(2,1)}, f32[8,512]{1,0:T(8,128)}) custom-call(s32[1]{0:T(128)} %bitcast.rank.refs_0_, f32[1536,512]{1,0:T(8,128)} %weights_10.1.refs_1_, bf16[2560,512]{1,0:T(8,128)(2,1)} %bitcast.49, bf16[5,3,576,128]{3,2,1,0:T(8,128)(2,1)} %get-tuple-element.164.refs_3_, ...), custom_call_target="tpu_custom_call" | custom-call | flops 3397386240 | bytes 16777216 | tf_op jit(solution)/shard_map/weights_5/pallas_call | solution.py:668
  209.1 15.1 %backward_0.1 = (bf16[5,512,512]{2,1,0:T(8,128)(2,1)}, f32[24,128]{1,0:T(8,128)}, f32[16,256]{1,0:T(8,128)}, bf16[512,256]{1,0:T(8,128)(2,1)}, bf16[320,256]{1,0:T(8,128)(2,1)}) custom-call(bf16[512,256]{1,0:T(8,128)(2,1)} %get-tuple-element.172.refs_0_, bf16[320,256]{1,0:T(8,128)(2,1)} %copy-done.21, s32[102]{0:T(128)} %pad_add_fusion.1.refs_5_.refs_2_.refs_0_.refs_4_, ...), custom_call_target="tpu_custom_call" | custom-call | flops 6543114240 | bytes 8388608 | tf_op jit(solution)/shard_map/backward_0/pallas_call | solution.py:547
  225.1 2.7 core_stage_1.1
  227.8 1.4 collective-permute-start.11
  229.2 8.3 %weights_0.1 = (f32[2,1536,128]{2,1,0:T(8,128)}, bf16[2,1536,128]{2,1,0:T(8,128)(2,1)}, f32[48,128]{1,0:T(8,128)}) custom-call(s32[1]{0:T(128)} %bitcast.rank.refs_0_, f32[24,128]{1,0:T(8,128)} %get-tuple-element.179.refs_1_, f32[24,128]{1,0:T(8,128)} %get-tuple-element.180.refs_2_, f32[8,512]{1,0:T(8,128)} %get-tuple-element.181.refs_3_, ...), custom_call_target="tpu_custom_call" | custom-call | flops 3397386240 | bytes 16777216 | tf_op jit(solution)/shard_map/weights_0/pallas_call | solution.py:668
  238.5 2.1 chip_stage_1.1
  240.5 3.4 %all-to-all-start.2 = ((bf16[8,16,1296]{2,1,0:T(8,128)(2,1)}), bf16[8,16,1296]{2,1,0:T(8,128)(2,1)S(1)}, u32[]{:S(2)}, u32[]{:S(2)}) async-start(bf16[8,16,1296]{2,1,0:T(8,128)(2,1)} %chip_stage_1.1), calls=%async_computation.2 | async-start | bytes 720896 | tf_op jit(solution)/shard_map/all_to_all | solution.py:1074
  244.0 2.8 core_stage_0.1
  246.8 1.5 collective-permute-start.13
  248.2 6.9 %all-to-all-done.2.got = bf16[8,16,1296]{2,1,0:T(8,128)(2,1)S(1)} async-done(((bf16[8,16,1296]{2,1,0:T(8,128)(2,1)}), bf16[8,16,1296]{2,1,0:T(8,128)(2,1)S(1)}, u32[]{:S(2)}, u32[]{:S(2)}) %all-to-all-start.2) | async-done | bytes 331808 | tf_op jit(solution)/shard_map/all_to_all | solution.py:1074
  255.9 1.7 sum_stage_1.1.refs_4_
  258.3 2.2 chip_stage_0.1
  260.5 5.2 %all-to-all-start.3 = ((bf16[8,16,1664]{2,1,0:T(8,128)(2,1)}), bf16[8,16,1664]{2,1,0:T(8,128)(2,1)S(1)}, u32[]{:S(2)}, u32[]{:S(2)}) async-start(bf16[8,16,1664]{2,1,0:T(8,128)(2,1)} %chip_stage_0.1), calls=%async_computation.3 | async-start | bytes 851968 | tf_op jit(solution)/shard_map/all_to_all | solution.py:1080
  265.8 1.5 collective-permute-start.15
  267.7 3.0 %collective-permute-done.16.refs_7_ = f32[16,1296]{1,0:T(8,128)S(1)} collective-permute-done((f32[16,1296]{1,0:T(8,128)S(1)}, f32[16,1296]{1,0:T(8,128)S(1)}, u32[]{:S(2)}, u32[]{:S(2)}) %collective-permute-start.16) | collective-permute-done | bytes 82976 | tf_op jit(solution)/shard_map/ppermute | solution.py:1078
  270.7 1.9 collective-permute-done.15.refs_6_
  272.7 4.3 %all-to-all-done.3.got = bf16[8,16,1664]{2,1,0:T(8,128)(2,1)S(1)} async-done(((bf16[8,16,1664]{2,1,0:T(8,128)(2,1)}), bf16[8,16,1664]{2,1,0:T(8,128)(2,1)S(1)}, u32[]{:S(2)}, u32[]{:S(2)}) %all-to-all-start.3) | async-done | bytes 426016 | tf_op jit(solution)/shard_map/all_to_all | solution.py:1080
  277.7 2.0 finish.1
  279.8 1.5 collective-permute-start.18
  281.7 3.3 %collective-permute-done.19.refs_3_ = f32[16,1296]{1,0:T(8,128)S(1)} collective-permute-done((f32[16,1296]{1,0:T(8,128)}, f32[16,1296]{1,0:T(8,128)S(1)}, u32[]{:S(2)}, u32[]{:S(2)}) %collective-permute-start.19) | collective-permute-done | bytes 82976 | tf_op jit(solution)/shard_map/ppermute | solution.py:1089
  284.9 1.9 collective-permute-done.18.refs_2_
  287.5 3.3 %update.1 = (f32[2,4,16,1296]{3,2,1,0:T(8,128)}, f32[2,4,16,1296]{3,2,1,0:T(8,128)}, f32[2,4,16,1296]{3,2,1,0:T(8,128)}, bf16[2,4,16,1296]{3,2,1,0:T(8,128)(2,1)}) custom-call(s32[1]{0:T(128)} %bitcast.rank.refs_0_, f32[8,128]{1,0:T(8,128)} %get-tuple-element.202.scalars, f32[16,1296]{1,0:T(8,128)} %get-tuple-element.203.refs_0_, f32[16,1296]{1,0:T(8,128)} %copy-done.14, ...), custom_call_target="tpu_custom_call" | custom-call | flops 1048576 | bytes 6291456 | tf_op jit(solution)/shard_map/update/pallas_call | solution.py:852
  (84 shorter events, 13.5 us)
Async XLA Ops:
  3.0 20.3 %all-to-all-start = ((bf16[8,16,1312]{2,1,0:T(8,128)(2,1)}), bf16[8,16,1312]{2,1,0:T(8,128)(2,1)S(1)}, u32[]{:S(2)}, u32[]{:S(2)}) async-start(bf16[8,16,1312]{2,1,0:T(8,128)(2,1)} %get-tuple-element.120), calls=%async_computation | async-start | bytes 720896 | tf_op jit(solution)/shard_map/all_to_all | solution.py:996
  23.3 11.6 %copy-start.6 = (bf16[8,16,1312]{2,1,0:T(8,128)(2,1)}, bf16[8,16,1312]{2,1,0:T(8,128)(2,1)S(1)}, u32[]{:S(2)}) copy-start(bf16[8,16,1312]{2,1,0:T(8,128)(2,1)S(1)} %all-to-all-done) | copy-start | bytes 1007620
  23.4 9.9 %collective-permute-start.1 = (bf16[128,1312]{1,0:T(8,128)(2,1)S(1)}, bf16[128,1312]{1,0:T(8,128)(2,1)S(1)}, u32[]{:S(2)}, u32[]{:S(2)}) collective-permute-start(bf16[128,1312]{1,0:T(8,128)(2,1)S(1)} %bitcast.27), channel_id=1, source_target_pairs={{0,16},{8,24},{16,0},{24,8},{1,17},{9,25},{17,1},{25,9},{2,18},{10... | collective-permute-start | bytes 1007624 | tf_op jit(solution)/shard_map/ppermute | solution.py:998
  25.0 28.4 %all-to-all-start.1 = ((bf16[8,32,1312]{2,1,0:T(8,128)(2,1)}), bf16[8,32,1312]{2,1,0:T(8,128)(2,1)S(1)}, u32[]{:S(2)}, u32[]{:S(2)}) async-start(bf16[8,32,1312]{2,1,0:T(8,128)(2,1)} %get-tuple-element.123), calls=%async_computation.1 | async-start | bytes 1441792 | tf_op jit(solution)/shard_map/all_to_all | solution.py:1001
  31.1 2.9 collective-permute-start
  33.3 1.7 copy-start.18
  33.3 1.7 collective-permute-start.2
  34.0 1.0 copy-start.19
  35.0 0.8 copy-start.20
  53.4 6.9 %copy-start.4 = (bf16[8,32,1312]{2,1,0:T(8,128)(2,1)}, bf16[8,32,1312]{2,1,0:T(8,128)(2,1)S(1)}, u32[]{:S(2)}) copy-start(bf16[8,32,1312]{2,1,0:T(8,128)(2,1)S(1)} %all-to-all-done.1.refs_1_) | copy-start | bytes 2015236
  53.5 6.9 %collective-permute-start.3 = (bf16[8,32,1312]{2,1,0:T(8,128)(2,1)S(1)}, bf16[8,32,1312]{2,1,0:T(8,128)(2,1)S(1)}, u32[]{:S(2)}, u32[]{:S(2)}) collective-permute-start(bf16[8,32,1312]{2,1,0:T(8,128)(2,1)S(1)} %all-to-all-done.1.refs_1_), channel_id=1, source_target_pairs={{0,8},{8,0},{16,24},{24,16},{1,9},{9,1},{17,25},{25,17},{2,10},{10... | collective-permute-start | bytes 2015240 | tf_op jit(solution)/shard_map/ppermute | solution.py:1017
  53.6 6.7 %collective-permute-start.4 = (bf16[320,256]{1,0:T(8,128)(2,1)}, bf16[320,256]{1,0:T(8,128)(2,1)S(1)}, u32[]{:S(2)}, u32[]{:S(2)}) collective-permute-start(bf16[320,256]{1,0:T(8,128)(2,1)} %get-tuple-element.132), channel_id=1, source_target_pairs={{2,0},{4,2},{6,4},{7,6},{5,7},{3,5},{1,3},{0,1},{10,8},{12,10},{14... | collective-permute-start | bytes 491528 | tf_op jit(solution)/shard_map/ppermute | solution.py:1023
  60.3 0.9 copy-start.17
  79.1 5.9 %collective-permute-start.5 = (bf16[320,256]{1,0:T(8,128)(2,1)}, bf16[320,256]{1,0:T(8,128)(2,1)S(1)}, u32[]{:S(2)}, u32[]{:S(2)}) collective-permute-start(bf16[320,256]{1,0:T(8,128)(2,1)} %get-tuple-element.134), channel_id=1, source_target_pairs={{2,0},{4,2},{6,4},{7,6},{5,7},{3,5},{1,3},{0,1},{10,8},{12,10},{14... | collective-permute-start | bytes 491528 | tf_op jit(solution)/shard_map/ppermute | solution.py:1023
  85.0 0.7 copy-start.26
  85.7 19.4 %copy-start.15 = (f32[16,128]{1,0:T(8,128)S(1)}, f32[16,128]{1,0:T(8,128)}, u32[]{:S(2)}) copy-start(f32[16,128]{1,0:T(8,128)} %refs_3_.1) | copy-start | bytes 24580
  85.7 20.0 %copy-start.16 = (f32[16]{0:T(128)S(1)}, f32[16]{0:T(128)}, u32[]{:S(2)}) copy-start(f32[16]{0:T(128)} %param.24) | copy-start | bytes 196
  103.1 5.8 %collective-permute-start.6 = (bf16[320,256]{1,0:T(8,128)(2,1)}, bf16[320,256]{1,0:T(8,128)(2,1)S(1)}, u32[]{:S(2)}, u32[]{:S(2)}) collective-permute-start(bf16[320,256]{1,0:T(8,128)(2,1)} %get-tuple-element.137), channel_id=1, source_target_pairs={{2,0},{4,2},{6,4},{7,6},{5,7},{3,5},{1,3},{0,1},{10,8},{12,10},{14... | collective-permute-start | bytes 491528 | tf_op jit(solution)/shard_map/ppermute | solution.py:1023
  143.6 10.0 %collective-permute-start.7 = (bf16[320,256]{1,0:T(8,128)(2,1)}, bf16[320,256]{1,0:T(8,128)(2,1)S(1)}, u32[]{:S(2)}, u32[]{:S(2)}) collective-permute-start(bf16[320,256]{1,0:T(8,128)(2,1)} %get-tuple-element.149), channel_id=1, source_target_pairs={{0,2},{2,4},{4,6},{6,7},{7,5},{5,3},{3,1},{1,0},{8,10},{10,12},{12... | collective-permute-start | bytes 491528 | tf_op jit(solution)/shard_map/ppermute | solution.py:1040
  153.6 0.7 copy-start.23
  170.6 10.4 %collective-permute-start.8 = (bf16[320,256]{1,0:T(8,128)(2,1)}, bf16[320,256]{1,0:T(8,128)(2,1)S(1)}, u32[]{:S(2)}, u32[]{:S(2)}) collective-permute-start(bf16[320,256]{1,0:T(8,128)(2,1)} %get-tuple-element.159), channel_id=1, source_target_pairs={{0,2},{2,4},{4,6},{6,7},{7,5},{5,3},{3,1},{1,0},{8,10},{10,12},{12... | collective-permute-start | bytes 491528 | tf_op jit(solution)/shard_map/ppermute | solution.py:1040
  181.0 0.7 copy-start.22
  198.3 10.1 %collective-permute-start.9 = (bf16[320,256]{1,0:T(8,128)(2,1)}, bf16[320,256]{1,0:T(8,128)(2,1)S(1)}, u32[]{:S(2)}, u32[]{:S(2)}) collective-permute-start(bf16[320,256]{1,0:T(8,128)(2,1)} %get-tuple-element.168), channel_id=1, source_target_pairs={{0,2},{2,4},{4,6},{6,7},{7,5},{5,3},{3,1},{1,0},{8,10},{10,12},{12... | collective-permute-start | bytes 491528 | tf_op jit(solution)/shard_map/ppermute | solution.py:1040
  208.4 0.7 copy-start.21
  208.4 15.8 %collective-permute-start.10 = (bf16[2,1536,128]{2,1,0:T(8,128)(2,1)}, bf16[2,1536,128]{2,1,0:T(8,128)(2,1)S(1)}, u32[]{:S(2)}, u32[]{:S(2)}) collective-permute-start(bf16[2,1536,128]{2,1,0:T(8,128)(2,1)} %get-tuple-element.169), channel_id=1, source_target_pairs={{0,8},{8,0},{16,24},{24,16},{1,9},{9,1},{17,25},{25,17},{2,10},{10... | collective-permute-start | bytes 2359304 | tf_op jit(solution)/shard_map/ppermute | solution.py:1066
  224.2 0.9 copy-start.2
  227.8 9.9 %collective-permute-start.11 = (bf16[1312,128]{1,0:T(8,128)(2,1)}, bf16[1312,128]{1,0:T(8,128)(2,1)S(1)}, u32[]{:S(2)}, u32[]{:S(2)}) collective-permute-start(bf16[1312,128]{1,0:T(8,128)(2,1)} %get-tuple-element.188), channel_id=1, source_target_pairs={{0,16},{8,24},{16,0},{24,8},{1,17},{9,25},{17,1},{25,9},{2,18},{10... | collective-permute-start | bytes 1007624 | tf_op jit(solution)/shard_map/ppermute | solution.py:1049
  237.7 0.7 copy-start.8
  237.7 2.8 collective-permute-start.12
  240.5 3.5 %copy-start.3 = (bf16[2,1536,128]{2,1,0:T(8,128)(2,1)}, bf16[2,1536,128]{2,1,0:T(8,128)(2,1)S(1)}, u32[]{:S(2)}) copy-start(bf16[2,1536,128]{2,1,0:T(8,128)(2,1)S(1)} %collective-permute-done.12.got) | copy-start | bytes 2359300
  240.5 14.6 %all-to-all-start.2 = ((bf16[8,16,1296]{2,1,0:T(8,128)(2,1)}), bf16[8,16,1296]{2,1,0:T(8,128)(2,1)S(1)}, u32[]{:S(2)}, u32[]{:S(2)}) async-start(bf16[8,16,1296]{2,1,0:T(8,128)(2,1)} %chip_stage_1.1), calls=%async_computation.2 | async-start | bytes 720896 | tf_op jit(solution)/shard_map/all_to_all | solution.py:1074
  246.8 10.8 %collective-permute-start.13 = (bf16[1408,128]{1,0:T(8,128)(2,1)}, bf16[1408,128]{1,0:T(8,128)(2,1)S(1)}, u32[]{:S(2)}, u32[]{:S(2)}) collective-permute-start(bf16[1408,128]{1,0:T(8,128)(2,1)} %get-tuple-element.195), channel_id=1, source_target_pairs={{0,16},{8,24},{16,0},{24,8},{1,17},{9,25},{17,1},{25,9},{2,18},{10... | collective-permute-start | bytes 1081352 | tf_op jit(solution)/shard_map/ppermute | solution.py:1076
  255.2 0.7 copy-start.1
  257.6 8.2 %copy-start.5 = (f32[16,1296]{1,0:T(8,128)S(1)}, f32[16,1296]{1,0:T(8,128)}, u32[]{:S(2)}) copy-start(f32[16,1296]{1,0:T(8,128)} %sum_stage_1.1.refs_4_) | copy-start | bytes 248836
  257.6 0.7 copy-start.7
  260.5 16.4 %all-to-all-start.3 = ((bf16[8,16,1664]{2,1,0:T(8,128)(2,1)}), bf16[8,16,1664]{2,1,0:T(8,128)(2,1)S(1)}, u32[]{:S(2)}, u32[]{:S(2)}) async-start(bf16[8,16,1664]{2,1,0:T(8,128)(2,1)} %chip_stage_0.1), calls=%async_computation.3 | async-start | bytes 851968 | tf_op jit(solution)/shard_map/all_to_all | solution.py:1080
  265.7 5.0 %collective-permute-start.16 = (f32[16,1296]{1,0:T(8,128)S(1)}, f32[16,1296]{1,0:T(8,128)S(1)}, u32[]{:S(2)}, u32[]{:S(2)}) collective-permute-start(f32[16,1296]{1,0:T(8,128)S(1)} %copy-done.5), channel_id=1, source_target_pairs={{0,24},{8,16},{16,8},{24,0},{1,25},{9,17},{17,9},{25,1},{2,26},{10... | collective-permute-start | bytes 248840 | tf_op jit(solution)/shard_map/ppermute | solution.py:1078
  265.8 6.8 %collective-permute-start.15 = (f32[16,1296]{1,0:T(8,128)S(1)}, f32[16,1296]{1,0:T(8,128)S(1)}, u32[]{:S(2)}, u32[]{:S(2)}) collective-permute-start(f32[16,1296]{1,0:T(8,128)S(1)} %copy-done.5), channel_id=1, source_target_pairs={{0,16},{8,24},{16,0},{24,8},{1,17},{9,25},{17,1},{25,9},{2,18},{10... | collective-permute-start | bytes 248840 | tf_op jit(solution)/shard_map/ppermute | solution.py:1078
  267.3 5.3 %collective-permute-start.14 = (f32[16,1296]{1,0:T(8,128)S(1)}, f32[16,1296]{1,0:T(8,128)S(1)}, u32[]{:S(2)}, u32[]{:S(2)}) collective-permute-start(f32[16,1296]{1,0:T(8,128)S(1)} %copy-done.5), channel_id=1, source_target_pairs={{0,8},{8,0},{16,24},{24,16},{1,9},{9,1},{17,25},{25,17},{2,10},{10... | collective-permute-start | bytes 248840 | tf_op jit(solution)/shard_map/ppermute | solution.py:1078
  270.7 16.2 %copy-start.9 = (f32[16,1296]{1,0:T(8,128)}, f32[16,1296]{1,0:T(8,128)S(1)}, u32[]{:S(2)}) copy-start(f32[16,1296]{1,0:T(8,128)S(1)} %collective-permute-done.16.refs_7_) | copy-start | bytes 248836
  272.6 14.2 %copy-start.10 = (f32[16,1296]{1,0:T(8,128)}, f32[16,1296]{1,0:T(8,128)S(1)}, u32[]{:S(2)}) copy-start(f32[16,1296]{1,0:T(8,128)S(1)} %collective-permute-done.15.refs_6_) | copy-start | bytes 248836
  272.7 14.2 %copy-start.11 = (f32[16,1296]{1,0:T(8,128)}, f32[16,1296]{1,0:T(8,128)S(1)}, u32[]{:S(2)}) copy-start(f32[16,1296]{1,0:T(8,128)S(1)} %collective-permute-done.14.refs_5_) | copy-start | bytes 248836
  276.9 0.8 copy-start
  279.7 5.2 %collective-permute-start.19 = (f32[16,1296]{1,0:T(8,128)}, f32[16,1296]{1,0:T(8,128)S(1)}, u32[]{:S(2)}, u32[]{:S(2)}) collective-permute-start(f32[16,1296]{1,0:T(8,128)} %get-tuple-element.203.refs_0_), channel_id=1, source_target_pairs={{0,24},{8,16},{16,8},{24,0},{1,25},{9,17},{17,9},{25,1},{2,26},{10... | collective-permute-start | bytes 248840 | tf_op jit(solution)/shard_map/ppermute | solution.py:1089
  279.8 7.0 %collective-permute-start.18 = (f32[16,1296]{1,0:T(8,128)}, f32[16,1296]{1,0:T(8,128)S(1)}, u32[]{:S(2)}, u32[]{:S(2)}) collective-permute-start(f32[16,1296]{1,0:T(8,128)} %get-tuple-element.203.refs_0_), channel_id=1, source_target_pairs={{0,16},{8,24},{16,0},{24,8},{1,17},{9,25},{17,1},{25,9},{2,18},{10... | collective-permute-start | bytes 248840 | tf_op jit(solution)/shard_map/ppermute | solution.py:1089
  281.3 5.5 %collective-permute-start.17 = (f32[16,1296]{1,0:T(8,128)}, f32[16,1296]{1,0:T(8,128)S(1)}, u32[]{:S(2)}, u32[]{:S(2)}) collective-permute-start(f32[16,1296]{1,0:T(8,128)} %get-tuple-element.203.refs_0_), channel_id=1, source_target_pairs={{0,8},{8,0},{16,24},{24,16},{1,9},{9,1},{17,25},{25,17},{2,10},{10... | collective-permute-start | bytes 248840 | tf_op jit(solution)/shard_map/ppermute | solution.py:1089
  284.9 2.0 copy-start.12
  286.9 0.7 copy-start.14
  (3 other events, 2.0 us)
where the time goes:
time: 292 us; the launch traced here: 291 us
  Pallas kernels  198 us (68%)
  starting transfers between devices  41.1 us (14%)
  waiting for transfers between devices  36.4 us (12%)
  local copies, waits for them, and re-layouts  11.5 us (4%)
    pallas_call x4, Pallas kernels, forward_call(): pl.pallas_call(functools.partial(forward_kernel, geo, layer, base, steps,...  70.3 us
    pallas_call x4, Pallas kernels, backward_call(): pl.pallas_call(functools.partial(backward_kernel, geo, layer, base, steps...  64.7 us
    pallas_call x4, Pallas kernels, weight_call(): pl.pallas_call(functools.partial(weight_kernel, geo, base, steps, acc is...  33.7 us
    pallas_call x7, Pallas kernels, plain_call(): pl.pallas_call(kernel, in_specs=specs, out_shape=out_shape, compiler_para...  15.8 us
    ppermute x3, waiting for transfers between devices, on_device(): far = lax.ppermute(got[6], 'gate', from_right)  11.6 us
    pallas_call x1, Pallas kernels, window_call(): pl.pallas_call(functools.partial(window_kernel, geo), in_specs=[smem, vme...  10.4 us
    unnamed x54, local copies, waits for them, and re-layouts  9.44 us
    all_to_all x1, starting transfers between devices, on_device(): lax.all_to_all(mine0, 'gate', 0, 0, tiled=True)  7.31 us
  transfers between devices with their start and end apart: 24, of which 12 were waited for; matrix products, arithmetic and copies ran while one was open for 1% of the time, Pallas kernels for 29%

commit v1 on v0

--- a/solution.py
+++ b/solution.py
@@ -249,14 +249,11 @@
         hb[:, front * rows :, :] = jnp.zeros((3, rows, 128), BF16)
         if first:
             hb[:, : front * rows, :] = jnp.zeros((3, front * rows, 128), BF16)
-            hnext[...] = jnp.zeros_like(hnext)
             cb[...] = jnp.zeros_like(cb)
         else:
             nb = back * rows
             make_variants(geo, near[:, :128].astype(F32), 0, hb, mrm, mrp, base)
             make_variants(geo, far[:, :128].astype(F32), nb, hb, mrm, mrp, base)
-            for c in (0, front - 1):
-                hnext[:, c * rows : (c + 1) * rows, :] = jnp.zeros((3, rows, 128), BF16)
             cb[:nb, :] = near[:, 128:].astype(F32)
             cb[nb:, :] = far[:, 128:].astype(F32)
         if gather:
@@ -281,19 +278,17 @@
         for k, row in enumerate(peephole_rows(wf)):
             peeps[k : k + 1, :] = row
 
-    s0, sn = (2 * halo - 1) * rows, (own + 2) * rows
-    for v in range(3):
-        hvar_out[0, v, :, :] = hb[v, s0 : s0 + sn, :]
-    cprev_out[0, :, :] = cb[halo * rows : (halo + back) * rows, :].astype(BF16)
-    for tap, (dr, dc) in enumerate(TAPS):
-        off = x0 + dc * rows + dr
-        part = slice(tap * chans, (tap + 1) * chans)
-        xs[part, :] = win[:, off : off + lanes] * keeps[part, :]
-    q0 = (2 * halo - 1) * rows
-    xown_out[0, :, :] = xs[:, q0 : q0 + own * rows]
-
-    for c0, cw in cut_by_four(front - 2, 4):
+    def input_taps(a, m):
+        for tap, (dr, dc) in enumerate(TAPS):
+            off = x0 + a + dc * rows + dr
+            part = slice(tap * chans, (tap + 1) * chans)
+            xs[part, a : a + m] = win[:, off : off + m] * keeps[part, a : a + m]
+
+    chunks = cut_by_four(front - 2, 2)
+    for c0, cw in chunks:
         r0, m = (c0 + 1) * rows, cw * rows
+        final = c0 == chunks[-1][0]
+        input_taps(c0 * rows, m)
         zero = front * rows
         lefts, rights = [], []
         for c in range(c0 + 1, c0 + 1 + cw):
@@ -307,27 +302,32 @@
         z = dot_nt(jnp.concatenate(parts, 1), wf[:, : 9 * 128]) + lax.dot_general(
             xs[:, r0 - rows : r0 - rows + m], wf[:, 9 * 128 :], (((0,), (1,)), ((), ())), preferred_element_type=F32
         )
-        c = cb[r0 : r0 + m, :]
-        gi = logistic(z[:, 0:128] + peeps[0:1, :] * c)
-        gf = logistic(z[:, 128:256] + peeps[1:2, :] * c)
-        gg = jnp.tanh(z[:, 384:512])
-        cn = gf * c + gi * gg
-        go = logistic(z[:, 256:384] + peeps[2:3, :] * cn)
-        h = go * jnp.tanh(cn)
-        cb[r0 : r0 + m, :] = cn
-        make_variants(geo, h, r0, hnext, mrm, mrp, base)
-        lo, hi = max(c0 + 1, halo), min(c0 + 1 + cw, halo + back)
-        a, b = (lo - c0 - 1) * rows, (hi - c0 - 1) * rows
-        o = (lo - halo) * rows
-        n = b - a
-        if n > 0:
-            gates_out[0, 0, o : o + n, :] = gi[a:b].astype(BF16)
-            gates_out[0, 1, o : o + n, :] = gf[a:b].astype(BF16)
-            gates_out[0, 2, o : o + n, :] = go[a:b].astype(BF16)
-            gates_out[0, 3, o : o + n, :] = gg[a:b].astype(BF16)
-            hnew_out[0, o : o + n, :] = h[a:b].astype(BF16)
-
-    hb[:, : front * rows, :] = hnext[...]
+        if final:
+            s0, sn = (2 * halo - 1) * rows, (own + 2) * rows
+            hvar_out[0, :, :, :] = hb[:, s0 : s0 + sn, :]
+            hb[:, rows:r0, :] = hnext[:, rows:r0, :]
+        for c in range(c0 + 1, c0 + 1 + cw):
+            at = slice(c * rows, (c + 1) * rows)
+            zi, zf, zo, zg = (z[(c - c0 - 1) * rows : (c - c0) * rows, n * 128 : (n + 1) * 128] for n in range(4))
+            cell = cb[at, :]
+            if halo <= c < halo + back:
+                cprev_out[0, (c - halo) * rows : (c - halo + 1) * rows, :] = cell.astype(BF16)
+            gi = logistic(zi + peeps[0:1, :] * cell)
+            gf = logistic(zf + peeps[1:2, :] * cell)
+            gg = jnp.tanh(zg)
+            cell = gf * cell + gi * gg
+            go = logistic(zo + peeps[2:3, :] * cell)
+            h = go * jnp.tanh(cell)
+            cb[at, :] = cell
+            make_variants(geo, h, c * rows, hb if final else hnext, mrm, mrp, base)
+            if halo <= c < halo + back:
+                out = slice((c - halo) * rows, (c - halo + 1) * rows)
+                for n, gate in enumerate((gi, gf, go, gg)):
+                    gates_out[0, n, out, :] = gate.astype(BF16)
+                hnew_out[0, out, :] = h.astype(BF16)
+
+    q0 = (2 * halo - 1) * rows
+    xown_out[0, :, :] = xs[:, q0 : q0 + own * rows]
 
     @pl.when(step == steps - 1)
     def _():
@@ -493,10 +493,10 @@
         below = pltpu.roll(acc[:, 256:] * mrp[g0 : g0 + m, :].astype(F32), 1, 0)
         dh[r0 : r0 + m, :] = (acc[:, 128:256] + above + below).astype(BF16)
 
-    for c0, cw in cut(half + 1, 2):
+    for c0, cw in cut(half + 1, max(1, (half + 1) // 1)):
         gates_chunk(c0, cw)
     hidden_chunk(0, half)
-    for c0, cw in cut(back - half - 1, 2):
+    for c0, cw in cut(back - half - 1, max(1, (back - half - 1) // 1)):
         gates_chunk(half + 1 + c0, cw)
     hidden_chunk(half, back - half)
     lo = (half + 1 - halo) * rows

time: 292 us -> 286 us (0.979)
  Pallas kernels: 198 us -> 193 us
    pallas_call x4, Pallas kernels: 64.7 us -> 61.1 us  [backward_call(): pl.pallas_call(functools.partial(backward_kernel, geo, layer, base, steps...]
where the time goes in v1:
time: 286 us; the launch traced here: 285 us
  Pallas kernels  193 us (67%)
  starting transfers between devices  41.2 us (14%)
  waiting for transfers between devices  36.3 us (13%)
  local copies, waits for them, and re-layouts  11.5 us (4%)
    pallas_call x4, Pallas kernels, forward_call(): pl.pallas_call(functools.partial(forward_kernel, geo, layer, base, steps,...  68.3 us
    pallas_call x4, Pallas kernels, backward_call(): pl.pallas_call(functools.partial(backward_kernel, geo, layer, base, steps...  61.1 us
    pallas_call x4, Pallas kernels, weight_call(): pl.pallas_call(functools.partial(weight_kernel, geo, base, steps, acc is...  33.7 us
    pallas_call x7, Pallas kernels, plain_call(): pl.pallas_call(kernel, in_specs=specs, out_shape=out_shape, compiler_para...  15.8 us
    ppermute x3, waiting for transfers between devices, on_device(): far = lax.ppermute(got[6], 'gate', from_right)  11.5 us
    pallas_call x1, Pallas kernels, window_call(): pl.pallas_call(functools.partial(window_kernel, geo), in_specs=[smem, vme...  10.4 us
    unnamed x54, local copies, waits for them, and re-layouts  9.44 us
    all_to_all x1, starting transfers between devices, on_device(): lax.all_to_all(mine0, 'gate', 0, 0, tiled=True)  7.31 us
  transfers between devices with their start and end apart: 24, of which 12 were waited for; matrix products, arithmetic and copies ran while one was open for 1% of the time, Pallas kernels for 29%

profile of v1, /device:TPU:0, one launch (start us, length us, event | category | flops | bytes accessed | tf_op | source)
XLA Modules:
  0.0 285.4 jit_solution(1648395225096092430)
XLA Ops:
  0.7 2.4 pack.1
  3.0 7.3 %all-to-all-start = ((bf16[8,16,1312]{2,1,0:T(8,128)(2,1)}), bf16[8,16,1312]{2,1,0:T(8,128)(2,1)S(1)}, u32[]{:S(2)}, u32[]{:S(2)}) async-start(bf16[8,16,1312]{2,1,0:T(8,128)(2,1)} %get-tuple-element.120), calls=%async_computation | async-start | bytes 720896 | tf_op jit(solution)/shard_map/all_to_all | solution.py:996
  10.3 1.2 dynamic_slice.6
  12.9 10.4 %window.1 = (bf16[320,1792]{1,0:T(8,128)(2,1)}, f32[16,1792]{1,0:T(8,128)}, bf16[1632,128]{1,0:T(8,128)(2,1)}, bf16[1632,128]{1,0:T(8,128)(2,1)}, bf16[1632,128]...) custom-call(s32[1]{0:T(128)} %bitcast.4.start, bf16[320,4096]{1,0:T(8,128)(2,1)} %bitcast.38, ...), custom_call_target="tpu_custom_call" | custom-call | flops 4932501504 | bytes 10485760 | tf_op jit(solution)/shard_map/window/pallas_call | solution.py:149
  23.4 1.6 collective-permute-start.1
  25.0 6.0 %all-to-all-start.1 = ((bf16[8,32,1312]{2,1,0:T(8,128)(2,1)}), bf16[8,32,1312]{2,1,0:T(8,128)(2,1)S(1)}, u32[]{:S(2)}, u32[]{:S(2)}) async-start(bf16[8,32,1312]{2,1,0:T(8,128)(2,1)} %get-tuple-element.123), calls=%async_computation.1 | async-start | bytes 1441792 | tf_op jit(solution)/shard_map/all_to_all | solution.py:1001
  31.1 2.2 collective-permute-done.1.refs_3_
  34.0 1.0 collective-permute-done.2.refs_4_
  35.7 17.1 %forward_0.1 = (bf16[5,4,832,128]{3,2,1,0:T(8,128)(2,1)}, bf16[5,832,128]{2,1,0:T(8,128)(2,1)}, bf16[5,3,576,128]{3,2,1,0:T(8,128)(2,1)}, bf16[5,832,128]{2,1,0:...) custom-call(s32[1]{0:T(128)} %bitcast.rank.refs_0_, ...), custom_call_target="tpu_custom_call" | custom-call | flops 7644119040 | bytes 8388608 | tf_op jit(solution)/shard_map/forward_0/pallas_call | solution.py:373
  53.1 1.7 collective-permute-start.4
  54.8 5.0 %collective-permute-done.4.refs_4_ = bf16[320,256]{1,0:T(8,128)(2,1)S(1)} collective-permute-done((bf16[320,256]{1,0:T(8,128)(2,1)}, bf16[320,256]{1,0:T(8,128)(2,1)S(1)}, u32[]{:S(2)}, u32[]{:S(2)}) %collective-permute-start.4) | collective-permute-done | bytes 163872 | tf_op jit(solution)/shard_map/ppermute | solution.py:1023
  60.7 17.4 %forward_5.1 = (bf16[5,4,832,128]{3,2,1,0:T(8,128)(2,1)}, bf16[5,832,128]{2,1,0:T(8,128)(2,1)}, bf16[5,3,576,128]{3,2,1,0:T(8,128)(2,1)}, bf16[5,832,128]{2,1,0:...) custom-call(s32[1]{0:T(128)} %bitcast.rank.refs_0_, ...), custom_call_target="tpu_custom_call" | custom-call | flops 7644119040 | bytes 8388608 | tf_op jit(solution)/shard_map/forward_5/pallas_call | solution.py:373
  78.1 1.8 collective-permute-start.5
  79.9 4.1 %collective-permute-done.5.refs_1_ = bf16[320,256]{1,0:T(8,128)(2,1)S(1)} collective-permute-done((bf16[320,256]{1,0:T(8,128)(2,1)}, bf16[320,256]{1,0:T(8,128)(2,1)S(1)}, u32[]{:S(2)}, u32[]{:S(2)}) %collective-permute-start.5) | collective-permute-done | bytes 163872 | tf_op jit(solution)/shard_map/ppermute | solution.py:1023
  84.7 16.9 %forward_10.1 = (bf16[5,4,832,128]{3,2,1,0:T(8,128)(2,1)}, bf16[5,832,128]{2,1,0:T(8,128)(2,1)}, bf16[5,3,576,128]{3,2,1,0:T(8,128)(2,1)}, bf16[5,832,128]{2,1,0...) custom-call(bf16[832,256]{1,0:T(8,128)(2,1)} %get-tuple-element.133.refs_0_, ...), custom_call_target="tpu_custom_call" | custom-call | flops 7644119040 | bytes 8388608 | tf_op jit(solution)/shard_map/forward_10/pallas_call | solution.py:373
  101.6 2.0 collective-permute-start.6
  104.9 2.5 collective-permute-done.6.refs_1_
  108.0 16.9 %forward_15.1 = (bf16[5,4,832,128]{3,2,1,0:T(8,128)(2,1)}, bf16[5,832,128]{2,1,0:T(8,128)(2,1)}, bf16[5,3,576,128]{3,2,1,0:T(8,128)(2,1)}, bf16[5,832,128]{2,1,0...) custom-call(bf16[832,256]{1,0:T(8,128)(2,1)} %get-tuple-element.136.refs_0_, ...), custom_call_target="tpu_custom_call" | custom-call | flops 7644119040 | bytes 8388608 | tf_op jit(solution)/shard_map/forward_15/pallas_call | solution.py:373
  125.0 15.8 %backward_15.1 = (bf16[5,512,512]{2,1,0:T(8,128)(2,1)}, f32[24,128]{1,0:T(8,128)}, f32[16,256]{1,0:T(8,128)}, bf16[512,256]{1,0:T(8,128)(2,1)}, bf16[320,256]{1,0:T(8,128)(2,1)}) custom-call(s32[102]{0:T(128)} %pad_add_fusion.1.refs_5_.refs_2_.refs_0_.refs_4_, bf16[5,4,832,128]{3,2,1,0:T(8,128)(2,1)} %get-tuple-element.138.refs_1_, ...), custom_call_target="tpu_custom_call" | custom-call | flops 6543114240 | bytes 8388608 | tf_op jit(solution)/shard_map/backward_15/pallas_call | solution.py:547
  140.8 1.8 collective-permute-start.7
  142.6 8.2 %weights_15.1.refs_0_ = f32[1536,512]{1,0:T(8,128)} custom-call(bf16[2560,512]{1,0:T(8,128)(2,1)} %bitcast.50, bf16[5,3,576,128]{3,2,1,0:T(8,128)(2,1)} %get-tuple-element.142.refs_1_, bf16[5,160,512]{2,1,0:T(8,128)(2,1)} %get-tuple-element.143.refs_2_, bf16[1632,128]{1,0:T(8,128)(2,1)} %get-tuple-element.144.refs_3_.refs_4_.refs_5_.refs_9_, ...), custom_call_target="tpu_custom_call" | custom-call | flops 3397386240 | bytes 16777216 | tf_op jit(solution)/shard_map/weights_15/pallas_call | solution.py:668
  151.4 15.4 %backward_10.1 = (bf16[5,512,512]{2,1,0:T(8,128)(2,1)}, f32[24,128]{1,0:T(8,128)}, f32[16,256]{1,0:T(8,128)}, bf16[512,256]{1,0:T(8,128)(2,1)}, bf16[320,256]{1,0:T(8,128)(2,1)}) custom-call(f32[24,128]{1,0:T(8,128)} %get-tuple-element.146.refs_0_, f32[16,256]{1,0:T(8,128)} %get-tuple-element.147.refs_1_, bf16[512,256]{1,0:T(8,128)(2,1)} %get-tuple-element.148.refs_2_, ...), custom_call_target="tpu_custom_call" | custom-call | flops 6543114240 | bytes 8388608 | tf_op jit(solution)/shard_map/backward_10/pallas_call | solution.py:547
  166.8 1.5 collective-permute-start.8
  168.3 8.6 %weights_10.1.refs_1_ = f32[1536,512]{1,0:T(8,128)} custom-call(f32[1536,512]{1,0:T(8,128)} %weights_15.1.refs_0_, bf16[2560,512]{1,0:T(8,128)(2,1)} %bitcast.26, bf16[5,3,576,128]{3,2,1,0:T(8,128)(2,1)} %get-tuple-element.154.refs_2_, bf16[5,160,512]{2,1,0:T(8,128)(2,1)} %get-tuple-element.155.refs_3_, ...), custom_call_target="tpu_custom_call" | custom-call | flops 3397386240 | bytes 16777216 | tf_op jit(solution)/shard_map/weights_10/pallas_call | solution.py:668
  177.6 16.0 %backward_5.1 = (bf16[5,512,512]{2,1,0:T(8,128)(2,1)}, f32[24,128]{1,0:T(8,128)}, f32[16,256]{1,0:T(8,128)}, bf16[512,256]{1,0:T(8,128)(2,1)}, bf16[320,256]{1,0:T(8,128)(2,1)}) custom-call(f32[24,128]{1,0:T(8,128)} %get-tuple-element.156.refs_0_, f32[16,256]{1,0:T(8,128)} %get-tuple-element.157.refs_1_, bf16[512,256]{1,0:T(8,128)(2,1)} %get-tuple-element.158.refs_2_, ...), custom_call_target="tpu_custom_call" | custom-call | flops 6543114240 | bytes 8388608 | tf_op jit(solution)/shard_map/backward_5/pallas_call | solution.py:547
  193.6 1.7 collective-permute-start.9
  195.3 8.5 %weights_5.1 = (f32[2,1536,128]{2,1,0:T(8,128)}, bf16[2,1536,128]{2,1,0:T(8,128)(2,1)}, f32[8,512]{1,0:T(8,128)}) custom-call(s32[1]{0:T(128)} %bitcast.rank.refs_0_, f32[1536,512]{1,0:T(8,128)} %weights_10.1.refs_1_, bf16[2560,512]{1,0:T(8,128)(2,1)} %bitcast.49, bf16[5,3,576,128]{3,2,1,0:T(8,128)(2,1)} %get-tuple-element.164.refs_3_, ...), custom_call_target="tpu_custom_call" | custom-call | flops 3397386240 | bytes 16777216 | tf_op jit(solution)/shard_map/weights_5/pallas_call | solution.py:668
  204.6 13.9 %backward_0.1 = (bf16[5,512,512]{2,1,0:T(8,128)(2,1)}, f32[24,128]{1,0:T(8,128)}, f32[16,256]{1,0:T(8,128)}, bf16[512,256]{1,0:T(8,128)(2,1)}, bf16[320,256]{1,0:T(8,128)(2,1)}) custom-call(bf16[512,256]{1,0:T(8,128)(2,1)} %get-tuple-element.172.refs_0_, bf16[320,256]{1,0:T(8,128)(2,1)} %copy-done.21, s32[102]{0:T(128)} %pad_add_fusion.1.refs_5_.refs_2_.refs_0_.refs_4_, ...), custom_call_target="tpu_custom_call" | custom-call | flops 6543114240 | bytes 8388608 | tf_op jit(solution)/shard_map/backward_0/pallas_call | solution.py:547
  219.4 2.7 core_stage_1.1
  222.1 1.5 collective-permute-start.11
  223.6 8.3 %weights_0.1 = (f32[2,1536,128]{2,1,0:T(8,128)}, bf16[2,1536,128]{2,1,0:T(8,128)(2,1)}, f32[48,128]{1,0:T(8,128)}) custom-call(s32[1]{0:T(128)} %bitcast.rank.refs_0_, f32[24,128]{1,0:T(8,128)} %get-tuple-element.179.refs_1_, f32[24,128]{1,0:T(8,128)} %get-tuple-element.180.refs_2_, f32[8,512]{1,0:T(8,128)} %get-tuple-element.181.refs_3_, ...), custom_call_target="tpu_custom_call" | custom-call | flops 3397386240 | bytes 16777216 | tf_op jit(solution)/shard_map/weights_0/pallas_call | solution.py:668
  232.8 2.1 chip_stage_1.1
  234.9 3.4 %all-to-all-start.2 = ((bf16[8,16,1296]{2,1,0:T(8,128)(2,1)}), bf16[8,16,1296]{2,1,0:T(8,128)(2,1)S(1)}, u32[]{:S(2)}, u32[]{:S(2)}) async-start(bf16[8,16,1296]{2,1,0:T(8,128)(2,1)} %chip_stage_1.1), calls=%async_computation.2 | async-start | bytes 720896 | tf_op jit(solution)/shard_map/all_to_all | solution.py:1074
  238.3 2.8 core_stage_0.1
  241.1 1.5 collective-permute-start.13
  242.6 6.9 %all-to-all-done.2.got = bf16[8,16,1296]{2,1,0:T(8,128)(2,1)S(1)} async-done(((bf16[8,16,1296]{2,1,0:T(8,128)(2,1)}), bf16[8,16,1296]{2,1,0:T(8,128)(2,1)S(1)}, u32[]{:S(2)}, u32[]{:S(2)}) %all-to-all-start.2) | async-done | bytes 331808 | tf_op jit(solution)/shard_map/all_to_all | solution.py:1074
  250.2 1.7 sum_stage_1.1.refs_4_
  252.6 2.2 chip_stage_0.1
  254.9 5.2 %all-to-all-start.3 = ((bf16[8,16,1664]{2,1,0:T(8,128)(2,1)}), bf16[8,16,1664]{2,1,0:T(8,128)(2,1)S(1)}, u32[]{:S(2)}, u32[]{:S(2)}) async-start(bf16[8,16,1664]{2,1,0:T(8,128)(2,1)} %chip_stage_0.1), calls=%async_computation.3 | async-start | bytes 851968 | tf_op jit(solution)/shard_map/all_to_all | solution.py:1080
  260.1 1.6 collective-permute-start.15
  262.0 3.0 %collective-permute-done.16.refs_7_ = f32[16,1296]{1,0:T(8,128)S(1)} collective-permute-done((f32[16,1296]{1,0:T(8,128)S(1)}, f32[16,1296]{1,0:T(8,128)S(1)}, u32[]{:S(2)}, u32[]{:S(2)}) %collective-permute-start.16) | collective-permute-done | bytes 82976 | tf_op jit(solution)/shard_map/ppermute | solution.py:1078
  265.0 2.0 collective-permute-done.15.refs_6_
  267.0 4.3 %all-to-all-done.3.got = bf16[8,16,1664]{2,1,0:T(8,128)(2,1)S(1)} async-done(((bf16[8,16,1664]{2,1,0:T(8,128)(2,1)}), bf16[8,16,1664]{2,1,0:T(8,128)(2,1)S(1)}, u32[]{:S(2)}, u32[]{:S(2)}) %all-to-all-start.3) | async-done | bytes 426016 | tf_op jit(solution)/shard_map/all_to_all | solution.py:1080
  272.0 2.0 finish.1
  274.2 1.6 collective-permute-start.18
  276.0 3.2 %collective-permute-done.19.refs_3_ = f32[16,1296]{1,0:T(8,128)S(1)} collective-permute-done((f32[16,1296]{1,0:T(8,128)}, f32[16,1296]{1,0:T(8,128)S(1)}, u32[]{:S(2)}, u32[]{:S(2)}) %collective-permute-start.19) | collective-permute-done | bytes 82976 | tf_op jit(solution)/shard_map/ppermute | solution.py:1089
  279.2 2.0 collective-permute-done.18.refs_2_
  281.9 3.3 %update.1 = (f32[2,4,16,1296]{3,2,1,0:T(8,128)}, f32[2,4,16,1296]{3,2,1,0:T(8,128)}, f32[2,4,16,1296]{3,2,1,0:T(8,128)}, bf16[2,4,16,1296]{3,2,1,0:T(8,128)(2,1)}) custom-call(s32[1]{0:T(128)} %bitcast.rank.refs_0_, f32[8,128]{1,0:T(8,128)} %get-tuple-element.202.scalars, f32[16,1296]{1,0:T(8,128)} %get-tuple-element.203.refs_0_, f32[16,1296]{1,0:T(8,128)} %copy-done.14, ...), custom_call_target="tpu_custom_call" | custom-call | flops 1048576 | bytes 6291456 | tf_op jit(solution)/shard_map/update/pallas_call | solution.py:852
  (84 shorter events, 13.3 us)
Async XLA Ops:
  3.0 20.3 %all-to-all-start = ((bf16[8,16,1312]{2,1,0:T(8,128)(2,1)}), bf16[8,16,1312]{2,1,0:T(8,128)(2,1)S(1)}, u32[]{:S(2)}, u32[]{:S(2)}) async-start(bf16[8,16,1312]{2,1,0:T(8,128)(2,1)} %get-tuple-element.120), calls=%async_computation | async-start | bytes 720896 | tf_op jit(solution)/shard_map/all_to_all | solution.py:996
  23.3 11.6 %copy-start.6 = (bf16[8,16,1312]{2,1,0:T(8,128)(2,1)}, bf16[8,16,1312]{2,1,0:T(8,128)(2,1)S(1)}, u32[]{:S(2)}) copy-start(bf16[8,16,1312]{2,1,0:T(8,128)(2,1)S(1)} %all-to-all-done) | copy-start | bytes 1007620
  23.4 9.9 %collective-permute-start.1 = (bf16[128,1312]{1,0:T(8,128)(2,1)S(1)}, bf16[128,1312]{1,0:T(8,128)(2,1)S(1)}, u32[]{:S(2)}, u32[]{:S(2)}) collective-permute-start(bf16[128,1312]{1,0:T(8,128)(2,1)S(1)} %bitcast.27), channel_id=1, source_target_pairs={{0,16},{8,24},{16,0},{24,8},{1,17},{9,25},{17,1},{25,9},{2,18},{10... | collective-permute-start | bytes 1007624 | tf_op jit(solution)/shard_map/ppermute | solution.py:998
  25.0 27.9 %all-to-all-start.1 = ((bf16[8,32,1312]{2,1,0:T(8,128)(2,1)}), bf16[8,32,1312]{2,1,0:T(8,128)(2,1)S(1)}, u32[]{:S(2)}, u32[]{:S(2)}) async-start(bf16[8,32,1312]{2,1,0:T(8,128)(2,1)} %get-tuple-element.123), calls=%async_computation.1 | async-start | bytes 1441792 | tf_op jit(solution)/shard_map/all_to_all | solution.py:1001
  31.1 2.9 %collective-permute-start = (bf16[128,1312]{1,0:T(8,128)(2,1)S(1)}, bf16[128,1312]{1,0:T(8,128)(2,1)S(1)}, u32[]{:S(2)}, u32[]{:S(2)}) collective-permute-start(bf16[128,1312]{1,0:T(8,128)(2,1)S(1)} %bitcast.28), channel_id=1, source_target_pairs={{0,8},{8,0},{16,24},{24,16},{1,9},{9,1},{17,25},{25,17},{2,10},{10... | collective-permute-start | bytes 1007624 | tf_op jit(solution)/shard_map/ppermute | solution.py:999
  33.3 1.7 copy-start.18
  33.3 1.7 collective-permute-start.2
  34.0 1.0 copy-start.19
  35.0 0.8 copy-start.20
  52.9 6.9 %copy-start.4 = (bf16[8,32,1312]{2,1,0:T(8,128)(2,1)}, bf16[8,32,1312]{2,1,0:T(8,128)(2,1)S(1)}, u32[]{:S(2)}) copy-start(bf16[8,32,1312]{2,1,0:T(8,128)(2,1)S(1)} %all-to-all-done.1.refs_1_) | copy-start | bytes 2015236
  52.9 6.9 %collective-permute-start.3 = (bf16[8,32,1312]{2,1,0:T(8,128)(2,1)S(1)}, bf16[8,32,1312]{2,1,0:T(8,128)(2,1)S(1)}, u32[]{:S(2)}, u32[]{:S(2)}) collective-permute-start(bf16[8,32,1312]{2,1,0:T(8,128)(2,1)S(1)} %all-to-all-done.1.refs_1_), channel_id=1, source_target_pairs={{0,8},{8,0},{16,24},{24,16},{1,9},{9,1},{17,25},{25,17},{2,10},{10... | collective-permute-start | bytes 2015240 | tf_op jit(solution)/shard_map/ppermute | solution.py:1017
  53.1 6.7 %collective-permute-start.4 = (bf16[320,256]{1,0:T(8,128)(2,1)}, bf16[320,256]{1,0:T(8,128)(2,1)S(1)}, u32[]{:S(2)}, u32[]{:S(2)}) collective-permute-start(bf16[320,256]{1,0:T(8,128)(2,1)} %get-tuple-element.132), channel_id=1, source_target_pairs={{2,0},{4,2},{6,4},{7,6},{5,7},{3,5},{1,3},{0,1},{10,8},{12,10},{14... | collective-permute-start | bytes 491528 | tf_op jit(solution)/shard_map/ppermute | solution.py:1023
  59.8 0.7 copy-start.24
  59.8 0.9 copy-start.17
  78.1 5.9 %collective-permute-start.5 = (bf16[320,256]{1,0:T(8,128)(2,1)}, bf16[320,256]{1,0:T(8,128)(2,1)S(1)}, u32[]{:S(2)}, u32[]{:S(2)}) collective-permute-start(bf16[320,256]{1,0:T(8,128)(2,1)} %get-tuple-element.134), channel_id=1, source_target_pairs={{2,0},{4,2},{6,4},{7,6},{5,7},{3,5},{1,3},{0,1},{10,8},{12,10},{14... | collective-permute-start | bytes 491528 | tf_op jit(solution)/shard_map/ppermute | solution.py:1023
  84.7 19.0 %copy-start.15 = (f32[16,128]{1,0:T(8,128)S(1)}, f32[16,128]{1,0:T(8,128)}, u32[]{:S(2)}) copy-start(f32[16,128]{1,0:T(8,128)} %refs_3_.1) | copy-start | bytes 24580
  84.7 19.6 %copy-start.16 = (f32[16]{0:T(128)S(1)}, f32[16]{0:T(128)}, u32[]{:S(2)}) copy-start(f32[16]{0:T(128)} %param.24) | copy-start | bytes 196
  101.6 5.8 %collective-permute-start.6 = (bf16[320,256]{1,0:T(8,128)(2,1)}, bf16[320,256]{1,0:T(8,128)(2,1)S(1)}, u32[]{:S(2)}, u32[]{:S(2)}) collective-permute-start(bf16[320,256]{1,0:T(8,128)(2,1)} %get-tuple-element.137), channel_id=1, source_target_pairs={{2,0},{4,2},{6,4},{7,6},{5,7},{3,5},{1,3},{0,1},{10,8},{12,10},{14... | collective-permute-start | bytes 491528 | tf_op jit(solution)/shard_map/ppermute | solution.py:1023
  140.8 10.0 %collective-permute-start.7 = (bf16[320,256]{1,0:T(8,128)(2,1)}, bf16[320,256]{1,0:T(8,128)(2,1)S(1)}, u32[]{:S(2)}, u32[]{:S(2)}) collective-permute-start(bf16[320,256]{1,0:T(8,128)(2,1)} %get-tuple-element.149), channel_id=1, source_target_pairs={{0,2},{2,4},{4,6},{6,7},{7,5},{5,3},{3,1},{1,0},{8,10},{10,12},{12... | collective-permute-start | bytes 491528 | tf_op jit(solution)/shard_map/ppermute | solution.py:1040
  150.8 0.7 copy-start.23
  166.8 10.1 %collective-permute-start.8 = (bf16[320,256]{1,0:T(8,128)(2,1)}, bf16[320,256]{1,0:T(8,128)(2,1)S(1)}, u32[]{:S(2)}, u32[]{:S(2)}) collective-permute-start(bf16[320,256]{1,0:T(8,128)(2,1)} %get-tuple-element.159), channel_id=1, source_target_pairs={{0,2},{2,4},{4,6},{6,7},{7,5},{5,3},{3,1},{1,0},{8,10},{10,12},{12... | collective-permute-start | bytes 491528 | tf_op jit(solution)/shard_map/ppermute | solution.py:1040
  176.9 0.7 copy-start.22
  193.6 10.3 %collective-permute-start.9 = (bf16[320,256]{1,0:T(8,128)(2,1)}, bf16[320,256]{1,0:T(8,128)(2,1)S(1)}, u32[]{:S(2)}, u32[]{:S(2)}) collective-permute-start(bf16[320,256]{1,0:T(8,128)(2,1)} %get-tuple-element.168), channel_id=1, source_target_pairs={{0,2},{2,4},{4,6},{6,7},{7,5},{5,3},{3,1},{1,0},{8,10},{10,12},{12... | collective-permute-start | bytes 491528 | tf_op jit(solution)/shard_map/ppermute | solution.py:1040
  203.9 0.7 copy-start.21
  203.9 14.6 %collective-permute-start.10 = (bf16[2,1536,128]{2,1,0:T(8,128)(2,1)}, bf16[2,1536,128]{2,1,0:T(8,128)(2,1)S(1)}, u32[]{:S(2)}, u32[]{:S(2)}) collective-permute-start(bf16[2,1536,128]{2,1,0:T(8,128)(2,1)} %get-tuple-element.169), channel_id=1, source_target_pairs={{0,8},{8,0},{16,24},{24,16},{1,9},{9,1},{17,25},{25,17},{2,10},{10... | collective-permute-start | bytes 2359304 | tf_op jit(solution)/shard_map/ppermute | solution.py:1066
  218.5 0.9 copy-start.2
  222.1 9.9 %collective-permute-start.11 = (bf16[1312,128]{1,0:T(8,128)(2,1)}, bf16[1312,128]{1,0:T(8,128)(2,1)S(1)}, u32[]{:S(2)}, u32[]{:S(2)}) collective-permute-start(bf16[1312,128]{1,0:T(8,128)(2,1)} %get-tuple-element.188), channel_id=1, source_target_pairs={{0,16},{8,24},{16,0},{24,8},{1,17},{9,25},{17,1},{25,9},{2,18},{10... | collective-permute-start | bytes 1007624 | tf_op jit(solution)/shard_map/ppermute | solution.py:1049
  232.1 0.7 copy-start.8
  232.1 2.8 collective-permute-start.12
  234.9 3.5 %copy-start.3 = (bf16[2,1536,128]{2,1,0:T(8,128)(2,1)}, bf16[2,1536,128]{2,1,0:T(8,128)(2,1)S(1)}, u32[]{:S(2)}) copy-start(bf16[2,1536,128]{2,1,0:T(8,128)(2,1)S(1)} %collective-permute-done.12.got) | copy-start | bytes 2359300
  234.9 14.6 %all-to-all-start.2 = ((bf16[8,16,1296]{2,1,0:T(8,128)(2,1)}), bf16[8,16,1296]{2,1,0:T(8,128)(2,1)S(1)}, u32[]{:S(2)}, u32[]{:S(2)}) async-start(bf16[8,16,1296]{2,1,0:T(8,128)(2,1)} %chip_stage_1.1), calls=%async_computation.2 | async-start | bytes 720896 | tf_op jit(solution)/shard_map/all_to_all | solution.py:1074
  241.1 10.8 %collective-permute-start.13 = (bf16[1408,128]{1,0:T(8,128)(2,1)}, bf16[1408,128]{1,0:T(8,128)(2,1)S(1)}, u32[]{:S(2)}, u32[]{:S(2)}) collective-permute-start(bf16[1408,128]{1,0:T(8,128)(2,1)} %get-tuple-element.195), channel_id=1, source_target_pairs={{0,16},{8,24},{16,0},{24,8},{1,17},{9,25},{17,1},{25,9},{2,18},{10... | collective-permute-start | bytes 1081352 | tf_op jit(solution)/shard_map/ppermute | solution.py:1076
  249.5 0.7 copy-start.1
  251.9 8.2 %copy-start.5 = (f32[16,1296]{1,0:T(8,128)S(1)}, f32[16,1296]{1,0:T(8,128)}, u32[]{:S(2)}) copy-start(f32[16,1296]{1,0:T(8,128)} %sum_stage_1.1.refs_4_) | copy-start | bytes 248836
  251.9 0.7 copy-start.7
  254.9 16.4 %all-to-all-start.3 = ((bf16[8,16,1664]{2,1,0:T(8,128)(2,1)}), bf16[8,16,1664]{2,1,0:T(8,128)(2,1)S(1)}, u32[]{:S(2)}, u32[]{:S(2)}) async-start(bf16[8,16,1664]{2,1,0:T(8,128)(2,1)} %chip_stage_0.1), calls=%async_computation.3 | async-start | bytes 851968 | tf_op jit(solution)/shard_map/all_to_all | solution.py:1080
  260.1 4.9 %collective-permute-start.16 = (f32[16,1296]{1,0:T(8,128)S(1)}, f32[16,1296]{1,0:T(8,128)S(1)}, u32[]{:S(2)}, u32[]{:S(2)}) collective-permute-start(f32[16,1296]{1,0:T(8,128)S(1)} %copy-done.5), channel_id=1, source_target_pairs={{0,24},{8,16},{16,8},{24,0},{1,25},{9,17},{17,9},{25,1},{2,26},{10... | collective-permute-start | bytes 248840 | tf_op jit(solution)/shard_map/ppermute | solution.py:1078
  260.1 6.8 %collective-permute-start.15 = (f32[16,1296]{1,0:T(8,128)S(1)}, f32[16,1296]{1,0:T(8,128)S(1)}, u32[]{:S(2)}, u32[]{:S(2)}) collective-permute-start(f32[16,1296]{1,0:T(8,128)S(1)} %copy-done.5), channel_id=1, source_target_pairs={{0,16},{8,24},{16,0},{24,8},{1,17},{9,25},{17,1},{25,9},{2,18},{10... | collective-permute-start | bytes 248840 | tf_op jit(solution)/shard_map/ppermute | solution.py:1078
  261.7 5.3 %collective-permute-start.14 = (f32[16,1296]{1,0:T(8,128)S(1)}, f32[16,1296]{1,0:T(8,128)S(1)}, u32[]{:S(2)}, u32[]{:S(2)}) collective-permute-start(f32[16,1296]{1,0:T(8,128)S(1)} %copy-done.5), channel_id=1, source_target_pairs={{0,8},{8,0},{16,24},{24,16},{1,9},{9,1},{17,25},{25,17},{2,10},{10... | collective-permute-start | bytes 248840 | tf_op jit(solution)/shard_map/ppermute | solution.py:1078
  265.0 16.2 %copy-start.9 = (f32[16,1296]{1,0:T(8,128)}, f32[16,1296]{1,0:T(8,128)S(1)}, u32[]{:S(2)}) copy-start(f32[16,1296]{1,0:T(8,128)S(1)} %collective-permute-done.16.refs_7_) | copy-start | bytes 248836
  267.0 14.2 %copy-start.10 = (f32[16,1296]{1,0:T(8,128)}, f32[16,1296]{1,0:T(8,128)S(1)}, u32[]{:S(2)}) copy-start(f32[16,1296]{1,0:T(8,128)S(1)} %collective-permute-done.15.refs_6_) | copy-start | bytes 248836
  267.0 14.2 %copy-start.11 = (f32[16,1296]{1,0:T(8,128)}, f32[16,1296]{1,0:T(8,128)S(1)}, u32[]{:S(2)}) copy-start(f32[16,1296]{1,0:T(8,128)S(1)} %collective-permute-done.14.refs_5_) | copy-start | bytes 248836
  271.3 0.8 copy-start
  274.1 5.1 %collective-permute-start.19 = (f32[16,1296]{1,0:T(8,128)}, f32[16,1296]{1,0:T(8,128)S(1)}, u32[]{:S(2)}, u32[]{:S(2)}) collective-permute-start(f32[16,1296]{1,0:T(8,128)} %get-tuple-element.203.refs_0_), channel_id=1, source_target_pairs={{0,24},{8,16},{16,8},{24,0},{1,25},{9,17},{17,9},{25,1},{2,26},{10... | collective-permute-start | bytes 248840 | tf_op jit(solution)/shard_map/ppermute | solution.py:1089
  274.2 7.0 %collective-permute-start.18 = (f32[16,1296]{1,0:T(8,128)}, f32[16,1296]{1,0:T(8,128)S(1)}, u32[]{:S(2)}, u32[]{:S(2)}) collective-permute-start(f32[16,1296]{1,0:T(8,128)} %get-tuple-element.203.refs_0_), channel_id=1, source_target_pairs={{0,16},{8,24},{16,0},{24,8},{1,17},{9,25},{17,1},{25,9},{2,18},{10... | collective-permute-start | bytes 248840 | tf_op jit(solution)/shard_map/ppermute | solution.py:1089
  275.7 5.5 %collective-permute-start.17 = (f32[16,1296]{1,0:T(8,128)}, f32[16,1296]{1,0:T(8,128)S(1)}, u32[]{:S(2)}, u32[]{:S(2)}) collective-permute-start(f32[16,1296]{1,0:T(8,128)} %get-tuple-element.203.refs_0_), channel_id=1, source_target_pairs={{0,8},{8,0},{16,24},{24,16},{1,9},{9,1},{17,25},{25,17},{2,10},{10... | collective-permute-start | bytes 248840 | tf_op jit(solution)/shard_map/ppermute | solution.py:1089
  279.2 2.0 copy-start.12
  281.2 0.7 copy-start.14
  (3 other events, 2.0 us)

commit v2 on v1

--- a/solution.py
+++ b/solution.py
@@ -42,8 +42,12 @@
     return [mom_new, avg_new, param_new, param_new.astype(BF16)]
 
 
-def logistic(v):
-    return 0.5 * jnp.tanh(0.5 * v) + 0.5
+def logistic_of_twice(v):
+    return 0.5 * jnp.tanh(v) + 0.5
+
+
+def halving(gate, lanes):
+    return jnp.full((1, lanes), jnp.where(gate == 3, 1.0, 0.5), F32).astype(BF16)
 
 
 def dot_nt(a, b):
@@ -259,14 +263,16 @@
         if gather:
             for k, piece in enumerate(pieces):
                 if gather == 4:
-                    wf[pl.ds(pl.multiple_of((rank[0] ^ k) * 128, 128), 128), :] = piece[...]
+                    gate = rank[0] ^ k
+                    wf[pl.ds(pl.multiple_of(gate * 128, 128), 128), :] = piece[...] * halving(gate, piece.shape[1])
                     continue
                 peers, span = piece.shape[0], piece.shape[1] // 2
-                half = pl.multiple_of(((rank[0] ^ k) & 1) * 256, 256)
-                for g in range(peers):
-                    for j in range(2):
-                        at = pl.multiple_of(half + j * 128 + g * span, span)
-                        wf[pl.ds(at, span), :] = piece[g, j * span : (j + 1) * span, :]
+                for j in range(2):
+                    gate = ((rank[0] ^ k) & 1) * 2 + j
+                    factor = halving(gate, piece.shape[2])
+                    for g in range(peers):
+                        at = pl.multiple_of(gate * 128 + g * span, span)
+                        wf[pl.ds(at, span), :] = piece[g, j * span : (j + 1) * span, :] * factor
         ids = meta[meta.shape[0] - 1 :, :]
         here = ids[:, x0 : x0 + lanes]
         for tap, (dr, dc) in enumerate(TAPS):
@@ -312,11 +318,11 @@
             cell = cb[at, :]
             if halo <= c < halo + back:
                 cprev_out[0, (c - halo) * rows : (c - halo + 1) * rows, :] = cell.astype(BF16)
-            gi = logistic(zi + peeps[0:1, :] * cell)
-            gf = logistic(zf + peeps[1:2, :] * cell)
+            gi = logistic_of_twice(zi + peeps[0:1, :] * cell)
+            gf = logistic_of_twice(zf + peeps[1:2, :] * cell)
             gg = jnp.tanh(zg)
             cell = gf * cell + gi * gg
-            go = logistic(zo + peeps[2:3, :] * cell)
+            go = logistic_of_twice(zo + peeps[2:3, :] * cell)
             h = go * jnp.tanh(cell)
             cb[at, :] = cell
             make_variants(geo, h, c * rows, hb if final else hnext, mrm, mrp, base)
@@ -418,13 +424,14 @@
         head_out[...] = head_in[...] if carried else jnp.zeros_like(head_out)
         for tap in range(9):
             across, along = tap % 3 * 512, tap // 3 * 128
-            wb[across : across + 512, along : along + 128] = wf[:, tap * 128 : (tap + 1) * 128]
+            wb[across : across + 384, along : along + 128] = wf[:384, tap * 128 : (tap + 1) * 128] * 2
+            wb[across + 384 : across + 512, along : along + 128] = wf[384:, tap * 128 : (tap + 1) * 128]
         edge = jnp.zeros((4, rows, 128), BF16)
         dz_near[:, :rows, :] = edge
         dz_far[:, :rows, :] = edge
         dz_far[:, (back - half) * rows :, :] = edge
         for k, row in enumerate(peephole_rows(wf)):
-            peeps[k : k + 1, :] = row
+            peeps[k : k + 1, :] = row * 2.0
         if first:
             dh[...] = jnp.zeros_like(dh)
             dc[...] = jnp.zeros_like(dc)
@@ -729,7 +736,7 @@
     total = got[0].astype(F32)
     for g in range(1, got.shape[0]):
         total = total + got[g].astype(F32)
-    out[...] = total
+    out[...] = total.astype(BF16)
 
 
 def finish_kernel(rate, chans, got, steps_done, *refs):
@@ -740,7 +747,7 @@
         total = total + got[g].astype(F32)
     width = shard.shape[1]
     share = total.shape[0]
-    shard[...] = total[:, :width]
+    shard[...] = total[:, :width].astype(BF16)
     cells = total[:, width : width + share] + total[:, width + share : width + 2 * share]
     at = width + 2 * share
     extra = total[:, at : at + 16] + total[:, at + 16 : at + 32]
@@ -801,13 +808,13 @@
 
 
 def sum_stage(name, got):
-    shape = jax.ShapeDtypeStruct(got.shape[1:], F32)
+    shape = jax.ShapeDtypeStruct(got.shape[1:], BF16)
     return plain_call(sum_stage_kernel, "sum_stage_" + name, shape, got, moved=1 << 20)
 
 
 def finish_stage(rate, chans, width, got, step_count, small_args):
     shapes = [
-        jax.ShapeDtypeStruct((got.shape[1], width), F32),
+        jax.ShapeDtypeStruct((got.shape[1], width), BF16),
         jax.ShapeDtypeStruct((8, 128), F32),
         jax.ShapeDtypeStruct((1, 1), F32),
     ]
@@ -828,7 +835,7 @@
         @pl.when(layer == l)
         def _():
             for k, piece in enumerate(pieces[l]):
-                v = piece[...]
+                v = piece[...].astype(F32)
                 parts = []
                 for tap in range(9):
                     parts.append(v[:, 9 * 128 + tap * chans : 9 * 128 + (tap + 1) * chans])
@@ -933,6 +940,8 @@
     gathered = gather_dp(everyone[None], ranks)
     full = gathered.transpose(2, 1, 0, 3, 4).reshape(2, groups, 4, share, sent_w)
     full = full.transpose(0, 2, 1, 3, 4).reshape(2, 4 * wide, sent_w)
+    gate = jnp.arange(4 * wide)[:, None] // wide
+    full = full * jnp.where(gate == 3, 1.0, 0.5).astype(BF16)
     return [full[0], full[1]]
 
 
@@ -968,8 +977,13 @@
     order = ring_order(groups)
     place = [order.index(g) for g in range(groups)]
     spot = jnp.asarray(place, jnp.int32)[gate_at]
-    from_right = [(order[(i + 1) % groups], order[i]) for i in range(groups)]
-    from_left = [(order[i], order[(i + 1) % groups]) for i in range(groups)]
+    spot = jnp.where(dp_at % 2 == 1, groups - 1 - spot, spot)
+    ring = ("dp", "gate")
+    from_right = []
+    for r in range(ranks):
+        walk = order[::-1] if r % 2 else order
+        from_right += [(r * groups + walk[(i + 1) % groups], r * groups + walk[i]) for i in range(groups)]
+    from_left = [(b, a) for a, b in from_right]
 
     slab = 4 * share // ranks
     packed_w = 9 * (wide + chans)
@@ -1020,7 +1034,7 @@
         out = got[5]
         t += steps
         if n + 1 < len(geo.calls):
-            far = lax.ppermute(got[6], "gate", from_right)
+            far = lax.ppermute(got[6], ring, from_right)
             state = (out, far)
 
     state = ()
@@ -1037,7 +1051,7 @@
             geo, layer, base, steps, n == 0, carried, state, saved, weights[layer], masks, extra
         )
         if n > 0:
-            far = lax.ppermute(got[4], "gate", from_left)
+            far = lax.ppermute(got[4], ring, from_left)
             state = (got[3], far)
         cell_sums[layer] = got[1]
         if layer == 1:

time: 286 us -> 282 us (0.986)
  waiting for transfers between devices: 36.3 us -> 32.6 us
where the time goes in v2:
time: 282 us; the launch traced here: 281 us
  Pallas kernels  192 us (68%)
  starting transfers between devices  41.2 us (15%)
  waiting for transfers between devices  32.6 us (12%)
  local copies, waits for them, and re-layouts  11.5 us (4%)
    pallas_call x4, Pallas kernels, forward_call(): pl.pallas_call(functools.partial(forward_kernel, geo, layer, base, steps,...  67.3 us
    pallas_call x4, Pallas kernels, backward_call(): pl.pallas_call(functools.partial(backward_kernel, geo, layer, base, steps...  61.3 us
    pallas_call x4, Pallas kernels, weight_call(): pl.pallas_call(functools.partial(weight_kernel, geo, base, steps, acc is...  33.7 us
    pallas_call x7, Pallas kernels, plain_call(): pl.pallas_call(kernel, in_specs=specs, out_shape=out_shape, compiler_para...  15.8 us
    pallas_call x1, Pallas kernels, window_call(): pl.pallas_call(functools.partial(window_kernel, geo), in_specs=[smem, vme...  10.4 us
    ppermute x3, waiting for transfers between devices, on_device(): far = lax.ppermute(got[6], ring, from_right)  10.1 us
    unnamed x54, local copies, waits for them, and re-layouts  9.4 us
    all_to_all x1, starting transfers between devices, on_device(): lax.all_to_all(mine0, 'gate', 0, 0, tiled=True)  7.31 us
  transfers between devices with their start and end apart: 24, of which 12 were waited for; matrix products, arithmetic and copies ran while one was open for 1% of the time, Pallas kernels for 29%

profile of v2, /device:TPU:0, one launch (start us, length us, event | category | flops | bytes accessed | tf_op | source)
XLA Modules:
  0.0 281.2 jit_solution(12368458792026605283)
XLA Ops:
  0.7 2.4 pack.1
  3.0 7.3 %all-to-all-start = ((bf16[8,16,1312]{2,1,0:T(8,128)(2,1)}), bf16[8,16,1312]{2,1,0:T(8,128)(2,1)S(1)}, u32[]{:S(2)}, u32[]{:S(2)}) async-start(bf16[8,16,1312]{2,1,0:T(8,128)(2,1)} %get-tuple-element.120), calls=%async_computation | async-start | bytes 720896 | tf_op jit(solution)/shard_map/all_to_all | solution.py:1010
  10.3 1.2 dynamic_slice.6
  13.6 10.4 %window.1 = (bf16[320,1792]{1,0:T(8,128)(2,1)}, f32[16,1792]{1,0:T(8,128)}, bf16[1632,128]{1,0:T(8,128)(2,1)}, bf16[1632,128]{1,0:T(8,128)(2,1)}, bf16[1632,128]...) custom-call(s32[1]{0:T(128)} %bitcast.4.start, bf16[320,4096]{1,0:T(8,128)(2,1)} %bitcast.38, ...), custom_call_target="tpu_custom_call" | custom-call | flops 4932501504 | bytes 10485760 | tf_op jit(solution)/shard_map/window/pallas_call | solution.py:153
  24.0 1.6 collective-permute-start.1
  25.6 6.0 %all-to-all-start.1 = ((bf16[8,32,1312]{2,1,0:T(8,128)(2,1)}), bf16[8,32,1312]{2,1,0:T(8,128)(2,1)S(1)}, u32[]{:S(2)}, u32[]{:S(2)}) async-start(bf16[8,32,1312]{2,1,0:T(8,128)(2,1)} %get-tuple-element.123), calls=%async_computation.1 | async-start | bytes 1441792 | tf_op jit(solution)/shard_map/all_to_all | solution.py:1015
  31.7 2.2 collective-permute-done.1.refs_3_
  34.6 1.0 collective-permute-done.2.refs_4_
  36.4 16.8 %forward_0.1 = (bf16[5,4,832,128]{3,2,1,0:T(8,128)(2,1)}, bf16[5,832,128]{2,1,0:T(8,128)(2,1)}, bf16[5,3,576,128]{3,2,1,0:T(8,128)(2,1)}, bf16[5,832,128]{2,1,0:...) custom-call(s32[1]{0:T(128)} %bitcast.rank.refs_0_, ...), custom_call_target="tpu_custom_call" | custom-call | flops 7644119040 | bytes 8388608 | tf_op jit(solution)/shard_map/forward_0/pallas_call | solution.py:379
  53.5 1.7 collective-permute-start.4
  55.2 3.8 %collective-permute-done.4.refs_4_ = bf16[320,256]{1,0:T(8,128)(2,1)S(1)} collective-permute-done((bf16[320,256]{1,0:T(8,128)(2,1)}, bf16[320,256]{1,0:T(8,128)(2,1)S(1)}, u32[]{:S(2)}, u32[]{:S(2)}) %collective-permute-start.4) | collective-permute-done | bytes 163872 | tf_op jit(solution)/shard_map/ppermute | solution.py:1037
  59.9 17.1 %forward_5.1 = (bf16[5,4,832,128]{3,2,1,0:T(8,128)(2,1)}, bf16[5,832,128]{2,1,0:T(8,128)(2,1)}, bf16[5,3,576,128]{3,2,1,0:T(8,128)(2,1)}, bf16[5,832,128]{2,1,0:...) custom-call(s32[1]{0:T(128)} %bitcast.rank.refs_0_, ...), custom_call_target="tpu_custom_call" | custom-call | flops 7644119040 | bytes 8388608 | tf_op jit(solution)/shard_map/forward_5/pallas_call | solution.py:379
  77.0 1.8 collective-permute-start.5
  78.8 3.8 %collective-permute-done.5.refs_1_ = bf16[320,256]{1,0:T(8,128)(2,1)S(1)} collective-permute-done((bf16[320,256]{1,0:T(8,128)(2,1)}, bf16[320,256]{1,0:T(8,128)(2,1)S(1)}, u32[]{:S(2)}, u32[]{:S(2)}) %collective-permute-start.5) | collective-permute-done | bytes 163872 | tf_op jit(solution)/shard_map/ppermute | solution.py:1037
  83.3 16.6 %forward_10.1 = (bf16[5,4,832,128]{3,2,1,0:T(8,128)(2,1)}, bf16[5,832,128]{2,1,0:T(8,128)(2,1)}, bf16[5,3,576,128]{3,2,1,0:T(8,128)(2,1)}, bf16[5,832,128]{2,1,0...) custom-call(bf16[832,256]{1,0:T(8,128)(2,1)} %get-tuple-element.133.refs_0_, ...), custom_call_target="tpu_custom_call" | custom-call | flops 7644119040 | bytes 8388608 | tf_op jit(solution)/shard_map/forward_10/pallas_call | solution.py:379
  99.9 2.0 collective-permute-start.6
  103.2 2.5 collective-permute-done.6.refs_1_
  106.4 16.7 %forward_15.1 = (bf16[5,4,832,128]{3,2,1,0:T(8,128)(2,1)}, bf16[5,832,128]{2,1,0:T(8,128)(2,1)}, bf16[5,3,576,128]{3,2,1,0:T(8,128)(2,1)}, bf16[5,832,128]{2,1,0...) custom-call(bf16[832,256]{1,0:T(8,128)(2,1)} %get-tuple-element.136.refs_0_, ...), custom_call_target="tpu_custom_call" | custom-call | flops 7644119040 | bytes 8388608 | tf_op jit(solution)/shard_map/forward_15/pallas_call | solution.py:379
  123.0 15.8 %backward_15.1 = (bf16[5,512,512]{2,1,0:T(8,128)(2,1)}, f32[24,128]{1,0:T(8,128)}, f32[16,256]{1,0:T(8,128)}, bf16[512,256]{1,0:T(8,128)(2,1)}, bf16[320,256]{1,0:T(8,128)(2,1)}) custom-call(s32[102]{0:T(128)} %pad_add_fusion.1.refs_5_.refs_2_.refs_0_.refs_4_, bf16[5,4,832,128]{3,2,1,0:T(8,128)(2,1)} %get-tuple-element.138.refs_1_, ...), custom_call_target="tpu_custom_call" | custom-call | flops 6543114240 | bytes 8388608 | tf_op jit(solution)/shard_map/backward_15/pallas_call | solution.py:554
  138.9 1.8 collective-permute-start.7
  140.7 8.2 %weights_15.1.refs_0_ = f32[1536,512]{1,0:T(8,128)} custom-call(bf16[2560,512]{1,0:T(8,128)(2,1)} %bitcast.50, bf16[5,3,576,128]{3,2,1,0:T(8,128)(2,1)} %get-tuple-element.142.refs_1_, bf16[5,160,512]{2,1,0:T(8,128)(2,1)} %get-tuple-element.143.refs_2_, bf16[1632,128]{1,0:T(8,128)(2,1)} %get-tuple-element.144.refs_3_.refs_4_.refs_5_.refs_9_, ...), custom_call_target="tpu_custom_call" | custom-call | flops 3397386240 | bytes 16777216 | tf_op jit(solution)/shard_map/weights_15/pallas_call | solution.py:675
  149.6 15.4 %backward_10.1 = (bf16[5,512,512]{2,1,0:T(8,128)(2,1)}, f32[24,128]{1,0:T(8,128)}, f32[16,256]{1,0:T(8,128)}, bf16[512,256]{1,0:T(8,128)(2,1)}, bf16[320,256]{1,0:T(8,128)(2,1)}) custom-call(f32[24,128]{1,0:T(8,128)} %get-tuple-element.146.refs_0_, f32[16,256]{1,0:T(8,128)} %get-tuple-element.147.refs_1_, bf16[512,256]{1,0:T(8,128)(2,1)} %get-tuple-element.148.refs_2_, ...), custom_call_target="tpu_custom_call" | custom-call | flops 6543114240 | bytes 8388608 | tf_op jit(solution)/shard_map/backward_10/pallas_call | solution.py:554
  165.0 1.7 collective-permute-start.8
  166.7 8.6 %weights_10.1.refs_1_ = f32[1536,512]{1,0:T(8,128)} custom-call(f32[1536,512]{1,0:T(8,128)} %weights_15.1.refs_0_, bf16[2560,512]{1,0:T(8,128)(2,1)} %bitcast.26, bf16[5,3,576,128]{3,2,1,0:T(8,128)(2,1)} %get-tuple-element.154.refs_2_, bf16[5,160,512]{2,1,0:T(8,128)(2,1)} %get-tuple-element.155.refs_3_, ...), custom_call_target="tpu_custom_call" | custom-call | flops 3397386240 | bytes 16777216 | tf_op jit(solution)/shard_map/weights_10/pallas_call | solution.py:675
  176.0 16.0 %backward_5.1 = (bf16[5,512,512]{2,1,0:T(8,128)(2,1)}, f32[24,128]{1,0:T(8,128)}, f32[16,256]{1,0:T(8,128)}, bf16[512,256]{1,0:T(8,128)(2,1)}, bf16[320,256]{1,0:T(8,128)(2,1)}) custom-call(f32[24,128]{1,0:T(8,128)} %get-tuple-element.156.refs_0_, f32[16,256]{1,0:T(8,128)} %get-tuple-element.157.refs_1_, bf16[512,256]{1,0:T(8,128)(2,1)} %get-tuple-element.158.refs_2_, ...), custom_call_target="tpu_custom_call" | custom-call | flops 6543114240 | bytes 8388608 | tf_op jit(solution)/shard_map/backward_5/pallas_call | solution.py:554
  192.1 1.5 collective-permute-start.9
  193.6 8.5 %weights_5.1 = (f32[2,1536,128]{2,1,0:T(8,128)}, bf16[2,1536,128]{2,1,0:T(8,128)(2,1)}, f32[8,512]{1,0:T(8,128)}) custom-call(s32[1]{0:T(128)} %bitcast.rank.refs_0_, f32[1536,512]{1,0:T(8,128)} %weights_10.1.refs_1_, bf16[2560,512]{1,0:T(8,128)(2,1)} %bitcast.49, bf16[5,3,576,128]{3,2,1,0:T(8,128)(2,1)} %get-tuple-element.164.refs_3_, ...), custom_call_target="tpu_custom_call" | custom-call | flops 3397386240 | bytes 16777216 | tf_op jit(solution)/shard_map/weights_5/pallas_call | solution.py:675
  202.8 14.0 %backward_0.1 = (bf16[5,512,512]{2,1,0:T(8,128)(2,1)}, f32[24,128]{1,0:T(8,128)}, f32[16,256]{1,0:T(8,128)}, bf16[512,256]{1,0:T(8,128)(2,1)}, bf16[320,256]{1,0:T(8,128)(2,1)}) custom-call(bf16[512,256]{1,0:T(8,128)(2,1)} %get-tuple-element.172.refs_0_, bf16[320,256]{1,0:T(8,128)(2,1)} %copy-done.21, s32[102]{0:T(128)} %pad_add_fusion.1.refs_5_.refs_2_.refs_0_.refs_4_, ...), custom_call_target="tpu_custom_call" | custom-call | flops 6543114240 | bytes 8388608 | tf_op jit(solution)/shard_map/backward_0/pallas_call | solution.py:554
  216.8 0.9 copy-done.2
  217.7 2.7 core_stage_1.1
  220.4 1.5 collective-permute-start.11
  221.9 8.3 %weights_0.1 = (f32[2,1536,128]{2,1,0:T(8,128)}, bf16[2,1536,128]{2,1,0:T(8,128)(2,1)}, f32[48,128]{1,0:T(8,128)}) custom-call(s32[1]{0:T(128)} %bitcast.rank.refs_0_, f32[24,128]{1,0:T(8,128)} %get-tuple-element.179.refs_1_, f32[24,128]{1,0:T(8,128)} %get-tuple-element.180.refs_2_, f32[8,512]{1,0:T(8,128)} %get-tuple-element.181.refs_3_, ...), custom_call_target="tpu_custom_call" | custom-call | flops 3397386240 | bytes 16777216 | tf_op jit(solution)/shard_map/weights_0/pallas_call | solution.py:675
  231.1 2.1 chip_stage_1.1
  233.2 3.4 %all-to-all-start.2 = ((bf16[8,16,1296]{2,1,0:T(8,128)(2,1)}), bf16[8,16,1296]{2,1,0:T(8,128)(2,1)S(1)}, u32[]{:S(2)}, u32[]{:S(2)}) async-start(bf16[8,16,1296]{2,1,0:T(8,128)(2,1)} %chip_stage_1.1), calls=%async_computation.2 | async-start | bytes 720896 | tf_op jit(solution)/shard_map/all_to_all | solution.py:1088
  236.6 2.8 core_stage_0.1
  239.4 1.5 collective-permute-start.13
  240.9 6.9 %all-to-all-done.2.got = bf16[8,16,1296]{2,1,0:T(8,128)(2,1)S(1)} async-done(((bf16[8,16,1296]{2,1,0:T(8,128)(2,1)}), bf16[8,16,1296]{2,1,0:T(8,128)(2,1)S(1)}, u32[]{:S(2)}, u32[]{:S(2)}) %all-to-all-start.2) | async-done | bytes 331808 | tf_op jit(solution)/shard_map/all_to_all | solution.py:1088
  248.5 1.6 sum_stage_1.1.refs_4_
  250.9 2.2 chip_stage_0.1
  253.1 5.2 %all-to-all-start.3 = ((bf16[8,16,1664]{2,1,0:T(8,128)(2,1)}), bf16[8,16,1664]{2,1,0:T(8,128)(2,1)S(1)}, u32[]{:S(2)}, u32[]{:S(2)}) async-start(bf16[8,16,1664]{2,1,0:T(8,128)(2,1)} %chip_stage_0.1), calls=%async_computation.3 | async-start | bytes 851968 | tf_op jit(solution)/shard_map/all_to_all | solution.py:1094
  258.4 1.6 collective-permute-start.15
  260.3 2.0 collective-permute-done.16.refs_7_
  262.3 0.8 collective-permute-done.15.refs_6_
  263.1 6.5 %all-to-all-done.3.got = bf16[8,16,1664]{2,1,0:T(8,128)(2,1)S(1)} async-done(((bf16[8,16,1664]{2,1,0:T(8,128)(2,1)}), bf16[8,16,1664]{2,1,0:T(8,128)(2,1)S(1)}, u32[]{:S(2)}, u32[]{:S(2)}) %all-to-all-start.3) | async-done | bytes 426016 | tf_op jit(solution)/shard_map/all_to_all | solution.py:1094
  270.3 2.0 finish.1
  272.4 1.6 collective-permute-start.18
  274.3 2.2 collective-permute-done.19.refs_3_
  277.9 3.1 %update.1 = (f32[2,4,16,1296]{3,2,1,0:T(8,128)}, f32[2,4,16,1296]{3,2,1,0:T(8,128)}, f32[2,4,16,1296]{3,2,1,0:T(8,128)}, bf16[2,4,16,1296]{3,2,1,0:T(8,128)(2,1)}) custom-call(s32[1]{0:T(128)} %bitcast.rank.refs_0_, f32[8,128]{1,0:T(8,128)} %get-tuple-element.202.scalars, bf16[16,1296]{1,0:T(8,128)(2,1)} %get-tuple-element.203.refs_0_, ...), custom_call_target="tpu_custom_call" | custom-call | flops 1048576 | bytes 6291456 | tf_op jit(solution)/shard_map/update/pallas_call | solution.py:859
  (84 shorter events, 13.2 us)
Async XLA Ops:
  3.0 21.0 %all-to-all-start = ((bf16[8,16,1312]{2,1,0:T(8,128)(2,1)}), bf16[8,16,1312]{2,1,0:T(8,128)(2,1)S(1)}, u32[]{:S(2)}, u32[]{:S(2)}) async-start(bf16[8,16,1312]{2,1,0:T(8,128)(2,1)} %get-tuple-element.120), calls=%async_computation | async-start | bytes 720896 | tf_op jit(solution)/shard_map/all_to_all | solution.py:1010
  24.0 11.6 %copy-start.5 = (bf16[8,16,1312]{2,1,0:T(8,128)(2,1)}, bf16[8,16,1312]{2,1,0:T(8,128)(2,1)S(1)}, u32[]{:S(2)}) copy-start(bf16[8,16,1312]{2,1,0:T(8,128)(2,1)S(1)} %all-to-all-done) | copy-start | bytes 1007620
  24.0 9.9 %collective-permute-start.1 = (bf16[128,1312]{1,0:T(8,128)(2,1)S(1)}, bf16[128,1312]{1,0:T(8,128)(2,1)S(1)}, u32[]{:S(2)}, u32[]{:S(2)}) collective-permute-start(bf16[128,1312]{1,0:T(8,128)(2,1)S(1)} %bitcast.27), channel_id=1, source_target_pairs={{0,16},{8,24},{16,0},{24,8},{1,17},{9,25},{17,1},{25,9},{2,18},{10... | collective-permute-start | bytes 1007624 | tf_op jit(solution)/shard_map/ppermute | solution.py:1012
  25.6 27.6 %all-to-all-start.1 = ((bf16[8,32,1312]{2,1,0:T(8,128)(2,1)}), bf16[8,32,1312]{2,1,0:T(8,128)(2,1)S(1)}, u32[]{:S(2)}, u32[]{:S(2)}) async-start(bf16[8,32,1312]{2,1,0:T(8,128)(2,1)} %get-tuple-element.123), calls=%async_computation.1 | async-start | bytes 1441792 | tf_op jit(solution)/shard_map/all_to_all | solution.py:1015
  31.7 2.9 %collective-permute-start = (bf16[128,1312]{1,0:T(8,128)(2,1)S(1)}, bf16[128,1312]{1,0:T(8,128)(2,1)S(1)}, u32[]{:S(2)}, u32[]{:S(2)}) collective-permute-start(bf16[128,1312]{1,0:T(8,128)(2,1)S(1)} %bitcast.28), channel_id=1, source_target_pairs={{0,8},{8,0},{16,24},{24,16},{1,9},{9,1},{17,25},{25,17},{2,10},{10... | collective-permute-start | bytes 1007624 | tf_op jit(solution)/shard_map/ppermute | solution.py:1013
  33.9 1.7 copy-start.18
  33.9 1.7 collective-permute-start.2
  34.6 1.0 copy-start.19
  35.6 0.8 copy-start.20
  53.3 5.7 %copy-start.4 = (bf16[8,32,1312]{2,1,0:T(8,128)(2,1)}, bf16[8,32,1312]{2,1,0:T(8,128)(2,1)S(1)}, u32[]{:S(2)}) copy-start(bf16[8,32,1312]{2,1,0:T(8,128)(2,1)S(1)} %all-to-all-done.1.refs_1_) | copy-start | bytes 2015236
  53.3 5.7 %collective-permute-start.3 = (bf16[8,32,1312]{2,1,0:T(8,128)(2,1)S(1)}, bf16[8,32,1312]{2,1,0:T(8,128)(2,1)S(1)}, u32[]{:S(2)}, u32[]{:S(2)}) collective-permute-start(bf16[8,32,1312]{2,1,0:T(8,128)(2,1)S(1)} %all-to-all-done.1.refs_1_), channel_id=1, source_target_pairs={{0,8},{8,0},{16,24},{24,16},{1,9},{9,1},{17,25},{25,17},{2,10},{10... | collective-permute-start | bytes 2015240 | tf_op jit(solution)/shard_map/ppermute | solution.py:1031
  53.5 5.5 %collective-permute-start.4 = (bf16[320,256]{1,0:T(8,128)(2,1)}, bf16[320,256]{1,0:T(8,128)(2,1)S(1)}, u32[]{:S(2)}, u32[]{:S(2)}) collective-permute-start(bf16[320,256]{1,0:T(8,128)(2,1)} %get-tuple-element.132), channel_id=1, source_target_pairs={{2,0},{4,2},{6,4},{7,6},{5,7},{3,5},{1,3},{0,1},{11,9},{13,11},{15... | collective-permute-start | bytes 491528 | tf_op jit(solution)/shard_map/ppermute | solution.py:1037
  59.0 0.7 copy-start.24
  59.0 0.9 copy-start.17
  77.0 5.6 %collective-permute-start.5 = (bf16[320,256]{1,0:T(8,128)(2,1)}, bf16[320,256]{1,0:T(8,128)(2,1)S(1)}, u32[]{:S(2)}, u32[]{:S(2)}) collective-permute-start(bf16[320,256]{1,0:T(8,128)(2,1)} %get-tuple-element.134), channel_id=1, source_target_pairs={{2,0},{4,2},{6,4},{7,6},{5,7},{3,5},{1,3},{0,1},{11,9},{13,11},{15... | collective-permute-start | bytes 491528 | tf_op jit(solution)/shard_map/ppermute | solution.py:1037
  82.6 0.7 copy-start.26
  83.3 18.6 %copy-start.15 = (f32[16,128]{1,0:T(8,128)S(1)}, f32[16,128]{1,0:T(8,128)}, u32[]{:S(2)}) copy-start(f32[16,128]{1,0:T(8,128)} %refs_3_.1) | copy-start | bytes 24580
  83.3 19.2 %copy-start.16 = (f32[16]{0:T(128)S(1)}, f32[16]{0:T(128)}, u32[]{:S(2)}) copy-start(f32[16]{0:T(128)} %param.24) | copy-start | bytes 196
  99.9 5.8 %collective-permute-start.6 = (bf16[320,256]{1,0:T(8,128)(2,1)}, bf16[320,256]{1,0:T(8,128)(2,1)S(1)}, u32[]{:S(2)}, u32[]{:S(2)}) collective-permute-start(bf16[320,256]{1,0:T(8,128)(2,1)} %get-tuple-element.137), channel_id=1, source_target_pairs={{2,0},{4,2},{6,4},{7,6},{5,7},{3,5},{1,3},{0,1},{11,9},{13,11},{15... | collective-permute-start | bytes 491528 | tf_op jit(solution)/shard_map/ppermute | solution.py:1037
  138.9 10.0 %collective-permute-start.7 = (bf16[320,256]{1,0:T(8,128)(2,1)}, bf16[320,256]{1,0:T(8,128)(2,1)S(1)}, u32[]{:S(2)}, u32[]{:S(2)}) collective-permute-start(bf16[320,256]{1,0:T(8,128)(2,1)} %get-tuple-element.149), channel_id=1, source_target_pairs={{0,2},{2,4},{4,6},{6,7},{7,5},{5,3},{3,1},{1,0},{9,11},{11,13},{13... | collective-permute-start | bytes 491528 | tf_op jit(solution)/shard_map/ppermute | solution.py:1054
  148.9 0.7 copy-start.23
  165.0 10.4 %collective-permute-start.8 = (bf16[320,256]{1,0:T(8,128)(2,1)}, bf16[320,256]{1,0:T(8,128)(2,1)S(1)}, u32[]{:S(2)}, u32[]{:S(2)}) collective-permute-start(bf16[320,256]{1,0:T(8,128)(2,1)} %get-tuple-element.159), channel_id=1, source_target_pairs={{0,2},{2,4},{4,6},{6,7},{7,5},{5,3},{3,1},{1,0},{9,11},{11,13},{13... | collective-permute-start | bytes 491528 | tf_op jit(solution)/shard_map/ppermute | solution.py:1054
  175.4 0.7 copy-start.22
  192.1 10.0 %collective-permute-start.9 = (bf16[320,256]{1,0:T(8,128)(2,1)}, bf16[320,256]{1,0:T(8,128)(2,1)S(1)}, u32[]{:S(2)}, u32[]{:S(2)}) collective-permute-start(bf16[320,256]{1,0:T(8,128)(2,1)} %get-tuple-element.168), channel_id=1, source_target_pairs={{0,2},{2,4},{4,6},{6,7},{7,5},{5,3},{3,1},{1,0},{9,11},{11,13},{13... | collective-permute-start | bytes 491528 | tf_op jit(solution)/shard_map/ppermute | solution.py:1054
  202.1 0.7 copy-start.21
  202.1 14.7 %collective-permute-start.10 = (bf16[2,1536,128]{2,1,0:T(8,128)(2,1)}, bf16[2,1536,128]{2,1,0:T(8,128)(2,1)S(1)}, u32[]{:S(2)}, u32[]{:S(2)}) collective-permute-start(bf16[2,1536,128]{2,1,0:T(8,128)(2,1)} %get-tuple-element.169), channel_id=1, source_target_pairs={{0,8},{8,0},{16,24},{24,16},{1,9},{9,1},{17,25},{25,17},{2,10},{10... | collective-permute-start | bytes 2359304 | tf_op jit(solution)/shard_map/ppermute | solution.py:1080
  216.8 0.9 copy-start.2
  220.4 10.0 %collective-permute-start.11 = (bf16[1312,128]{1,0:T(8,128)(2,1)}, bf16[1312,128]{1,0:T(8,128)(2,1)S(1)}, u32[]{:S(2)}, u32[]{:S(2)}) collective-permute-start(bf16[1312,128]{1,0:T(8,128)(2,1)} %get-tuple-element.188), channel_id=1, source_target_pairs={{0,16},{8,24},{16,0},{24,8},{1,17},{9,25},{17,1},{25,9},{2,18},{10... | collective-permute-start | bytes 1007624 | tf_op jit(solution)/shard_map/ppermute | solution.py:1063
  230.3 0.7 copy-start.7
  230.3 2.8 %collective-permute-start.12 = (bf16[2,1536,128]{2,1,0:T(8,128)(2,1)}, bf16[2,1536,128]{2,1,0:T(8,128)(2,1)S(1)}, u32[]{:S(2)}, u32[]{:S(2)}) collective-permute-start(bf16[2,1536,128]{2,1,0:T(8,128)(2,1)} %get-tuple-element.190), channel_id=1, source_target_pairs={{0,8},{8,0},{16,24},{24,16},{1,9},{9,1},{17,25},{25,17},{2,10},{10... | collective-permute-start | bytes 2359304 | tf_op jit(solution)/shard_map/ppermute | solution.py:1086
  233.2 3.5 %copy-start.3 = (bf16[2,1536,128]{2,1,0:T(8,128)(2,1)}, bf16[2,1536,128]{2,1,0:T(8,128)(2,1)S(1)}, u32[]{:S(2)}) copy-start(bf16[2,1536,128]{2,1,0:T(8,128)(2,1)S(1)} %collective-permute-done.12.got) | copy-start | bytes 2359300
  233.2 14.6 %all-to-all-start.2 = ((bf16[8,16,1296]{2,1,0:T(8,128)(2,1)}), bf16[8,16,1296]{2,1,0:T(8,128)(2,1)S(1)}, u32[]{:S(2)}, u32[]{:S(2)}) async-start(bf16[8,16,1296]{2,1,0:T(8,128)(2,1)} %chip_stage_1.1), calls=%async_computation.2 | async-start | bytes 720896 | tf_op jit(solution)/shard_map/all_to_all | solution.py:1088
  239.4 10.8 %collective-permute-start.13 = (bf16[1408,128]{1,0:T(8,128)(2,1)}, bf16[1408,128]{1,0:T(8,128)(2,1)S(1)}, u32[]{:S(2)}, u32[]{:S(2)}) collective-permute-start(bf16[1408,128]{1,0:T(8,128)(2,1)} %get-tuple-element.195), channel_id=1, source_target_pairs={{0,16},{8,24},{16,0},{24,8},{1,17},{9,25},{17,1},{25,9},{2,18},{10... | collective-permute-start | bytes 1081352 | tf_op jit(solution)/shard_map/ppermute | solution.py:1090
  247.8 0.7 copy-start.1
  250.2 8.2 %copy-start.8 = (bf16[16,1296]{1,0:T(8,128)(2,1)S(1)}, bf16[16,1296]{1,0:T(8,128)(2,1)}, u32[]{:S(2)}) copy-start(bf16[16,1296]{1,0:T(8,128)(2,1)} %sum_stage_1.1.refs_4_) | copy-start | bytes 124420
  250.2 0.7 copy-start.6
  253.1 16.4 %all-to-all-start.3 = ((bf16[8,16,1664]{2,1,0:T(8,128)(2,1)}), bf16[8,16,1664]{2,1,0:T(8,128)(2,1)S(1)}, u32[]{:S(2)}, u32[]{:S(2)}) async-start(bf16[8,16,1664]{2,1,0:T(8,128)(2,1)} %chip_stage_0.1), calls=%async_computation.3 | async-start | bytes 851968 | tf_op jit(solution)/shard_map/all_to_all | solution.py:1094
  258.3 4.0 %collective-permute-start.16 = (bf16[16,1296]{1,0:T(8,128)(2,1)S(1)}, bf16[16,1296]{1,0:T(8,128)(2,1)S(1)}, u32[]{:S(2)}, u32[]{:S(2)}) collective-permute-start(bf16[16,1296]{1,0:T(8,128)(2,1)S(1)} %copy-done.8), channel_id=1, source_target_pairs={{0,24},{8,16},{16,8},{24,0},{1,25},{9,17},{17,9},{25,1},{2,26},{10... | collective-permute-start | bytes 124424 | tf_op jit(solution)/shard_map/ppermute | solution.py:1092
  258.4 4.6 %collective-permute-start.15 = (bf16[16,1296]{1,0:T(8,128)(2,1)S(1)}, bf16[16,1296]{1,0:T(8,128)(2,1)S(1)}, u32[]{:S(2)}, u32[]{:S(2)}) collective-permute-start(bf16[16,1296]{1,0:T(8,128)(2,1)S(1)} %copy-done.8), channel_id=1, source_target_pairs={{0,16},{8,24},{16,0},{24,8},{1,17},{9,25},{17,1},{25,9},{2,18},{10... | collective-permute-start | bytes 124424 | tf_op jit(solution)/shard_map/ppermute | solution.py:1092
  260.0 3.1 %collective-permute-start.14 = (bf16[16,1296]{1,0:T(8,128)(2,1)S(1)}, bf16[16,1296]{1,0:T(8,128)(2,1)S(1)}, u32[]{:S(2)}, u32[]{:S(2)}) collective-permute-start(bf16[16,1296]{1,0:T(8,128)(2,1)S(1)} %copy-done.8), channel_id=1, source_target_pairs={{0,8},{8,0},{16,24},{24,16},{1,9},{9,1},{17,25},{25,17},{2,10},{10... | collective-permute-start | bytes 124424 | tf_op jit(solution)/shard_map/ppermute | solution.py:1092
  262.3 15.0 %copy-start.9 = (bf16[16,1296]{1,0:T(8,128)(2,1)}, bf16[16,1296]{1,0:T(8,128)(2,1)S(1)}, u32[]{:S(2)}) copy-start(bf16[16,1296]{1,0:T(8,128)(2,1)S(1)} %collective-permute-done.16.refs_7_) | copy-start | bytes 124420
  263.1 14.2 %copy-start.10 = (bf16[16,1296]{1,0:T(8,128)(2,1)}, bf16[16,1296]{1,0:T(8,128)(2,1)S(1)}, u32[]{:S(2)}) copy-start(bf16[16,1296]{1,0:T(8,128)(2,1)S(1)} %collective-permute-done.15.refs_6_) | copy-start | bytes 124420
  263.1 14.2 %copy-start.11 = (bf16[16,1296]{1,0:T(8,128)(2,1)}, bf16[16,1296]{1,0:T(8,128)(2,1)S(1)}, u32[]{:S(2)}) copy-start(bf16[16,1296]{1,0:T(8,128)(2,1)S(1)} %collective-permute-done.14.refs_5_) | copy-start | bytes 124420
  269.6 0.8 copy-start
  272.3 4.2 %collective-permute-start.19 = (bf16[16,1296]{1,0:T(8,128)(2,1)}, bf16[16,1296]{1,0:T(8,128)(2,1)S(1)}, u32[]{:S(2)}, u32[]{:S(2)}) collective-permute-start(bf16[16,1296]{1,0:T(8,128)(2,1)} %get-tuple-element.203.refs_0_), channel_id=1, source_target_pairs={{0,24},{8,16},{16,8},{24,0},{1,25},{9,17},{17,9},{25,1},{2,26},{10... | collective-permute-start | bytes 124424 | tf_op jit(solution)/shard_map/ppermute | solution.py:1103
  272.4 4.9 %collective-permute-start.18 = (bf16[16,1296]{1,0:T(8,128)(2,1)}, bf16[16,1296]{1,0:T(8,128)(2,1)S(1)}, u32[]{:S(2)}, u32[]{:S(2)}) collective-permute-start(bf16[16,1296]{1,0:T(8,128)(2,1)} %get-tuple-element.203.refs_0_), channel_id=1, source_target_pairs={{0,16},{8,24},{16,0},{24,8},{1,17},{9,25},{17,1},{25,9},{2,18},{10... | collective-permute-start | bytes 124424 | tf_op jit(solution)/shard_map/ppermute | solution.py:1103
  274.0 3.3 %collective-permute-start.17 = (bf16[16,1296]{1,0:T(8,128)(2,1)}, bf16[16,1296]{1,0:T(8,128)(2,1)S(1)}, u32[]{:S(2)}, u32[]{:S(2)}) collective-permute-start(bf16[16,1296]{1,0:T(8,128)(2,1)} %get-tuple-element.203.refs_0_), channel_id=1, source_target_pairs={{0,8},{8,0},{16,24},{24,16},{1,9},{9,1},{17,25},{25,17},{2,10},{10... | collective-permute-start | bytes 124424 | tf_op jit(solution)/shard_map/ppermute | solution.py:1103
  276.5 0.8 copy-start.12
  (3 other events, 1.9 us)

commit v3 on v2

--- a/solution.py
+++ b/solution.py
@@ -95,7 +95,7 @@
 CELL_COLS = 16
 
 
-def window_kernel(geo, start, frames, valid, regions, win, meta, mrm, mrp, mcm, mcp, count, lhs, pick):
+def window_kernel(geo, start, frames, valid, regions, win, meta, mrm, mrp, count, lhs, pick):
     rows, own, halo, union, width = geo.rows, geo.own, geo.halo, geo.union, geo.window
     nf = frames.shape[0]
     nv = valid.shape[0]
@@ -122,14 +122,10 @@
     lax.fori_loop(0, width // 256, one, 0)
     px = union * rows
     ids = meta[nv : nv + 1, :]
-    bands = jnp.floor(ids * 0.5)
     here = ids[:, rows : rows + px]
-    band_here = bands[:, rows : rows + px]
     picked = [
         ids[:, rows - 1 : rows - 1 + px] == here,
         ids[:, rows + 1 : rows + 1 + px] == here,
-        bands[:, :px] == band_here,
-        bands[:, 2 * rows : 2 * rows + px] == band_here,
     ]
     row_at = lax.broadcasted_iota(jnp.int32, (8, px), 0)
     stack = jnp.zeros((8, px), F32)
@@ -137,7 +133,7 @@
         stack = jnp.where(row_at == k, jnp.broadcast_to(m.astype(F32), (8, px)), stack)
     stack = stack.astype(BF16)
     sel = lax.broadcasted_iota(jnp.int32, (8, 128), 0)
-    for k, out in enumerate((mrm, mrp, mcm, mcp)):
+    for k, out in enumerate((mrm, mrp)):
         out[...] = dot_tn(stack, (sel == k).astype(F32).astype(BF16)).astype(BF16)
     a = (2 * halo + 1) * rows
     count[...] = jnp.broadcast_to(jnp.sum(meta[:nv, a : a + own * rows]), count.shape)
@@ -153,12 +149,12 @@
     return pl.pallas_call(
         functools.partial(window_kernel, geo),
         in_specs=[smem, vmem, vmem, vmem],
-        out_specs=[vmem] * 7,
+        out_specs=[vmem] * 5,
         out_shape=[
             jax.ShapeDtypeStruct((nf, geo.window), BF16),
             jax.ShapeDtypeStruct((nv + 1, geo.window), F32),
         ]
-        + [jax.ShapeDtypeStruct((px, 128), BF16)] * 4
+        + [jax.ShapeDtypeStruct((px, 128), BF16)] * 2
         + [jax.ShapeDtypeStruct((8, 128), F32)],
         scratch_shapes=[pltpu.VMEM((total, pixels), BF16), pltpu.VMEM((pixels, 256), BF16)],
         compiler_params=pltpu.CompilerParams(vmem_limit_bytes=VMEM_LIMIT),
@@ -357,7 +353,7 @@
     depth = sent_w - 9 * 128
     by_step = lambda *dims: pl.BlockSpec((1,) + dims, lambda t: (t,) + (0,) * len(dims))
     lead = list(weights) if gather else []
-    cols, masks = masks[4], masks[:2]
+    cols, masks = masks[2], masks[:2]
     smem = pl.BlockSpec(memory_space=pltpu.SMEM)
     operands = lead + list(state) + [cols, win, meta] + ([] if gather else [weights]) + list(masks)
     in_specs = [smem] if gather else []
@@ -526,7 +522,7 @@
     by_step = lambda *dims: pl.BlockSpec((1,) + dims, lambda t: (steps - 1 - t,) + (0,) * len(dims))
     first_live = saved["t"] - EIN
     lead = list(carried) + list(state)
-    cols, masks = masks[4], masks[:2]
+    cols, masks = masks[2], masks[:2]
     operands = lead + [cols, saved["gates"], saved["cprev"], wf] + list(masks)
     in_specs = [whole(s.shape) for s in lead] + [pl.BlockSpec(memory_space=pltpu.SMEM)]
     in_specs += [by_step(4, back * rows, 128), by_step(back * rows, 128)]
@@ -592,11 +588,10 @@
     if small:
         sums0, sums1, bias1, head, count = refs[:5]
         refs = refs[5:]
-    dz, hvar, xown, mcm, mcp = refs[:5]
-    outs, rhs = refs[5:-1], refs[-1]
+    cols, dz, hvar, xown = refs[:4]
+    outs, rhs = refs[4:-1], refs[-1]
     rows, own, halo = geo.rows, geo.own, geo.halo
     on = own * rows
-    g0 = (base + 2 * halo) * rows
     wide = hvar.shape[-1]
     part = pl.program_id(0)
     if final:
@@ -620,13 +615,17 @@
     @pl.when(part < 3)
     def _():
         for dc in range(3):
-            for j in range(steps):
-                v = hvar[j, 0, dc * rows : dc * rows + on, :]
-                if dc == 0:
-                    v = v * mcm[g0 : g0 + on, :]
-                elif dc == 2:
-                    v = v * mcp[g0 : g0 + on, :]
-                rhs[j * on : (j + 1) * on, dc * wide : (dc + 1) * wide] = v
+            lanes = slice(dc * wide, (dc + 1) * wide)
+            if dc == 1:
+                for j in range(steps):
+                    rhs[j * on : (j + 1) * on, lanes] = hvar[j, 0, rows : rows + on, :]
+                continue
+            for c in range(own):
+                keep = cols[dc // 2 * geo.union + base + 2 * halo + c].astype(F32)
+                keep = jnp.full((1, wide), keep, F32).astype(BF16)
+                for j in range(steps):
+                    at = j * on + c * rows
+                    rhs[at : at + rows, lanes] = hvar[j, 0, (dc + c) * rows : (dc + c + 1) * rows, :] * keep
         put(dot_tn(rhs[...], dz[...]))
 
     @pl.when(part == 3)
@@ -652,17 +651,17 @@
             outs[1][0, depth : depth + 96, :] = split_low(few)
 
 
-def weight_call(geo, base, steps, acc, dz, hvar, xown, mcm, mcp, rank=None, small=()):
+def weight_call(geo, base, steps, acc, dz, hvar, xown, cols, rank=None, small=()):
     on = geo.own * geo.rows
     dz = dz.reshape(steps * on, 512)
     final = rank is not None
     band = 3 * hvar.shape[-1]
-    operands = ([rank] if final else []) + ([] if acc is None else [acc]) + list(small) + [dz, hvar, xown, mcm, mcp]
+    operands = ([rank] if final else []) + ([] if acc is None else [acc]) + list(small) + [cols, dz, hvar, xown]
     specs = [pl.BlockSpec(memory_space=pltpu.SMEM)] if final else []
     specs += [] if acc is None else [pl.BlockSpec((band, 512), lambda i: (i, 0))]
-    specs += [whole(v.shape) for v in small] + [whole(dz.shape)]
+    specs += [whole(v.shape) for v in small] + [pl.BlockSpec(memory_space=pltpu.SMEM), whole(dz.shape)]
     specs += [pl.BlockSpec((steps, 1) + hvar.shape[2:], lambda i: (0, jnp.minimum(i, 2), 0, 0))]
-    specs += [whole(v.shape) for v in (xown, mcm, mcp)]
+    specs += [whole(xown.shape)]
     out_shape = jax.ShapeDtypeStruct((4 * band, 512), F32)
     out_specs = pl.BlockSpec((band, 512), lambda i: (i, 0))
     if final:
@@ -992,14 +991,14 @@
     rank = dp_at.astype(jnp.int32).reshape(1)
 
     start = jnp.mod(spot * own - 2 * halo - 1, COLS).astype(jnp.int32).reshape(1)
-    win, meta, mrm, mrp, mcm, mcp, counted = window_call(
+    win, meta, mrm, mrp, counted = window_call(
         geo, start, frames.reshape(-1, pixels), valid, regions.reshape(1, pixels)
     )
     first_row = lax.slice_in_dim(regions, 0, COLS) // 2
     bands = lax.dynamic_slice_in_dim(jnp.concatenate([first_row, first_row]), start[0], union + 2)
     same = (bands[1:] == bands[:-1]).astype(jnp.int32)
     cols = jnp.concatenate([same[:-1], same[1:]])
-    masks = (mrm, mrp, mcm, mcp, cols)
+    masks = (mrm, mrp, cols)
 
     head_low = head_w.astype(BF16)
     head_bias = head_b[:, None]
@@ -1069,8 +1068,7 @@
             dz,
             saved["hvar"],
             saved["xown"],
-            masks[2],
-            masks[3],
+            cols,
             rank if done else None,
             (cell_sums[0], cell_sums[1], grads[1][2], head_sums, counted) if done and layer == 0 else (),
         )

time: 282 us -> 281 us (level)
  no operation moved by 1% of the time
where the time goes in v3:
time: 281 us; the launch traced here: 280 us
  Pallas kernels  190 us (68%)
  starting transfers between devices  41.2 us (15%)
  waiting for transfers between devices  33 us (12%)
  local copies, waits for them, and re-layouts  11.5 us (4%)
    pallas_call x4, Pallas kernels, forward_call(): pl.pallas_call(functools.partial(forward_kernel, geo, layer, base, steps,...  67.3 us
    pallas_call x4, Pallas kernels, backward_call(): pl.pallas_call(functools.partial(backward_kernel, geo, layer, base, steps...  61.3 us
    pallas_call x4, Pallas kernels, weight_call(): pl.pallas_call(functools.partial(weight_kernel, geo, base, steps, acc is...  32.5 us
    pallas_call x7, Pallas kernels, plain_call(): pl.pallas_call(kernel, in_specs=specs, out_shape=out_shape, compiler_para...  15.8 us
    ppermute x3, waiting for transfers between devices, on_device(): far = lax.ppermute(got[6], ring, from_right)  10.1 us
    pallas_call x1, Pallas kernels, window_call(): pl.pallas_call(functools.partial(window_kernel, geo), in_specs=[smem, vme...  9.93 us
    unnamed x54, local copies, waits for them, and re-layouts  9.4 us
    all_to_all x1, starting transfers between devices, on_device(): lax.all_to_all(mine0, 'gate', 0, 0, tiled=True)  7.31 us
  transfers between devices with their start and end apart: 24, of which 12 were waited for; matrix products, arithmetic and copies ran while one was open for 1% of the time, Pallas kernels for 29%

profile of v3, /device:TPU:0, one launch (start us, length us, event | category | flops | bytes accessed | tf_op | source)
XLA Modules:
  0.0 279.8 jit_solution(12536685027072525562)
XLA Ops:
  0.7 2.4 pack.1
  3.0 7.3 %all-to-all-start = ((bf16[8,16,1312]{2,1,0:T(8,128)(2,1)}), bf16[8,16,1312]{2,1,0:T(8,128)(2,1)S(1)}, u32[]{:S(2)}, u32[]{:S(2)}) async-start(bf16[8,16,1312]{2,1,0:T(8,128)(2,1)} %get-tuple-element.118), calls=%async_computation | async-start | bytes 720896 | tf_op jit(solution)/shard_map/all_to_all | solution.py:1009
  10.3 1.2 dynamic_slice.6
  13.6 9.9 %window.1 = (bf16[320,1792]{1,0:T(8,128)(2,1)}, f32[16,1792]{1,0:T(8,128)}, bf16[1632,128]{1,0:T(8,128)(2,1)}, bf16[1632,128]{1,0:T(8,128)(2,1)}, f32[8,128]{1,0:T(8,128)}) custom-call(s32[1]{0:T(128)} %bitcast.4.start, bf16[320,4096]{1,0:T(8,128)(2,1)} %bitcast.37, s32[15,4096]{1,0:T(8,128)} %valid.1, s32[1,4096]{1,0:T(1,128)} %bitcast.38), custom_call_target="tpu_custom_call" | custom-call | flops 4932501504 | bytes 10485760 | tf_op jit(solution)/shard_map/window/pallas_call | solution.py:149
  23.5 1.6 collective-permute-start.1
  25.2 6.0 %all-to-all-start.1 = ((bf16[8,32,1312]{2,1,0:T(8,128)(2,1)}), bf16[8,32,1312]{2,1,0:T(8,128)(2,1)S(1)}, u32[]{:S(2)}, u32[]{:S(2)}) async-start(bf16[8,32,1312]{2,1,0:T(8,128)(2,1)} %get-tuple-element.121), calls=%async_computation.1 | async-start | bytes 1441792 | tf_op jit(solution)/shard_map/all_to_all | solution.py:1014
  31.2 2.2 collective-permute-done.1.refs_3_
  34.1 1.0 collective-permute-done.2.refs_4_
  35.9 16.8 %forward_0.1 = (bf16[5,4,832,128]{3,2,1,0:T(8,128)(2,1)}, bf16[5,832,128]{2,1,0:T(8,128)(2,1)}, bf16[5,3,576,128]{3,2,1,0:T(8,128)(2,1)}, bf16[5,832,128]{2,1,0:...) custom-call(s32[1]{0:T(128)} %bitcast.rank.refs_0_, ...), custom_call_target="tpu_custom_call" | custom-call | flops 7644119040 | bytes 8388608 | tf_op jit(solution)/shard_map/forward_0/pallas_call | solution.py:375
  53.0 1.7 collective-permute-start.4
  54.7 3.8 %collective-permute-done.4.refs_4_ = bf16[320,256]{1,0:T(8,128)(2,1)S(1)} collective-permute-done((bf16[320,256]{1,0:T(8,128)(2,1)}, bf16[320,256]{1,0:T(8,128)(2,1)S(1)}, u32[]{:S(2)}, u32[]{:S(2)}) %collective-permute-start.4) | collective-permute-done | bytes 163872 | tf_op jit(solution)/shard_map/ppermute | solution.py:1036
  59.4 17.1 %forward_5.1 = (bf16[5,4,832,128]{3,2,1,0:T(8,128)(2,1)}, bf16[5,832,128]{2,1,0:T(8,128)(2,1)}, bf16[5,3,576,128]{3,2,1,0:T(8,128)(2,1)}, bf16[5,832,128]{2,1,0:...) custom-call(s32[1]{0:T(128)} %bitcast.rank.refs_0_, ...), custom_call_target="tpu_custom_call" | custom-call | flops 7644119040 | bytes 8388608 | tf_op jit(solution)/shard_map/forward_5/pallas_call | solution.py:375
  76.6 1.8 collective-permute-start.5
  78.4 3.8 %collective-permute-done.5.refs_1_ = bf16[320,256]{1,0:T(8,128)(2,1)S(1)} collective-permute-done((bf16[320,256]{1,0:T(8,128)(2,1)}, bf16[320,256]{1,0:T(8,128)(2,1)S(1)}, u32[]{:S(2)}, u32[]{:S(2)}) %collective-permute-start.5) | collective-permute-done | bytes 163872 | tf_op jit(solution)/shard_map/ppermute | solution.py:1036
  82.8 16.6 %forward_10.1 = (bf16[5,4,832,128]{3,2,1,0:T(8,128)(2,1)}, bf16[5,832,128]{2,1,0:T(8,128)(2,1)}, bf16[5,3,576,128]{3,2,1,0:T(8,128)(2,1)}, bf16[5,832,128]{2,1,0...) custom-call(bf16[832,256]{1,0:T(8,128)(2,1)} %get-tuple-element.131.refs_0_, ...), custom_call_target="tpu_custom_call" | custom-call | flops 7644119040 | bytes 8388608 | tf_op jit(solution)/shard_map/forward_10/pallas_call | solution.py:375
  99.5 2.0 collective-permute-start.6
  102.7 2.5 collective-permute-done.6.refs_1_
  105.9 16.7 %forward_15.1 = (bf16[5,4,832,128]{3,2,1,0:T(8,128)(2,1)}, bf16[5,832,128]{2,1,0:T(8,128)(2,1)}, bf16[5,3,576,128]{3,2,1,0:T(8,128)(2,1)}, bf16[5,832,128]{2,1,0...) custom-call(bf16[832,256]{1,0:T(8,128)(2,1)} %get-tuple-element.134.refs_0_, ...), custom_call_target="tpu_custom_call" | custom-call | flops 7644119040 | bytes 8388608 | tf_op jit(solution)/shard_map/forward_15/pallas_call | solution.py:375
  122.6 15.9 %backward_15.1 = (bf16[5,512,512]{2,1,0:T(8,128)(2,1)}, f32[24,128]{1,0:T(8,128)}, f32[16,256]{1,0:T(8,128)}, bf16[512,256]{1,0:T(8,128)(2,1)}, bf16[320,256]{1,0:T(8,128)(2,1)}) custom-call(s32[102]{0:T(128)} %pad_add_fusion.1.refs_5_.refs_2_.refs_0_.refs_4_.refs_1_.refs_6_, bf16[5,4,832,128]{3,2,1,0:T(8,128)(2,1)} %get-tuple-element.136.refs_1_, ...), custom_call_target="tpu_custom_call" | custom-call | flops 6543114240 | bytes 8388608 | tf_op jit(solution)/shard_map/backward_15/pallas_call | solution.py:550
  138.4 1.8 collective-permute-start.7
  140.2 7.9 %weights_15.1.refs_0_ = f32[1536,512]{1,0:T(8,128)} custom-call(s32[102]{0:T(128)} %pad_add_fusion.1.refs_5_.refs_2_.refs_0_.refs_4_.refs_1_.refs_6_, bf16[2560,512]{1,0:T(8,128)(2,1)} %bitcast.50, bf16[5,3,576,128]{3,2,1,0:T(8,128)(2,1)} %get-tuple-element.140.refs_2_, bf16[5,160,512]{2,1,0:T(8,128)(2,1)} %get-tuple-element.141.refs_3_), custom_call_target="tpu_custom_call" | custom-call | flops 3397386240 | bytes 16777216 | tf_op jit(solution)/shard_map/weights_15/pallas_call | solution.py:674
  148.7 15.4 %backward_10.1 = (bf16[5,512,512]{2,1,0:T(8,128)(2,1)}, f32[24,128]{1,0:T(8,128)}, f32[16,256]{1,0:T(8,128)}, bf16[512,256]{1,0:T(8,128)(2,1)}, bf16[320,256]{1,0:T(8,128)(2,1)}) custom-call(f32[24,128]{1,0:T(8,128)} %get-tuple-element.142.refs_0_, f32[16,256]{1,0:T(8,128)} %get-tuple-element.143.refs_1_, bf16[512,256]{1,0:T(8,128)(2,1)} %get-tuple-element.144.refs_2_, ...), custom_call_target="tpu_custom_call" | custom-call | flops 6543114240 | bytes 8388608 | tf_op jit(solution)/shard_map/backward_10/pallas_call | solution.py:550
  164.2 1.5 collective-permute-start.8
  165.7 8.3 %weights_10.1.refs_1_ = f32[1536,512]{1,0:T(8,128)} custom-call(f32[1536,512]{1,0:T(8,128)} %weights_15.1.refs_0_, s32[102]{0:T(128)} %pad_add_fusion.1.refs_5_.refs_2_.refs_0_.refs_4_.refs_1_.refs_6_, bf16[2560,512]{1,0:T(8,128)(2,1)} %bitcast.49, bf16[5,3,576,128]{3,2,1,0:T(8,128)(2,1)} %get-tuple-element.150.refs_3_, ...), custom_call_target="tpu_custom_call" | custom-call | flops 3397386240 | bytes 16777216 | tf_op jit(solution)/shard_map/weights_10/pallas_call | solution.py:674
  174.7 16.0 %backward_5.1 = (bf16[5,512,512]{2,1,0:T(8,128)(2,1)}, f32[24,128]{1,0:T(8,128)}, f32[16,256]{1,0:T(8,128)}, bf16[512,256]{1,0:T(8,128)(2,1)}, bf16[320,256]{1,0:T(8,128)(2,1)}) custom-call(f32[24,128]{1,0:T(8,128)} %get-tuple-element.152.refs_0_, f32[16,256]{1,0:T(8,128)} %get-tuple-element.153.refs_1_, bf16[512,256]{1,0:T(8,128)(2,1)} %get-tuple-element.154.refs_2_, ...), custom_call_target="tpu_custom_call" | custom-call | flops 6543114240 | bytes 8388608 | tf_op jit(solution)/shard_map/backward_5/pallas_call | solution.py:550
  190.7 1.7 collective-permute-start.9
  192.5 8.2 %weights_5.1 = (f32[2,1536,128]{2,1,0:T(8,128)}, bf16[2,1536,128]{2,1,0:T(8,128)(2,1)}, f32[8,512]{1,0:T(8,128)}) custom-call(s32[1]{0:T(128)} %bitcast.rank.refs_0_, f32[1536,512]{1,0:T(8,128)} %weights_10.1.refs_1_, s32[102]{0:T(128)} %pad_add_fusion.1.refs_5_.refs_2_.refs_0_.refs_4_.refs_1_.refs_6_, bf16[2560,512]{1,0:T(8,128)(2,1)} %bitcast.48, ...), custom_call_target="tpu_custom_call" | custom-call | flops 3397386240 | bytes 16777216 | tf_op jit(solution)/shard_map/weights_5/pallas_call | solution.py:674
  201.4 14.0 %backward_0.1 = (bf16[5,512,512]{2,1,0:T(8,128)(2,1)}, f32[24,128]{1,0:T(8,128)}, f32[16,256]{1,0:T(8,128)}, bf16[512,256]{1,0:T(8,128)(2,1)}, bf16[320,256]{1,0:T(8,128)(2,1)}) custom-call(bf16[512,256]{1,0:T(8,128)(2,1)} %get-tuple-element.168.refs_0_, bf16[320,256]{1,0:T(8,128)(2,1)} %copy-done.21, ...), custom_call_target="tpu_custom_call" | custom-call | flops 6543114240 | bytes 8388608 | tf_op jit(solution)/shard_map/backward_0/pallas_call | solution.py:550
  215.4 0.9 copy-done.2
  216.4 2.7 core_stage_1.1
  219.0 1.5 collective-permute-start.11
  220.5 8.0 %weights_0.1 = (f32[2,1536,128]{2,1,0:T(8,128)}, bf16[2,1536,128]{2,1,0:T(8,128)(2,1)}, f32[48,128]{1,0:T(8,128)}) custom-call(s32[1]{0:T(128)} %bitcast.rank.refs_0_, f32[24,128]{1,0:T(8,128)} %get-tuple-element.175.refs_1_, f32[24,128]{1,0:T(8,128)} %get-tuple-element.176.refs_2_, f32[8,512]{1,0:T(8,128)} %get-tuple-element.177.refs_3_, ...), custom_call_target="tpu_custom_call" | custom-call | flops 3397386240 | bytes 16777216 | tf_op jit(solution)/shard_map/weights_0/pallas_call | solution.py:674
  229.7 2.1 chip_stage_1.1
  231.8 3.4 %all-to-all-start.2 = ((bf16[8,16,1296]{2,1,0:T(8,128)(2,1)}), bf16[8,16,1296]{2,1,0:T(8,128)(2,1)S(1)}, u32[]{:S(2)}, u32[]{:S(2)}) async-start(bf16[8,16,1296]{2,1,0:T(8,128)(2,1)} %chip_stage_1.1), calls=%async_computation.2 | async-start | bytes 720896 | tf_op jit(solution)/shard_map/all_to_all | solution.py:1086
  235.3 2.8 core_stage_0.1
  238.0 1.5 collective-permute-start.13
  239.5 6.9 %all-to-all-done.2.got = bf16[8,16,1296]{2,1,0:T(8,128)(2,1)S(1)} async-done(((bf16[8,16,1296]{2,1,0:T(8,128)(2,1)}), bf16[8,16,1296]{2,1,0:T(8,128)(2,1)S(1)}, u32[]{:S(2)}, u32[]{:S(2)}) %all-to-all-start.2) | async-done | bytes 331808 | tf_op jit(solution)/shard_map/all_to_all | solution.py:1086
  247.1 1.6 sum_stage_1.1.refs_4_
  249.5 2.2 chip_stage_0.1
  251.8 5.2 %all-to-all-start.3 = ((bf16[8,16,1664]{2,1,0:T(8,128)(2,1)}), bf16[8,16,1664]{2,1,0:T(8,128)(2,1)S(1)}, u32[]{:S(2)}, u32[]{:S(2)}) async-start(bf16[8,16,1664]{2,1,0:T(8,128)(2,1)} %chip_stage_0.1), calls=%async_computation.3 | async-start | bytes 851968 | tf_op jit(solution)/shard_map/all_to_all | solution.py:1092
  257.1 1.5 collective-permute-start.15
  258.9 2.1 collective-permute-done.16.refs_7_
  261.0 0.8 collective-permute-done.15.refs_6_
  261.7 6.5 %all-to-all-done.3.got = bf16[8,16,1664]{2,1,0:T(8,128)(2,1)S(1)} async-done(((bf16[8,16,1664]{2,1,0:T(8,128)(2,1)}), bf16[8,16,1664]{2,1,0:T(8,128)(2,1)S(1)}, u32[]{:S(2)}, u32[]{:S(2)}) %all-to-all-start.3) | async-done | bytes 426016 | tf_op jit(solution)/shard_map/all_to_all | solution.py:1092
  269.0 2.0 finish.1
  271.1 1.5 collective-permute-start.18
  272.9 2.3 collective-permute-done.19.refs_3_
  276.6 3.1 %update.1 = (f32[2,4,16,1296]{3,2,1,0:T(8,128)}, f32[2,4,16,1296]{3,2,1,0:T(8,128)}, f32[2,4,16,1296]{3,2,1,0:T(8,128)}, bf16[2,4,16,1296]{3,2,1,0:T(8,128)(2,1)}) custom-call(s32[1]{0:T(128)} %bitcast.rank.refs_0_, f32[8,128]{1,0:T(8,128)} %get-tuple-element.198.scalars, bf16[16,1296]{1,0:T(8,128)(2,1)} %get-tuple-element.199.refs_0_, ...), custom_call_target="tpu_custom_call" | custom-call | flops 1048576 | bytes 6291456 | tf_op jit(solution)/shard_map/update/pallas_call | solution.py:858
  (84 shorter events, 13.6 us)
Async XLA Ops:
  3.0 20.5 %all-to-all-start = ((bf16[8,16,1312]{2,1,0:T(8,128)(2,1)}), bf16[8,16,1312]{2,1,0:T(8,128)(2,1)S(1)}, u32[]{:S(2)}, u32[]{:S(2)}) async-start(bf16[8,16,1312]{2,1,0:T(8,128)(2,1)} %get-tuple-element.118), calls=%async_computation | async-start | bytes 720896 | tf_op jit(solution)/shard_map/all_to_all | solution.py:1009
  23.5 11.6 %copy-start.5 = (bf16[8,16,1312]{2,1,0:T(8,128)(2,1)}, bf16[8,16,1312]{2,1,0:T(8,128)(2,1)S(1)}, u32[]{:S(2)}) copy-start(bf16[8,16,1312]{2,1,0:T(8,128)(2,1)S(1)} %all-to-all-done) | copy-start | bytes 1007620
  23.5 9.9 %collective-permute-start.1 = (bf16[128,1312]{1,0:T(8,128)(2,1)S(1)}, bf16[128,1312]{1,0:T(8,128)(2,1)S(1)}, u32[]{:S(2)}, u32[]{:S(2)}) collective-permute-start(bf16[128,1312]{1,0:T(8,128)(2,1)S(1)} %bitcast.26), channel_id=1, source_target_pairs={{0,16},{8,24},{16,0},{24,8},{1,17},{9,25},{17,1},{25,9},{2,18},{10... | collective-permute-start | bytes 1007624 | tf_op jit(solution)/shard_map/ppermute | solution.py:1011
  25.2 27.6 %all-to-all-start.1 = ((bf16[8,32,1312]{2,1,0:T(8,128)(2,1)}), bf16[8,32,1312]{2,1,0:T(8,128)(2,1)S(1)}, u32[]{:S(2)}, u32[]{:S(2)}) async-start(bf16[8,32,1312]{2,1,0:T(8,128)(2,1)} %get-tuple-element.121), calls=%async_computation.1 | async-start | bytes 1441792 | tf_op jit(solution)/shard_map/all_to_all | solution.py:1014
  31.2 2.9 %collective-permute-start = (bf16[128,1312]{1,0:T(8,128)(2,1)S(1)}, bf16[128,1312]{1,0:T(8,128)(2,1)S(1)}, u32[]{:S(2)}, u32[]{:S(2)}) collective-permute-start(bf16[128,1312]{1,0:T(8,128)(2,1)S(1)} %bitcast.27), channel_id=1, source_target_pairs={{0,8},{8,0},{16,24},{24,16},{1,9},{9,1},{17,25},{25,17},{2,10},{10... | collective-permute-start | bytes 1007624 | tf_op jit(solution)/shard_map/ppermute | solution.py:1012
  33.5 1.7 copy-start.18
  33.5 1.7 collective-permute-start.2
  34.1 1.0 copy-start.19
  35.1 0.8 copy-start.20
  52.8 5.8 %copy-start.4 = (bf16[8,32,1312]{2,1,0:T(8,128)(2,1)}, bf16[8,32,1312]{2,1,0:T(8,128)(2,1)S(1)}, u32[]{:S(2)}) copy-start(bf16[8,32,1312]{2,1,0:T(8,128)(2,1)S(1)} %all-to-all-done.1.refs_1_) | copy-start | bytes 2015236
  52.8 5.7 %collective-permute-start.3 = (bf16[8,32,1312]{2,1,0:T(8,128)(2,1)S(1)}, bf16[8,32,1312]{2,1,0:T(8,128)(2,1)S(1)}, u32[]{:S(2)}, u32[]{:S(2)}) collective-permute-start(bf16[8,32,1312]{2,1,0:T(8,128)(2,1)S(1)} %all-to-all-done.1.refs_1_), channel_id=1, source_target_pairs={{0,8},{8,0},{16,24},{24,16},{1,9},{9,1},{17,25},{25,17},{2,10},{10... | collective-permute-start | bytes 2015240 | tf_op jit(solution)/shard_map/ppermute | solution.py:1030
  53.0 5.5 %collective-permute-start.4 = (bf16[320,256]{1,0:T(8,128)(2,1)}, bf16[320,256]{1,0:T(8,128)(2,1)S(1)}, u32[]{:S(2)}, u32[]{:S(2)}) collective-permute-start(bf16[320,256]{1,0:T(8,128)(2,1)} %get-tuple-element.130), channel_id=1, source_target_pairs={{2,0},{4,2},{6,4},{7,6},{5,7},{3,5},{1,3},{0,1},{11,9},{13,11},{15... | collective-permute-start | bytes 491528 | tf_op jit(solution)/shard_map/ppermute | solution.py:1036
  58.5 0.7 copy-start.24
  58.5 0.9 copy-start.17
  76.6 5.6 %collective-permute-start.5 = (bf16[320,256]{1,0:T(8,128)(2,1)}, bf16[320,256]{1,0:T(8,128)(2,1)S(1)}, u32[]{:S(2)}, u32[]{:S(2)}) collective-permute-start(bf16[320,256]{1,0:T(8,128)(2,1)} %get-tuple-element.132), channel_id=1, source_target_pairs={{2,0},{4,2},{6,4},{7,6},{5,7},{3,5},{1,3},{0,1},{11,9},{13,11},{15... | collective-permute-start | bytes 491528 | tf_op jit(solution)/shard_map/ppermute | solution.py:1036
  82.2 0.7 copy-start.26
  82.8 18.6 %copy-start.15 = (f32[16,128]{1,0:T(8,128)S(1)}, f32[16,128]{1,0:T(8,128)}, u32[]{:S(2)}) copy-start(f32[16,128]{1,0:T(8,128)} %refs_3_.1) | copy-start | bytes 24580
  82.8 19.2 %copy-start.16 = (f32[16]{0:T(128)S(1)}, f32[16]{0:T(128)}, u32[]{:S(2)}) copy-start(f32[16]{0:T(128)} %param.24) | copy-start | bytes 196
  99.5 5.8 %collective-permute-start.6 = (bf16[320,256]{1,0:T(8,128)(2,1)}, bf16[320,256]{1,0:T(8,128)(2,1)S(1)}, u32[]{:S(2)}, u32[]{:S(2)}) collective-permute-start(bf16[320,256]{1,0:T(8,128)(2,1)} %get-tuple-element.135), channel_id=1, source_target_pairs={{2,0},{4,2},{6,4},{7,6},{5,7},{3,5},{1,3},{0,1},{11,9},{13,11},{15... | collective-permute-start | bytes 491528 | tf_op jit(solution)/shard_map/ppermute | solution.py:1036
  138.4 9.7 %collective-permute-start.7 = (bf16[320,256]{1,0:T(8,128)(2,1)}, bf16[320,256]{1,0:T(8,128)(2,1)S(1)}, u32[]{:S(2)}, u32[]{:S(2)}) collective-permute-start(bf16[320,256]{1,0:T(8,128)(2,1)} %get-tuple-element.145), channel_id=1, source_target_pairs={{0,2},{2,4},{4,6},{6,7},{7,5},{5,3},{3,1},{1,0},{9,11},{11,13},{13... | collective-permute-start | bytes 491528 | tf_op jit(solution)/shard_map/ppermute | solution.py:1053
  148.1 0.7 copy-start.23
  164.2 9.9 %collective-permute-start.8 = (bf16[320,256]{1,0:T(8,128)(2,1)}, bf16[320,256]{1,0:T(8,128)(2,1)S(1)}, u32[]{:S(2)}, u32[]{:S(2)}) collective-permute-start(bf16[320,256]{1,0:T(8,128)(2,1)} %get-tuple-element.155), channel_id=1, source_target_pairs={{0,2},{2,4},{4,6},{6,7},{7,5},{5,3},{3,1},{1,0},{9,11},{11,13},{13... | collective-permute-start | bytes 491528 | tf_op jit(solution)/shard_map/ppermute | solution.py:1053
  174.0 0.7 copy-start.22
  190.7 10.0 %collective-permute-start.9 = (bf16[320,256]{1,0:T(8,128)(2,1)}, bf16[320,256]{1,0:T(8,128)(2,1)S(1)}, u32[]{:S(2)}, u32[]{:S(2)}) collective-permute-start(bf16[320,256]{1,0:T(8,128)(2,1)} %get-tuple-element.164), channel_id=1, source_target_pairs={{0,2},{2,4},{4,6},{6,7},{7,5},{5,3},{3,1},{1,0},{9,11},{11,13},{13... | collective-permute-start | bytes 491528 | tf_op jit(solution)/shard_map/ppermute | solution.py:1053
  200.7 0.7 copy-start.21
  200.8 14.7 %collective-permute-start.10 = (bf16[2,1536,128]{2,1,0:T(8,128)(2,1)}, bf16[2,1536,128]{2,1,0:T(8,128)(2,1)S(1)}, u32[]{:S(2)}, u32[]{:S(2)}) collective-permute-start(bf16[2,1536,128]{2,1,0:T(8,128)(2,1)} %get-tuple-element.165), channel_id=1, source_target_pairs={{0,8},{8,0},{16,24},{24,16},{1,9},{9,1},{17,25},{25,17},{2,10},{10... | collective-permute-start | bytes 2359304 | tf_op jit(solution)/shard_map/ppermute | solution.py:1078
  215.4 0.9 copy-start.2
  219.0 9.9 %collective-permute-start.11 = (bf16[1312,128]{1,0:T(8,128)(2,1)}, bf16[1312,128]{1,0:T(8,128)(2,1)S(1)}, u32[]{:S(2)}, u32[]{:S(2)}) collective-permute-start(bf16[1312,128]{1,0:T(8,128)(2,1)} %get-tuple-element.184), channel_id=1, source_target_pairs={{0,16},{8,24},{16,0},{24,8},{1,17},{9,25},{17,1},{25,9},{2,18},{10... | collective-permute-start | bytes 1007624 | tf_op jit(solution)/shard_map/ppermute | solution.py:1062
  229.0 0.7 copy-start.7
  229.0 2.8 %collective-permute-start.12 = (bf16[2,1536,128]{2,1,0:T(8,128)(2,1)}, bf16[2,1536,128]{2,1,0:T(8,128)(2,1)S(1)}, u32[]{:S(2)}, u32[]{:S(2)}) collective-permute-start(bf16[2,1536,128]{2,1,0:T(8,128)(2,1)} %get-tuple-element.186), channel_id=1, source_target_pairs={{0,8},{8,0},{16,24},{24,16},{1,9},{9,1},{17,25},{25,17},{2,10},{10... | collective-permute-start | bytes 2359304 | tf_op jit(solution)/shard_map/ppermute | solution.py:1084
  231.8 3.5 %copy-start.3 = (bf16[2,1536,128]{2,1,0:T(8,128)(2,1)}, bf16[2,1536,128]{2,1,0:T(8,128)(2,1)S(1)}, u32[]{:S(2)}) copy-start(bf16[2,1536,128]{2,1,0:T(8,128)(2,1)S(1)} %collective-permute-done.12.got) | copy-start | bytes 2359300
  231.8 14.6 %all-to-all-start.2 = ((bf16[8,16,1296]{2,1,0:T(8,128)(2,1)}), bf16[8,16,1296]{2,1,0:T(8,128)(2,1)S(1)}, u32[]{:S(2)}, u32[]{:S(2)}) async-start(bf16[8,16,1296]{2,1,0:T(8,128)(2,1)} %chip_stage_1.1), calls=%async_computation.2 | async-start | bytes 720896 | tf_op jit(solution)/shard_map/all_to_all | solution.py:1086
  238.0 10.8 %collective-permute-start.13 = (bf16[1408,128]{1,0:T(8,128)(2,1)}, bf16[1408,128]{1,0:T(8,128)(2,1)S(1)}, u32[]{:S(2)}, u32[]{:S(2)}) collective-permute-start(bf16[1408,128]{1,0:T(8,128)(2,1)} %get-tuple-element.191), channel_id=1, source_target_pairs={{0,16},{8,24},{16,0},{24,8},{1,17},{9,25},{17,1},{25,9},{2,18},{10... | collective-permute-start | bytes 1081352 | tf_op jit(solution)/shard_map/ppermute | solution.py:1088
  246.4 0.7 copy-start.1
  248.8 8.2 %copy-start.8 = (bf16[16,1296]{1,0:T(8,128)(2,1)S(1)}, bf16[16,1296]{1,0:T(8,128)(2,1)}, u32[]{:S(2)}) copy-start(bf16[16,1296]{1,0:T(8,128)(2,1)} %sum_stage_1.1.refs_4_) | copy-start | bytes 124420
  248.8 0.7 copy-start.6
  251.8 16.4 %all-to-all-start.3 = ((bf16[8,16,1664]{2,1,0:T(8,128)(2,1)}), bf16[8,16,1664]{2,1,0:T(8,128)(2,1)S(1)}, u32[]{:S(2)}, u32[]{:S(2)}) async-start(bf16[8,16,1664]{2,1,0:T(8,128)(2,1)} %chip_stage_0.1), calls=%async_computation.3 | async-start | bytes 851968 | tf_op jit(solution)/shard_map/all_to_all | solution.py:1092
  257.0 4.0 %collective-permute-start.16 = (bf16[16,1296]{1,0:T(8,128)(2,1)S(1)}, bf16[16,1296]{1,0:T(8,128)(2,1)S(1)}, u32[]{:S(2)}, u32[]{:S(2)}) collective-permute-start(bf16[16,1296]{1,0:T(8,128)(2,1)S(1)} %copy-done.8), channel_id=1, source_target_pairs={{0,24},{8,16},{16,8},{24,0},{1,25},{9,17},{17,9},{25,1},{2,26},{10... | collective-permute-start | bytes 124424 | tf_op jit(solution)/shard_map/ppermute | solution.py:1090
  257.1 4.7 %collective-permute-start.15 = (bf16[16,1296]{1,0:T(8,128)(2,1)S(1)}, bf16[16,1296]{1,0:T(8,128)(2,1)S(1)}, u32[]{:S(2)}, u32[]{:S(2)}) collective-permute-start(bf16[16,1296]{1,0:T(8,128)(2,1)S(1)} %copy-done.8), channel_id=1, source_target_pairs={{0,16},{8,24},{16,0},{24,8},{1,17},{9,25},{17,1},{25,9},{2,18},{10... | collective-permute-start | bytes 124424 | tf_op jit(solution)/shard_map/ppermute | solution.py:1090
  258.6 3.1 %collective-permute-start.14 = (bf16[16,1296]{1,0:T(8,128)(2,1)S(1)}, bf16[16,1296]{1,0:T(8,128)(2,1)S(1)}, u32[]{:S(2)}, u32[]{:S(2)}) collective-permute-start(bf16[16,1296]{1,0:T(8,128)(2,1)S(1)} %copy-done.8), channel_id=1, source_target_pairs={{0,8},{8,0},{16,24},{24,16},{1,9},{9,1},{17,25},{25,17},{2,10},{10... | collective-permute-start | bytes 124424 | tf_op jit(solution)/shard_map/ppermute | solution.py:1090
  261.0 15.0 %copy-start.9 = (bf16[16,1296]{1,0:T(8,128)(2,1)}, bf16[16,1296]{1,0:T(8,128)(2,1)S(1)}, u32[]{:S(2)}) copy-start(bf16[16,1296]{1,0:T(8,128)(2,1)S(1)} %collective-permute-done.16.refs_7_) | copy-start | bytes 124420
  261.7 14.2 %copy-start.10 = (bf16[16,1296]{1,0:T(8,128)(2,1)}, bf16[16,1296]{1,0:T(8,128)(2,1)S(1)}, u32[]{:S(2)}) copy-start(bf16[16,1296]{1,0:T(8,128)(2,1)S(1)} %collective-permute-done.15.refs_6_) | copy-start | bytes 124420
  261.7 14.2 %copy-start.11 = (bf16[16,1296]{1,0:T(8,128)(2,1)}, bf16[16,1296]{1,0:T(8,128)(2,1)S(1)}, u32[]{:S(2)}) copy-start(bf16[16,1296]{1,0:T(8,128)(2,1)S(1)} %collective-permute-done.14.refs_5_) | copy-start | bytes 124420
  268.2 0.8 copy-start
  271.0 4.2 %collective-permute-start.19 = (bf16[16,1296]{1,0:T(8,128)(2,1)}, bf16[16,1296]{1,0:T(8,128)(2,1)S(1)}, u32[]{:S(2)}, u32[]{:S(2)}) collective-permute-start(bf16[16,1296]{1,0:T(8,128)(2,1)} %get-tuple-element.199.refs_0_), channel_id=1, source_target_pairs={{0,24},{8,16},{16,8},{24,0},{1,25},{9,17},{17,9},{25,1},{2,26},{10... | collective-permute-start | bytes 124424 | tf_op jit(solution)/shard_map/ppermute | solution.py:1101
  271.1 4.9 %collective-permute-start.18 = (bf16[16,1296]{1,0:T(8,128)(2,1)}, bf16[16,1296]{1,0:T(8,128)(2,1)S(1)}, u32[]{:S(2)}, u32[]{:S(2)}) collective-permute-start(bf16[16,1296]{1,0:T(8,128)(2,1)} %get-tuple-element.199.refs_0_), channel_id=1, source_target_pairs={{0,16},{8,24},{16,0},{24,8},{1,17},{9,25},{17,1},{25,9},{2,18},{10... | collective-permute-start | bytes 124424 | tf_op jit(solution)/shard_map/ppermute | solution.py:1101
  272.6 3.4 %collective-permute-start.17 = (bf16[16,1296]{1,0:T(8,128)(2,1)}, bf16[16,1296]{1,0:T(8,128)(2,1)S(1)}, u32[]{:S(2)}, u32[]{:S(2)}) collective-permute-start(bf16[16,1296]{1,0:T(8,128)(2,1)} %get-tuple-element.199.refs_0_), channel_id=1, source_target_pairs={{0,8},{8,0},{16,24},{24,16},{1,9},{9,1},{17,25},{25,17},{2,10},{10... | collective-permute-start | bytes 124424 | tf_op jit(solution)/shard_map/ppermute | solution.py:1101
  275.2 0.8 copy-start.12
  (3 other events, 1.9 us)
